TPU v7x, 512 devices: a whole 4x4x16 slice. The times are simulated.
512 devices in a mesh: fsdp: 16 (over x, y), dp: 32 (over z, core).
Axes of the slice: x: 4, y: 4, z: 16, core: 2. Of those that a mesh axis runs over, the one named last changes fastest.
Arguments:
- tokens: bfloat16 [65536, 4096], P(('fsdp', 'dp')), may hold values from -6 to 6
- master_old: float32 [512, 128, 128], P(('fsdp', 'dp')), may hold values from -0.25 to 0.25
- moment_old: float32 [512, 128, 128], P(('fsdp', 'dp')), may hold values from -6 to 6
- second_old: float32 [512, 128, 128], P(('fsdp', 'dp')), may hold values from 0.01 to 1
- old_cell: int32 [112, 4], P('fsdp'), may hold values from 0 to 31, as said below
- new_cell: int32 [112, 4], P('fsdp'), may hold values from 0 to 31, as said below
- regrown: int32 [112, 4], P('fsdp'), may hold values 0 or 1
- new_rows: int32 [112, 4], replicated, may hold values from 0 to 31, as said below
Outputs:
- hidden: bfloat16 [65536, 14336], P(('fsdp', 'dp'))
- master_new: float32 [512, 128, 128], P(('fsdp', 'dp'))
- moment_new: float32 [512, 128, 128], P(('fsdp', 'dp'))
- second_new: float32 [512, 128, 128], P(('fsdp', 'dp'))
Inputs may be any that keep to these rules, and one draw needn't show every extreme that they name: `old_cell`: within one fsdp index, taking its slots column by column and then by k, the old cells strictly increase; a cell's index // 1 is its holder along dp and index % 1 its place in that holder's buffer. `new_cell`: strictly increasing in the same order; every slot's new cell differs from its old cell by at most 4, and by exactly 4 for some slot of every fsdp index. `new_rows`: the 4 block rows of one block column are distinct.
All inputs are finite; a program needn't handle non-finite values. No bound on the sum of `regrown` on one device may be relied on, other than what follows from the above.
Results may differ from a plain program's by a relative error of at most 0.007.
Values may be sent and summed in bfloat16 or wider, within the bound.
No kernel may reach another device: no remote copies, remote signals or barrier semaphores. Data moves between devices by JAX's collectives and lax.ppermute only.
A program may use at most 128 MiB of HBM per device.

v0:
```python
import jax
import jax.numpy as jnp
from jax import lax
from jax.sharding import PartitionSpec as P


def passed_along(block, axis, distance):
    devices = range(lax.axis_size(axis))
    route = [(i - distance, i) for i in devices if i - distance in devices]
    return lax.ppermute(block, axis, route)


def on_device(tokens, master_old, moment_old, second_old, old_cell, new_cell, regrown, new_rows):
    block_size = master_old.shape[1]
    capacity = master_old.shape[0]
    column_count = old_cell.shape[0]
    nonzero_count = old_cell.shape[1]
    slot_count = column_count * nonzero_count
    axis_width = lax.axis_size("dp")
    cell_count = axis_width * capacity
    farthest = min((cell_count - slot_count + capacity - 1) // capacity, axis_width - 1)
    holder = lax.axis_index("dp")
    old_flat = old_cell.reshape(-1)
    new_flat = new_cell.reshape(-1)
    keep_flag = regrown.reshape(-1) == 0
    my_cells = holder * capacity + jnp.arange(capacity, dtype=jnp.int32)
    matches = new_flat[None, :] == my_cells[:, None]
    present = jnp.any(matches & keep_flag[None, :], axis=1)
    source = jnp.sum(jnp.where(matches, old_flat[None, :], 0), axis=1)
    offset = holder - source // capacity
    slot_place = source % capacity
    candidate = jnp.where(offset > 0, 2 * offset - 1, jnp.where(offset < 0, -2 * offset, 0))
    pick_index = candidate * capacity + slot_place
    own_states = (master_old, moment_old, second_old)
    shift_list = []
    for distance in range(1, farthest + 1):
        shift_list.append(distance)
        shift_list.append(-distance)
    received_list = [own_states]
    for by_value in shift_list:
        received_list.append(
            (
                passed_along(own_states[0].astype(jnp.bfloat16), "dp", by_value).astype(
                    jnp.float32
                ),
                passed_along(own_states[1].astype(jnp.bfloat16), "dp", by_value).astype(
                    jnp.float32
                ),
                passed_along(own_states[2].astype(jnp.bfloat16), "dp", by_value).astype(
                    jnp.float32
                ),
            )
        )

    def settle(member):
        pool = jnp.concatenate([entry[member] for entry in received_list], axis=0)
        chosen = jnp.take(pool, pick_index, axis=0, mode="clip")
        return jnp.where(present[:, None, None], chosen, jnp.float32(0.0))

    master_new = settle(0)
    moment_new = settle(1)
    second_new = settle(2)
    cell_blocks = master_new.astype(jnp.bfloat16)
    group_cells = lax.all_gather(cell_blocks, "dp", axis=0, tiled=True)
    panel = jnp.take(group_cells, new_flat, axis=0).reshape(
        column_count, nonzero_count, block_size, block_size
    )
    token_count = tokens.shape[0]
    token_blocks = tokens.reshape(token_count, tokens.shape[1] // block_size, block_size)
    panel_piece = lax.all_gather(panel, "fsdp", axis=0, tiled=True)
    count = panel_piece.shape[0]
    picked = jnp.take(token_blocks, new_rows.reshape(-1), axis=1)
    picked = picked.reshape(token_count, count, nonzero_count, block_size)
    product = jnp.einsum("tcka,ckab->tcb", picked, panel_piece, preferred_element_type=jnp.float32)
    hidden = product.reshape(token_count, count * block_size).astype(jnp.bfloat16)
    return (hidden, master_new, moment_new, second_new)


def solution(mesh):
    return jax.shard_map(
        on_device,
        mesh=mesh,
        in_specs=(
            P(("fsdp", "dp"), None),
            P(("fsdp", "dp"), None, None),
            P(("fsdp", "dp"), None, None),
            P(("fsdp", "dp"), None, None),
            P("fsdp", None),
            P("fsdp", None),
            P("fsdp", None),
            P(),
        ),
        out_specs=(
            P(("fsdp", "dp"), None),
            P(("fsdp", "dp"), None, None),
            P(("fsdp", "dp"), None, None),
            P(("fsdp", "dp"), None, None),
        ),
        check_vma=False,
    )
```

profile of v0, /device:TPU:1, one launch (start us, length us, event | category | flops | bytes accessed | tf_op | source)
XLA Modules:
  0.0 264.1 jit_solution(16962180668199227297)
XLA Ops:
  8.1 4.9 %collective-permute-start = (bf16[1,128,128]{2,1,0:T(8,128)(2,1)S(1)}, bf16[1,128,128]{2,1,0:T(8,128)(2,1)S(1)}, u32[]{:S(2)}, u32[]{:S(2)}) collective-permute-start(bf16[1,128,128]{2,1,0:T(8,128)(2,1)S(1)} %get-tuple-element.61), channel_id=1, source_target_pairs={{0,1},{1,2},{2,3},{3,4},{4,5},{5,6},{6,7},{7,8},{8,9},{9,10},{10,1... | collective-permute-start | bytes 98312 | tf_op jit(solution)/shard_map/ppermute | solution.py:10
  13.1 5.1 %collective-permute-start.1 = (bf16[1,128,128]{2,1,0:T(8,128)(2,1)S(1)}, bf16[1,128,128]{2,1,0:T(8,128)(2,1)S(1)}, u32[]{:S(2)}, u32[]{:S(2)}) collective-permute-start(bf16[1,128,128]{2,1,0:T(8,128)(2,1)S(1)} %get-tuple-element.61), channel_id=1, source_target_pairs={{1,0},{2,1},{3,2},{4,3},{5,4},{6,5},{7,6},{8,7},{9,8},{10,9},{11,1... | collective-permute-start | bytes 98312 | tf_op jit(solution)/shard_map/ppermute | solution.py:10
  20.8 5.0 %collective-permute-start.4 = (bf16[1,128,128]{2,1,0:T(8,128)(2,1)S(1)}, bf16[1,128,128]{2,1,0:T(8,128)(2,1)S(1)}, u32[]{:S(2)}, u32[]{:S(2)}) collective-permute-start(bf16[1,128,128]{2,1,0:T(8,128)(2,1)S(1)} %get-tuple-element.61), channel_id=1, source_target_pairs={{0,3},{1,4},{2,5},{3,6},{4,7},{5,8},{6,9},{7,10},{8,11},{9,12},{10... | collective-permute-start | bytes 98312 | tf_op jit(solution)/shard_map/ppermute | solution.py:10
  25.9 1.4 and_reduce_fusion
  30.6 9.2 %collective-permute-start.6 = (bf16[1,128,128]{2,1,0:T(8,128)(2,1)S(1)}, bf16[1,128,128]{2,1,0:T(8,128)(2,1)S(1)}, u32[]{:S(2)}, u32[]{:S(2)}) collective-permute-start(bf16[1,128,128]{2,1,0:T(8,128)(2,1)S(1)} %get-tuple-element.61), channel_id=1, source_target_pairs={{0,4},{1,5},{2,6},{3,7},{4,8},{5,9},{6,10},{7,11},{8,12},{9,13},{1... | collective-permute-start | bytes 98312 | tf_op jit(solution)/shard_map/ppermute | solution.py:10
  41.2 4.1 %collective-permute-done.7 = bf16[1,128,128]{2,1,0:T(8,128)(2,1)S(1)} collective-permute-done((bf16[1,128,128]{2,1,0:T(8,128)(2,1)S(1)}, bf16[1,128,128]{2,1,0:T(8,128)(2,1)S(1)}, u32[]{:S(2)}, u32[]{:S(2)}) %collective-permute-start.7) | collective-permute-done | bytes 32800 | tf_op jit(solution)/shard_map/ppermute | solution.py:10
  47.7 73.8 %all-gather.3.cloned.1.call-done = bf16[32,128,128]{2,1,0:T(8,128)(2,1)} async-done(((bf16[1,128,128]{2,1,0:T(8,128)(2,1)}), bf16[32,128,128]{2,1,0:T(8,128)(2,1)}) %all-gather.3.cloned.1.call-update) | async-done | bytes 1048592 | tf_op jit(solution)/shard_map/all_gather | solution.py:64
  121.4 1.9 gather_fusion
  125.4 3.2 %collective-permute-start.16 = (bf16[1,128,128]{2,1,0:T(8,128)(2,1)S(1)}, bf16[1,128,128]{2,1,0:T(8,128)(2,1)S(1)}, u32[]{:S(2)}, u32[]{:S(2)}) collective-permute-start(bf16[1,128,128]{2,1,0:T(8,128)(2,1)S(1)} %get-tuple-element.57), channel_id=1, source_target_pairs={{0,1},{1,2},{2,3},{3,4},{4,5},{5,6},{6,7},{7,8},{8,9},{9,10},{10,1... | collective-permute-start | bytes 98312 | tf_op jit(solution)/shard_map/ppermute | solution.py:10
  128.6 1.9 collective-permute-start.17
  130.5 2.3 collective-permute-start.18
  134.1 6.0 %collective-permute-start.20 = (bf16[1,128,128]{2,1,0:T(8,128)(2,1)S(1)}, bf16[1,128,128]{2,1,0:T(8,128)(2,1)S(1)}, u32[]{:S(2)}, u32[]{:S(2)}) collective-permute-start(bf16[1,128,128]{2,1,0:T(8,128)(2,1)S(1)} %get-tuple-element.57), channel_id=1, source_target_pairs={{0,3},{1,4},{2,5},{3,6},{4,7},{5,8},{6,9},{7,10},{8,11},{9,12},{10... | collective-permute-start | bytes 98312 | tf_op jit(solution)/shard_map/ppermute | solution.py:10
  142.7 1.6 copy.35
  145.1 13.3 %gather_fusion.1 = bf16[448,128,128]{2,1,0:T(8,128)(2,1)} fusion(bf16[128,32,128]{2,0,1:T(8,128)(2,1)S(1)} %copy.37, s32[1024]{0:T(1024)S(1)} %pad_clamp_fusion), kind=kCustom, calls=%fused_computation.1 | custom fusion | bytes 29361920 | tf_op jit(solution)/shard_map/jit(_take)/gather | solution.py:72
  159.7 6.6 %collective-permute-start.22 = (bf16[1,128,128]{2,1,0:T(8,128)(2,1)S(1)}, bf16[1,128,128]{2,1,0:T(8,128)(2,1)S(1)}, u32[]{:S(2)}, u32[]{:S(2)}) collective-permute-start(bf16[1,128,128]{2,1,0:T(8,128)(2,1)S(1)} %get-tuple-element.57), channel_id=1, source_target_pairs={{0,4},{1,5},{2,6},{3,7},{4,8},{5,9},{6,10},{7,11},{8,12},{9,13},{1... | collective-permute-start | bytes 98312 | tf_op jit(solution)/shard_map/ppermute | solution.py:10
  167.6 2.2 collective-permute-start.8
  169.8 2.2 collective-permute-start.9
  172.0 6.4 %collective-permute-start.10 = (bf16[1,128,128]{2,1,0:T(8,128)(2,1)S(1)}, bf16[1,128,128]{2,1,0:T(8,128)(2,1)S(1)}, u32[]{:S(2)}, u32[]{:S(2)}) collective-permute-start(bf16[1,128,128]{2,1,0:T(8,128)(2,1)S(1)} %get-tuple-element.59), channel_id=1, source_target_pairs={{0,2},{1,3},{2,4},{3,5},{4,6},{5,7},{6,8},{7,9},{8,10},{9,11},{10,... | collective-permute-start | bytes 98312 | tf_op jit(solution)/shard_map/ppermute | solution.py:10
  179.8 6.0 %collective-permute-start.12 = (bf16[1,128,128]{2,1,0:T(8,128)(2,1)S(1)}, bf16[1,128,128]{2,1,0:T(8,128)(2,1)S(1)}, u32[]{:S(2)}, u32[]{:S(2)}) collective-permute-start(bf16[1,128,128]{2,1,0:T(8,128)(2,1)S(1)} %get-tuple-element.59), channel_id=1, source_target_pairs={{0,3},{1,4},{2,5},{3,6},{4,7},{5,8},{6,9},{7,10},{8,11},{9,12},{10... | collective-permute-start | bytes 98312 | tf_op jit(solution)/shard_map/ppermute | solution.py:10
  187.2 8.8 %collective-permute-start.14 = (bf16[1,128,128]{2,1,0:T(8,128)(2,1)S(1)}, bf16[1,128,128]{2,1,0:T(8,128)(2,1)S(1)}, u32[]{:S(2)}, u32[]{:S(2)}) collective-permute-start(bf16[1,128,128]{2,1,0:T(8,128)(2,1)S(1)} %get-tuple-element.59), channel_id=1, source_target_pairs={{0,4},{1,5},{2,6},{3,7},{4,8},{5,9},{6,10},{7,11},{8,12},{9,13},{1... | collective-permute-start | bytes 98312 | tf_op jit(solution)/shard_map/ppermute | solution.py:10
  198.7 3.3 %collective-permute-done.15 = bf16[1,128,128]{2,1,0:T(8,128)(2,1)S(1)} collective-permute-done((bf16[1,128,128]{2,1,0:T(8,128)(2,1)S(1)}, bf16[1,128,128]{2,1,0:T(8,128)(2,1)S(1)}, u32[]{:S(2)}, u32[]{:S(2)}) %collective-permute-start.15) | collective-permute-done | bytes 32800 | tf_op jit(solution)/shard_map/ppermute | solution.py:10
  203.3 34.5 %all-gather.5.cloned.1.call-done = bf16[112,4,128,128]{3,2,1,0:T(8,128)(2,1)} async-done(((bf16[7,4,128,128]{3,2,1,0:T(8,128)(2,1)}), bf16[112,4,128,128]{3,2,1,0:T(8,128)(2,1)}) %all-gather.5.cloned.1.call-update) | async-done | bytes 14680080 | tf_op jit(solution)/shard_map/all_gather | solution.py:70
  237.7 13.5 %bitcast_convert_fusion = bf16[112,128,128]{2,1,0:T(8,128)(2,1)} fusion(bf16[112,4,128,128]{3,2,1,0:T(8,128)(2,1)} %all-gather.5.cloned.1.call-done, bf16[128,112,4,128]{3,0,2,1:T(8,128)(2,1)} %bitcast.15, pred[112,4]{1,0:T(8,128)(4,1)S(1)} %copy.34), kind=kOutput, calls=%fused_computation.5 | convolution fusion | flops 1888223232 | bytes 33030592 | tf_op jit(solution)/shard_map/tcka,ckab->tcb/dot_general | solution.py:74
  251.2 6.1 %copy.39 = bf16[128,14336]{1,0:T(8,128)(2,1)} copy(bf16[128,14336]{0,1:T(8,128)(2,1)} %bitcast.17) | data formatting | bytes 7340032
  (80 shorter events, 25.6 us)
Async XLA Ops:
  7.2 114.3 %all-gather.3.cloned.1.call-start = ((), (), s32[]{:S(2)}) async-start(), calls=%async_computation | async-start | bytes 1081344 | tf_op jit(solution)/shard_map/all_gather | solution.py:64
  8.1 21.1 %collective-permute-start = (bf16[1,128,128]{2,1,0:T(8,128)(2,1)S(1)}, bf16[1,128,128]{2,1,0:T(8,128)(2,1)S(1)}, u32[]{:S(2)}, u32[]{:S(2)}) collective-permute-start(bf16[1,128,128]{2,1,0:T(8,128)(2,1)S(1)} %get-tuple-element.61), channel_id=1, source_target_pairs={{0,1},{1,2},{2,3},{3,4},{4,5},{5,6},{6,7},{7,8},{8,9},{9,10},{10,1... | collective-permute-start | bytes 98312 | tf_op jit(solution)/shard_map/ppermute | solution.py:10
  13.1 17.5 %collective-permute-start.1 = (bf16[1,128,128]{2,1,0:T(8,128)(2,1)S(1)}, bf16[1,128,128]{2,1,0:T(8,128)(2,1)S(1)}, u32[]{:S(2)}, u32[]{:S(2)}) collective-permute-start(bf16[1,128,128]{2,1,0:T(8,128)(2,1)S(1)} %get-tuple-element.61), channel_id=1, source_target_pairs={{1,0},{2,1},{3,2},{4,3},{5,4},{6,5},{7,6},{8,7},{9,8},{10,9},{11,1... | collective-permute-start | bytes 98312 | tf_op jit(solution)/shard_map/ppermute | solution.py:10
  18.2 21.5 %collective-permute-start.2 = (bf16[1,128,128]{2,1,0:T(8,128)(2,1)S(1)}, bf16[1,128,128]{2,1,0:T(8,128)(2,1)S(1)}, u32[]{:S(2)}, u32[]{:S(2)}) collective-permute-start(bf16[1,128,128]{2,1,0:T(8,128)(2,1)S(1)} %get-tuple-element.61), channel_id=1, source_target_pairs={{0,2},{1,3},{2,4},{3,5},{4,6},{5,7},{6,8},{7,9},{8,10},{9,11},{10,... | collective-permute-start | bytes 98312 | tf_op jit(solution)/shard_map/ppermute | solution.py:10
  19.5 21.6 %collective-permute-start.3 = (bf16[1,128,128]{2,1,0:T(8,128)(2,1)S(1)}, bf16[1,128,128]{2,1,0:T(8,128)(2,1)S(1)}, u32[]{:S(2)}, u32[]{:S(2)}) collective-permute-start(bf16[1,128,128]{2,1,0:T(8,128)(2,1)S(1)} %get-tuple-element.61), channel_id=1, source_target_pairs={{2,0},{3,1},{4,2},{5,3},{6,4},{7,5},{8,6},{9,7},{10,8},{11,9},{12,... | collective-permute-start | bytes 98312 | tf_op jit(solution)/shard_map/ppermute | solution.py:10
  20.8 20.3 %collective-permute-start.4 = (bf16[1,128,128]{2,1,0:T(8,128)(2,1)S(1)}, bf16[1,128,128]{2,1,0:T(8,128)(2,1)S(1)}, u32[]{:S(2)}, u32[]{:S(2)}) collective-permute-start(bf16[1,128,128]{2,1,0:T(8,128)(2,1)S(1)} %get-tuple-element.61), channel_id=1, source_target_pairs={{0,3},{1,4},{2,5},{3,6},{4,7},{5,8},{6,9},{7,10},{8,11},{9,12},{10... | collective-permute-start | bytes 98312 | tf_op jit(solution)/shard_map/ppermute | solution.py:10
  29.3 11.9 %collective-permute-start.5 = (bf16[1,128,128]{2,1,0:T(8,128)(2,1)S(1)}, bf16[1,128,128]{2,1,0:T(8,128)(2,1)S(1)}, u32[]{:S(2)}, u32[]{:S(2)}) collective-permute-start(bf16[1,128,128]{2,1,0:T(8,128)(2,1)S(1)} %get-tuple-element.61), channel_id=1, source_target_pairs={{3,0},{4,1},{5,2},{6,3},{7,4},{8,5},{9,6},{10,7},{11,8},{12,9},{13... | collective-permute-start | bytes 98312 | tf_op jit(solution)/shard_map/ppermute | solution.py:10
  30.6 10.6 %collective-permute-start.6 = (bf16[1,128,128]{2,1,0:T(8,128)(2,1)S(1)}, bf16[1,128,128]{2,1,0:T(8,128)(2,1)S(1)}, u32[]{:S(2)}, u32[]{:S(2)}) collective-permute-start(bf16[1,128,128]{2,1,0:T(8,128)(2,1)S(1)} %get-tuple-element.61), channel_id=1, source_target_pairs={{0,4},{1,5},{2,6},{3,7},{4,8},{5,9},{6,10},{7,11},{8,12},{9,13},{1... | collective-permute-start | bytes 98312 | tf_op jit(solution)/shard_map/ppermute | solution.py:10
  46.6 191.1 %all-gather.5.cloned.1.call-start = ((), (), s32[]{:S(2)}) async-start(), calls=%async_computation.1 | async-start | bytes 15597568 | tf_op jit(solution)/shard_map/all_gather | solution.py:70
  125.4 33.0 %collective-permute-start.16 = (bf16[1,128,128]{2,1,0:T(8,128)(2,1)S(1)}, bf16[1,128,128]{2,1,0:T(8,128)(2,1)S(1)}, u32[]{:S(2)}, u32[]{:S(2)}) collective-permute-start(bf16[1,128,128]{2,1,0:T(8,128)(2,1)S(1)} %get-tuple-element.57), channel_id=1, source_target_pairs={{0,1},{1,2},{2,3},{3,4},{4,5},{5,6},{6,7},{7,8},{8,9},{9,10},{10,1... | collective-permute-start | bytes 98312 | tf_op jit(solution)/shard_map/ppermute | solution.py:10
  128.6 31.1 %collective-permute-start.17 = (bf16[1,128,128]{2,1,0:T(8,128)(2,1)S(1)}, bf16[1,128,128]{2,1,0:T(8,128)(2,1)S(1)}, u32[]{:S(2)}, u32[]{:S(2)}) collective-permute-start(bf16[1,128,128]{2,1,0:T(8,128)(2,1)S(1)} %get-tuple-element.57), channel_id=1, source_target_pairs={{1,0},{2,1},{3,2},{4,3},{5,4},{6,5},{7,6},{8,7},{9,8},{10,9},{11,1... | collective-permute-start | bytes 98312 | tf_op jit(solution)/shard_map/ppermute | solution.py:10
  130.5 35.8 %collective-permute-start.18 = (bf16[1,128,128]{2,1,0:T(8,128)(2,1)S(1)}, bf16[1,128,128]{2,1,0:T(8,128)(2,1)S(1)}, u32[]{:S(2)}, u32[]{:S(2)}) collective-permute-start(bf16[1,128,128]{2,1,0:T(8,128)(2,1)S(1)} %get-tuple-element.57), channel_id=1, source_target_pairs={{0,2},{1,3},{2,4},{3,5},{4,6},{5,7},{6,8},{7,9},{8,10},{9,11},{10,... | collective-permute-start | bytes 98312 | tf_op jit(solution)/shard_map/ppermute | solution.py:10
  132.8 34.8 %collective-permute-start.19 = (bf16[1,128,128]{2,1,0:T(8,128)(2,1)S(1)}, bf16[1,128,128]{2,1,0:T(8,128)(2,1)S(1)}, u32[]{:S(2)}, u32[]{:S(2)}) collective-permute-start(bf16[1,128,128]{2,1,0:T(8,128)(2,1)S(1)} %get-tuple-element.57), channel_id=1, source_target_pairs={{2,0},{3,1},{4,2},{5,3},{6,4},{7,5},{8,6},{9,7},{10,8},{11,9},{12,... | collective-permute-start | bytes 98312 | tf_op jit(solution)/shard_map/ppermute | solution.py:10
  134.1 35.7 %collective-permute-start.20 = (bf16[1,128,128]{2,1,0:T(8,128)(2,1)S(1)}, bf16[1,128,128]{2,1,0:T(8,128)(2,1)S(1)}, u32[]{:S(2)}, u32[]{:S(2)}) collective-permute-start(bf16[1,128,128]{2,1,0:T(8,128)(2,1)S(1)} %get-tuple-element.57), channel_id=1, source_target_pairs={{0,3},{1,4},{2,5},{3,6},{4,7},{5,8},{6,9},{7,10},{8,11},{9,12},{10... | collective-permute-start | bytes 98312 | tf_op jit(solution)/shard_map/ppermute | solution.py:10
  158.4 13.7 %collective-permute-start.21 = (bf16[1,128,128]{2,1,0:T(8,128)(2,1)S(1)}, bf16[1,128,128]{2,1,0:T(8,128)(2,1)S(1)}, u32[]{:S(2)}, u32[]{:S(2)}) collective-permute-start(bf16[1,128,128]{2,1,0:T(8,128)(2,1)S(1)} %get-tuple-element.57), channel_id=1, source_target_pairs={{3,0},{4,1},{5,2},{6,3},{7,4},{8,5},{9,6},{10,7},{11,8},{12,9},{13... | collective-permute-start | bytes 98312 | tf_op jit(solution)/shard_map/ppermute | solution.py:10
  159.7 18.8 %collective-permute-start.22 = (bf16[1,128,128]{2,1,0:T(8,128)(2,1)S(1)}, bf16[1,128,128]{2,1,0:T(8,128)(2,1)S(1)}, u32[]{:S(2)}, u32[]{:S(2)}) collective-permute-start(bf16[1,128,128]{2,1,0:T(8,128)(2,1)S(1)} %get-tuple-element.57), channel_id=1, source_target_pairs={{0,4},{1,5},{2,6},{3,7},{4,8},{5,9},{6,10},{7,11},{8,12},{9,13},{1... | collective-permute-start | bytes 98312 | tf_op jit(solution)/shard_map/ppermute | solution.py:10
  166.3 13.5 %collective-permute-start.23 = (bf16[1,128,128]{2,1,0:T(8,128)(2,1)S(1)}, bf16[1,128,128]{2,1,0:T(8,128)(2,1)S(1)}, u32[]{:S(2)}, u32[]{:S(2)}) collective-permute-start(bf16[1,128,128]{2,1,0:T(8,128)(2,1)S(1)} %get-tuple-element.57), channel_id=1, source_target_pairs={{4,0},{5,1},{6,2},{7,3},{8,4},{9,5},{10,6},{11,7},{12,8},{13,9},{1... | collective-permute-start | bytes 98312 | tf_op jit(solution)/shard_map/ppermute | solution.py:10
  167.6 18.2 %collective-permute-start.8 = (bf16[1,128,128]{2,1,0:T(8,128)(2,1)S(1)}, bf16[1,128,128]{2,1,0:T(8,128)(2,1)S(1)}, u32[]{:S(2)}, u32[]{:S(2)}) collective-permute-start(bf16[1,128,128]{2,1,0:T(8,128)(2,1)S(1)} %get-tuple-element.59), channel_id=1, source_target_pairs={{0,1},{1,2},{2,3},{3,4},{4,5},{5,6},{6,7},{7,8},{8,9},{9,10},{10,1... | collective-permute-start | bytes 98312 | tf_op jit(solution)/shard_map/ppermute | solution.py:10
  169.8 17.3 %collective-permute-start.9 = (bf16[1,128,128]{2,1,0:T(8,128)(2,1)S(1)}, bf16[1,128,128]{2,1,0:T(8,128)(2,1)S(1)}, u32[]{:S(2)}, u32[]{:S(2)}) collective-permute-start(bf16[1,128,128]{2,1,0:T(8,128)(2,1)S(1)} %get-tuple-element.59), channel_id=1, source_target_pairs={{1,0},{2,1},{3,2},{4,3},{5,4},{6,5},{7,6},{8,7},{9,8},{10,9},{11,1... | collective-permute-start | bytes 98312 | tf_op jit(solution)/shard_map/ppermute | solution.py:10
  172.0 24.0 %collective-permute-start.10 = (bf16[1,128,128]{2,1,0:T(8,128)(2,1)S(1)}, bf16[1,128,128]{2,1,0:T(8,128)(2,1)S(1)}, u32[]{:S(2)}, u32[]{:S(2)}) collective-permute-start(bf16[1,128,128]{2,1,0:T(8,128)(2,1)S(1)} %get-tuple-element.59), channel_id=1, source_target_pairs={{0,2},{1,3},{2,4},{3,5},{4,6},{5,7},{6,8},{7,9},{8,10},{9,11},{10,... | collective-permute-start | bytes 98312 | tf_op jit(solution)/shard_map/ppermute | solution.py:10
  178.5 18.8 %collective-permute-start.11 = (bf16[1,128,128]{2,1,0:T(8,128)(2,1)S(1)}, bf16[1,128,128]{2,1,0:T(8,128)(2,1)S(1)}, u32[]{:S(2)}, u32[]{:S(2)}) collective-permute-start(bf16[1,128,128]{2,1,0:T(8,128)(2,1)S(1)} %get-tuple-element.59), channel_id=1, source_target_pairs={{2,0},{3,1},{4,2},{5,3},{6,4},{7,5},{8,6},{9,7},{10,8},{11,9},{12,... | collective-permute-start | bytes 98312 | tf_op jit(solution)/shard_map/ppermute | solution.py:10
  179.8 17.5 %collective-permute-start.12 = (bf16[1,128,128]{2,1,0:T(8,128)(2,1)S(1)}, bf16[1,128,128]{2,1,0:T(8,128)(2,1)S(1)}, u32[]{:S(2)}, u32[]{:S(2)}) collective-permute-start(bf16[1,128,128]{2,1,0:T(8,128)(2,1)S(1)} %get-tuple-element.59), channel_id=1, source_target_pairs={{0,3},{1,4},{2,5},{3,6},{4,7},{5,8},{6,9},{7,10},{8,11},{9,12},{10... | collective-permute-start | bytes 98312 | tf_op jit(solution)/shard_map/ppermute | solution.py:10
  185.9 11.5 %collective-permute-start.13 = (bf16[1,128,128]{2,1,0:T(8,128)(2,1)S(1)}, bf16[1,128,128]{2,1,0:T(8,128)(2,1)S(1)}, u32[]{:S(2)}, u32[]{:S(2)}) collective-permute-start(bf16[1,128,128]{2,1,0:T(8,128)(2,1)S(1)} %get-tuple-element.59), channel_id=1, source_target_pairs={{3,0},{4,1},{5,2},{6,3},{7,4},{8,5},{9,6},{10,7},{11,8},{12,9},{13... | collective-permute-start | bytes 98312 | tf_op jit(solution)/shard_map/ppermute | solution.py:10
  187.2 10.2 %collective-permute-start.14 = (bf16[1,128,128]{2,1,0:T(8,128)(2,1)S(1)}, bf16[1,128,128]{2,1,0:T(8,128)(2,1)S(1)}, u32[]{:S(2)}, u32[]{:S(2)}) collective-permute-start(bf16[1,128,128]{2,1,0:T(8,128)(2,1)S(1)} %get-tuple-element.59), channel_id=1, source_target_pairs={{0,4},{1,5},{2,6},{3,7},{4,8},{5,9},{6,10},{7,11},{8,12},{9,13},{1... | collective-permute-start | bytes 98312 | tf_op jit(solution)/shard_map/ppermute | solution.py:10
  (2 other events, 11.5 us)
Sparse Core Ops, SparseCore 0:
  46.8 74.6 all-gather.2
  125.1 112.6 all-gather.4
where the time goes:
time: 265 us; the launch traced here: 264 us
  waiting for transfers between devices  116 us (44%)
  starting transfers between devices  82.8 us (31%)
  local copies, waits for them, and re-layouts  25.6 us (10%)
  between operations  15.3 us (6%)
  matrix products  13.5 us (5%)
  other arithmetic  11.3 us (4%)
    ppermute x24, starting transfers between devices, passed_along(): return lax.ppermute(block, axis, route)  82.7 us
    all_gather x1, waiting for transfers between devices, on_device(): group_cells = lax.all_gather(cell_blocks, 'dp', axis=0, tiled=True)  73.8 us
    all_gather x1, waiting for transfers between devices, on_device(): panel_piece = lax.all_gather(panel, 'fsdp', axis=0, tiled=True)  34.5 us
    dot_general x1, matrix products, on_device(): jnp.einsum('tcka,ckab->tcb', picked, panel_piece, preferred_element_type=...  13.5 us
    gather x1, local copies, waits for them, and re-layouts, on_device(): picked = jnp.take(token_blocks, new_rows.reshape(-1), axis=1)  13.3 us
    unnamed x4, local copies, waits for them, and re-layouts  9.25 us
    ppermute x24, waiting for transfers between devices, passed_along(): return lax.ppermute(block, axis, route)  7.47 us
  transfers between devices with their start and end apart: 26, of which 4 were waited for; matrix products, arithmetic and copies ran while one was open for 10% of the time, Pallas kernels for 0%

commit v1 on v0

v1 whole, which is shorter than its diff:
```python
import numpy as np
import jax
import jax.numpy as jnp
from jax import lax
from jax.experimental import pallas as pl
from jax.experimental.pallas import tpu as pltpu
from jax.sharding import Mesh, PartitionSpec as P

BF = jnp.bfloat16
F32 = jnp.float32
X, Y, Z, C = 4, 4, 16, 2
G = X * Y
B = 128
COLS = 7
K = 4
MINE = 14
T = 128
ALL = ("x", "y", "z", "core")
VMEM = pl.BlockSpec(memory_space=pltpu.VMEM)
SMEM = pl.BlockSpec(memory_space=pltpu.SMEM)
PARAMS = pltpu.CompilerParams(vmem_limit_bytes=48 << 20)


def device(x, y, z, c):
    return ((x * Y + y) * Z + z) * C + c


def line_groups(first):
    out = []
    for c in range(C):
        for z in range(Z):
            for o in range(4):
                along_x = (c == 0) == first
                out.append([device(i, o, z, c) if along_x else device(o, i, z, c) for i in range(4)])
    return out


def slot_of(c, j):
    return (3 * c + j // K, j % K) if j < 12 else (COLS - 1, 2 * c + j - 12)


def group_at(c, i):
    return jnp.where(c == 0, (i % 4) * 4 + i // 4, i)


def prep_kernel(place, old, new, regrown, master, block, info):
    cell = place[0]
    above, below = (cell + 1) % (Z * C), (cell - 1) % (Z * C)

    def look(s, carry):
        kept, o0, k0, op, om = carry
        o, n, r = old[s % K, s // K], new[s % K, s // K], regrown[s % K, s // K]
        kept = jnp.where((o == cell) & (r == 0), 1, kept)
        k0 = jnp.where((n == cell) & (r == 0), 1, k0)
        o0 = jnp.where(n == cell, o, o0)
        op = jnp.where(n == above, o, op)
        om = jnp.where(n == below, o, om)
        return kept, o0, k0, op, om

    kept, o0, k0, op, om = lax.fori_loop(
        0, COLS * K, look, (jnp.int32(0), cell, jnp.int32(0), above, below), unroll=True
    )

    def split(d):
        a = (d + 1 > 1).astype(jnp.int32) * (d > 1).astype(jnp.int32) - (d < -1).astype(jnp.int32)
        return a, d - 3 * a

    a0, b0 = split(cell - o0)
    ap, _ = split(above - op)
    am, _ = split(below - om)
    info[0] = k0
    info[1] = a0
    info[2] = b0
    info[3] = ap
    info[4] = am
    block[0] = jnp.where(kept == 1, master[0], 0.0).astype(BF)


def middle_kernel(info, own, low, high, up, down):
    for out, at in ((up, 3), (down, 4)):
        a = info[at]
        out[...] = jnp.where(a == 0, own[...], jnp.where(a == 1, low[...], high[...]))


def settle_kernel(info, master, moment, second, low, high, below, above, *outs):
    keep, a, b = info[0], info[1], info[2]
    for m, (own, out) in enumerate(zip((master, moment, second), outs)):
        same = jnp.where(a == 0, own[0], jnp.where(a == 1, low[m], high[m]).astype(F32))
        moved = jnp.where(b == 1, below[m], above[m]).astype(F32)
        value = jnp.where(b == 0, same, moved)
        out[0] = jnp.where(keep == 1, value, 0.0)


def pick_kernel(place, old, own, other, out):
    c = place[1]
    for j in range(MINE):
        if j < 12:
            o = old[j % K, 3 * c + j // K]
        else:
            o = old[2 * c + j - 12, COLS - 1]
        at = o // 2
        block = jnp.where(o % 2 == c, own[at], other[at])
        for t in range(4):
            out[t, j] = block


def product_kernel(place, rows, mine, theirs, blocks, own3, own6, send):
    c = place[1]

    def group(i, _):
        f = group_at(c, i)
        for j in range(4):
            col = f * COLS + (3 * c + j if j < 3 else COLS - 1)
            count = K if j < 3 else 2
            ks = [k if j < 3 else 2 * c + k for k in range(count)]
            at = [pl.multiple_of(rows[k, col] * B, B) for k in ks]
            left = jnp.concatenate(
                [jnp.concatenate([ref[:, pl.ds(p, B)] for p in at], axis=1) for ref in (mine, theirs)], axis=0
            )
            right = blocks[pl.ds(i * MINE + j * K, count)].reshape(count * B, B)
            acc = jnp.dot(left, right, preferred_element_type=F32)
            if j < 3:
                own3[:, pl.ds(pl.multiple_of(i * 384 + j * B, B), B)] = acc[:T].astype(BF)
            else:
                own6[:, pl.ds(pl.multiple_of(i * B, B), B)] = acc[:T]
            send[:, pl.ds(pl.multiple_of(i * 512 + j * B, B), B)] = acc[T:].astype(BF)
        return 0

    lax.fori_loop(0, G, group, 0)


def join_kernel(place, own3, own6, got, out):
    c = place[1]
    for t in range(4):
        f = pl.program_id(0) * 4 + t
        turned = (f % 4) * 4 + f // 4
        i = jnp.where(c == 0, turned, f)
        o = jnp.where(c == 0, f, turned)
        base = t * COLS * B
        out[:, pl.ds(pl.multiple_of(base + c * 384, B), 384)] = own3[:, pl.ds(pl.multiple_of(i * 384, B), 384)]
        out[:, pl.ds(pl.multiple_of(base + (1 - c) * 384, B), 384)] = got[:, pl.ds(pl.multiple_of(o * 512, B), 384)]
        last = own6[:, pl.ds(pl.multiple_of(i * B, B), B)]
        last = last + got[:, pl.ds(pl.multiple_of(o * 512 + 384, B), B)].astype(F32)
        out[:, base + 768 : base + 896] = last.astype(BF)


def gather(blocks, groups):
    return lax.all_to_all(blocks, ALL, 0, 0, tiled=True, axis_index_groups=groups)


def to_sibling(value):
    return lax.ppermute(value, "core", [(0, 1), (1, 0)])


def along_cells(value, distance):
    route = [(i, (i + distance) % (Z * C)) for i in range(Z * C)]
    return lax.ppermute(value, ("z", "core"), route)


def call(kernel, shapes, in_specs, out_specs, name, **more):
    out = [jax.ShapeDtypeStruct(s, d) for s, d in shapes]
    return pl.pallas_call(
        kernel, out_shape=out, in_specs=in_specs, out_specs=out_specs, name=name, compiler_params=PARAMS, **more
    )


def on_device(tokens, master, moment, second, old_cell, new_cell, regrown, new_rows):
    c = lax.axis_index("core")
    cell = lax.axis_index("z") * C + c
    place = jnp.stack([cell, c]).astype(jnp.int32)
    theirs = to_sibling(tokens)
    old_cell, new_cell, regrown = old_cell.T, new_cell.T, regrown.T
    block, info = call(
        prep_kernel, [((1, B, B), BF), ((8,), jnp.int32)], [SMEM] * 4 + [VMEM], [VMEM, SMEM], "prep"
    )(place, old_cell, new_cell, regrown, master)
    own = lax.all_gather(block, "z", axis=0, tiled=True)
    other = to_sibling(own)
    (picked,) = call(pick_kernel, [((4, MINE, B, B), BF)], [SMEM, SMEM, VMEM, VMEM], [VMEM], "pick")(
        place, old_cell, own, other
    )
    line = gather(picked, line_groups(True)).reshape(4 * MINE, B, B)
    line, master, moment, second = lax.optimization_barrier((line, master, moment, second))
    load = jnp.concatenate([master, moment, second]).astype(BF)
    low = along_cells(load, 3)
    high = along_cells(load, -3)
    up, down = call(middle_kernel, [((3, B, B), BF)] * 2, [SMEM] + [VMEM] * 3, [VMEM] * 2, "middle")(
        info, load, low, high
    )
    below = along_cells(up, 1)
    above = along_cells(down, -1)
    wide = jnp.broadcast_to(line[None], (4, 4 * MINE, B, B))
    blocks = gather(wide, line_groups(False)).reshape(G * MINE, B, B)
    states = call(settle_kernel, [((1, B, B), F32)] * 3, [SMEM] + [VMEM] * 7, [VMEM] * 3, "settle")(
        info, master, moment, second, low, high, below, above
    )
    tokens, theirs, states = lax.optimization_barrier((tokens, theirs, tuple(states)))
    own3, own6, send = call(
        product_kernel,
        [((T, G * 384), BF), ((T, G * B), F32), ((T, G * 512), BF)],
        [SMEM, SMEM, VMEM, VMEM, VMEM],
        [VMEM] * 3,
        "product",
    )(place, new_rows.T, tokens, theirs, blocks)
    got = to_sibling(send)
    (hidden,) = call(
        join_kernel,
        [((T, G * COLS * B), BF)],
        [SMEM, VMEM, VMEM, VMEM],
        [pl.BlockSpec((T, 4 * COLS * B), lambda g: (0, g))],
        "join",
        grid=(4,),
    )(place, own3, own6, got)
    return (hidden, *states)


def solution(mesh):
    fine = Mesh(np.asarray(mesh.devices).reshape(X, Y, Z, C), ALL)
    return jax.shard_map(
        on_device,
        mesh=fine,
        in_specs=(P(ALL, None),) + (P(ALL, None, None),) * 3 + (P(("x", "y"), None),) * 3 + (P(),),
        out_specs=(P(ALL, None),) + (P(ALL, None, None),) * 3,
        check_vma=False,
    )
```

time: 265 us -> 145 us (0.55)
  waiting for transfers between devices: 116 us -> 35.5 us
  starting transfers between devices: 82.8 us -> 31.6 us
  blocking collectives: 0 us -> 50 us
  Pallas kernels: 0 us -> 18.3 us
  local copies, waits for them, and re-layouts: 25.6 us -> 7.78 us
  between operations: 15.3 us -> 0.8 us
  matrix products: 13.5 us -> 0 us
  other arithmetic: 11.3 us -> 0.11 us
    all_gather x2 -> x0, waiting for transfers between devices: 108 us -> none  [the longest x1 73.8 us: on_device(): group_cells = lax.all_gather(cell_blocks, 'dp', axis=0, tiled=True)]
    ppermute x24 -> x7, starting transfers between devices: 82.7 us -> 26 us  [the longest x3 17.4 us: to_sibling(): return lax.ppermute(value, 'core', [(0, 1), (1, 0)])]
    all_gather x0 -> x1, blocking collectives: none -> 31.8 us  [on_device(): own = lax.all_gather(block, 'z', axis=0, tiled=True)]
    all_to_all x0 -> x1, waiting for transfers between devices: none -> 22.2 us  [gather(): lax.all_to_all(blocks, ALL, 0, 0, tiled=True, axis_index_groups=groups)]
    pallas_call x0 -> x6, Pallas kernels: none -> 18.3 us  [the longest x1 11 us: on_device(): call(product_kernel, [((T, G * 384), BF), ((T, G * B), F32), ((T, G * 512...]
    all_to_all x0 -> x1, blocking collectives: none -> 18.2 us  [gather(): lax.all_to_all(blocks, ALL, 0, 0, tiled=True, axis_index_groups=groups)]
    gather x2 -> x0, local copies, waits for them, and re-layouts: 15.2 us -> none  [the longest x1 13.3 us: on_device(): picked = jnp.take(token_blocks, new_rows.reshape(-1), axis=1)]
    dot_general x1 -> x0, matrix products: 13.5 us -> none  [on_device(): jnp.einsum('tcka,ckab->tcb', picked, panel_piece, preferred_element_type=...]
  transfers between devices with their start and end apart: 26 -> 8, of which waited for: 4 -> 7; matrix products, arithmetic and copies ran while one was open for 10% -> 0% of each run, Pallas kernels for 0% -> 1%
where the time goes in v1:
time: 145 us; the launch traced here: 144 us
  blocking collectives  50 us (34%)
  waiting for transfers between devices  35.5 us (24%)
  starting transfers between devices  31.6 us (22%)
  Pallas kernels  18.3 us (13%)
  local copies, waits for them, and re-layouts  7.78 us (5%)
    all_gather x1, blocking collectives, on_device(): own = lax.all_gather(block, 'z', axis=0, tiled=True)  31.8 us
    all_to_all x1, waiting for transfers between devices, gather(): lax.all_to_all(blocks, ALL, 0, 0, tiled=True, axis_index_groups=groups)  22.2 us
    all_to_all x1, blocking collectives, gather(): lax.all_to_all(blocks, ALL, 0, 0, tiled=True, axis_index_groups=groups)  18.2 us
    ppermute x3, starting transfers between devices, to_sibling(): return lax.ppermute(value, 'core', [(0, 1), (1, 0)])  17.4 us
    pallas_call x1, Pallas kernels, on_device(): call(product_kernel, [((T, G * 384), BF), ((T, G * B), F32), ((T, G * 512...  11 us
    ppermute x4, starting transfers between devices, along_cells(): return lax.ppermute(value, ('z', 'core'), route)  8.56 us
    ppermute x4, waiting for transfers between devices, along_cells(): return lax.ppermute(value, ('z', 'core'), route)  7.79 us
    all_to_all x1, starting transfers between devices, gather(): lax.all_to_all(blocks, ALL, 0, 0, tiled=True, axis_index_groups=groups)  5.6 us
  transfers between devices with their start and end apart: 8, of which 7 were waited for; matrix products, arithmetic and copies ran while one was open for 0% of the time, Pallas kernels for 1%

profile of v1, /device:TPU:1, one launch (start us, length us, event | category | flops | bytes accessed | tf_op | source)
XLA Modules:
  0.0 144.1 jit_solution(12187026939212868688)
XLA Ops:
  0.7 0.8 copy-done.1
  3.6 1.4 prep.1
  5.0 31.8 %all_gather.3.own = bf16[16,128,128]{2,1,0:T(8,128)(2,1)S(1)} all-gather(bf16[1,128,128]{2,1,0:T(8,128)(2,1)S(1)} %get-tuple-element.24), channel_id=1, replica_groups=mesh['x'=4,'y'=4,'z'=16,'core'=2] {'z'}, dimensions={0}, use_global_device_ids=true | all-gather | bytes 557056 | tf_op jit(solution)/shard_map/all_gather | solution.py:176
  36.8 10.1 %collective-permute-start.1 = (bf16[16,128,128]{2,1,0:T(8,128)(2,1)S(1)}, bf16[16,128,128]{2,1,0:T(8,128)(2,1)S(1)}, u32[]{:S(2)}, u32[]{:S(2)}) collective-permute-start(bf16[16,128,128]{2,1,0:T(8,128)(2,1)S(1)} %all_gather.3.own), channel_id=1, source_target_pairs={{0,1},{1,0},{2,3},{3,2},{4,5},{5,4},{6,7},{7,6},{8,9},{9,8},{10,11... | collective-permute-start | bytes 1572872 | tf_op jit(solution)/shard_map/ppermute | solution.py:152
  46.9 1.5 %collective-permute-done.1.other = bf16[16,128,128]{2,1,0:T(8,128)(2,1)S(1)} collective-permute-done((bf16[16,128,128]{2,1,0:T(8,128)(2,1)S(1)}, bf16[16,128,128]{2,1,0:T(8,128)(2,1)S(1)}, u32[]{:S(2)}, u32[]{:S(2)}) %collective-permute-start.1) | collective-permute-done | bytes 524320 | tf_op jit(solution)/shard_map/ppermute | solution.py:152
  48.5 0.9 pick.1
  49.3 18.2 %all_to_all.10 = bf16[4,14,128,128]{3,2,1,0:T(8,128)(2,1)S(1)} all-to-all(bf16[4,14,128,128]{3,2,1,0:T(8,128)(2,1)S(1)} %pick.1), channel_id=1, replica_groups={{0,128,256,384},{32,160,288,416},{64,192,320,448},{96,224,352,480},{2,1..., dimensions={0} | all-to-all | bytes 3670016 | tf_op jit(solution)/shard_map/all_to_all | solution.py:148
  67.6 4.9 %broadcast_in_dim.2 = bf16[4,56,128,128]{3,2,1,0:T(8,128)(2,1)} broadcast(bf16[56,128,128]{2,1,0:T(8,128)(2,1)S(1)} %bitcast.13), dimensions={1,2,3} | broadcast | bytes 9175040 | tf_op jit(solution)/shard_map/broadcast_in_dim | solution.py:191
  72.5 5.6 %all-to-all-start.1 = ((bf16[4,56,128,128]{3,2,1,0:T(8,128)(2,1)}), bf16[4,56,128,128]{3,2,1,0:T(8,128)(2,1)}, u32[]{:S(2)}, u32[]{:S(2)}) async-start(bf16[4,56,128,128]{3,2,1,0:T(8,128)(2,1)} %broadcast_in_dim.2), calls=%async_computation.1 | async-start | bytes 14680064 | tf_op jit(solution)/shard_map/all_to_all | solution.py:148
  78.1 3.2 %collective-permute-start = (bf16[128,4096]{1,0:T(8,128)(2,1)S(1)}, bf16[128,4096]{1,0:T(8,128)(2,1)S(1)}, u32[]{:S(2)}, u32[]{:S(2)}) collective-permute-start(bf16[128,4096]{1,0:T(8,128)(2,1)S(1)} %copy-done), channel_id=1, source_target_pairs={{0,1},{1,0},{2,3},{3,2},{4,5},{5,4},{6,7},{7,6},{8,9},{9,8},{10,11... | collective-permute-start | bytes 3145736 | tf_op jit(solution)/shard_map/ppermute | solution.py:152
  81.4 1.9 %collective-permute-start.3 = (bf16[3,128,128]{2,1,0:T(8,128)(2,1)S(1)}, bf16[3,128,128]{2,1,0:T(8,128)(2,1)S(1)}, u32[]{:S(2)}, u32[]{:S(2)}) collective-permute-start(bf16[3,128,128]{2,1,0:T(8,128)(2,1)S(1)} %pad_maximum_fusion.own), channel_id=1, source_target_pairs={{0,29},{1,30},{2,31},{3,0},{4,1},{5,2},{6,3},{7,4},{8,5},{9,6},{10... | collective-permute-start | bytes 294920 | tf_op jit(solution)/shard_map/ppermute | solution.py:157
  83.4 4.5 %collective-permute-start.2 = (bf16[3,128,128]{2,1,0:T(8,128)(2,1)S(1)}, bf16[3,128,128]{2,1,0:T(8,128)(2,1)S(1)}, u32[]{:S(2)}, u32[]{:S(2)}) collective-permute-start(bf16[3,128,128]{2,1,0:T(8,128)(2,1)S(1)} %pad_maximum_fusion.own), channel_id=1, source_target_pairs={{0,3},{1,4},{2,5},{3,6},{4,7},{5,8},{6,9},{7,10},{8,11},{9,12},{10... | collective-permute-start | bytes 294920 | tf_op jit(solution)/shard_map/ppermute | solution.py:157
  87.9 1.0 collective-permute-done.3.high
  88.9 3.0 %collective-permute-done.2.low = bf16[3,128,128]{2,1,0:T(8,128)(2,1)S(1)} collective-permute-done((bf16[3,128,128]{2,1,0:T(8,128)(2,1)S(1)}, bf16[3,128,128]{2,1,0:T(8,128)(2,1)S(1)}, u32[]{:S(2)}, u32[]{:S(2)}) %collective-permute-start.2) | collective-permute-done | bytes 98336 | tf_op jit(solution)/shard_map/ppermute | solution.py:157
  92.6 1.4 collective-permute-start.4
  94.0 0.7 collective-permute-start.5
  94.7 0.9 collective-permute-done.4.below
  95.6 2.8 %collective-permute-done.5.above = bf16[3,128,128]{2,1,0:T(8,128)(2,1)S(1)} collective-permute-done((bf16[3,128,128]{2,1,0:T(8,128)(2,1)S(1)}, bf16[3,128,128]{2,1,0:T(8,128)(2,1)S(1)}, u32[]{:S(2)}, u32[]{:S(2)}) %collective-permute-start.5) | collective-permute-done | bytes 98336 | tf_op jit(solution)/shard_map/ppermute | solution.py:157
  98.4 1.3 settle.1
  99.7 22.2 %all-to-all-done.1 = bf16[4,56,128,128]{3,2,1,0:T(8,128)(2,1)} async-done(((bf16[4,56,128,128]{3,2,1,0:T(8,128)(2,1)}), bf16[4,56,128,128]{3,2,1,0:T(8,128)(2,1)}, u32[]{:S(2)}, u32[]{:S(2)}) %all-to-all-start.1) | async-done | bytes 7340064 | tf_op jit(solution)/shard_map/all_to_all | solution.py:148
  121.9 11.0 %product.1 = (bf16[128,6144]{1,0:T(8,128)(2,1)S(1)}, f32[128,2048]{1,0:T(8,128)S(1)}, bf16[128,8192]{1,0:T(8,128)(2,1)}) custom-call(s32[2]{0:T(128)S(1)} %pad_add_fusion.place, s32[4,112]{1,0:T(4,128)S(1)} %bitcast.12, bf16[128,4096]{1,0:T(8,128)(2,1)S(1)} %copy-done, bf16[128,4096]{1,0:T(8,128)(2,1)S(1)} %collective-permute-done.theirs, ...), custom_call_target="tpu_custom_call" | custom-call | tf_op jit(solution)/shard_map/product/pallas_call | solution.py:197
  132.9 4.1 %collective-permute-start.6 = (bf16[128,8192]{1,0:T(8,128)(2,1)}, bf16[128,8192]{1,0:T(8,128)(2,1)S(1)}, u32[]{:S(2)}, u32[]{:S(2)}) collective-permute-start(bf16[128,8192]{1,0:T(8,128)(2,1)} %get-tuple-element.38), channel_id=1, source_target_pairs={{0,1},{1,0},{2,3},{3,2},{4,5},{5,4},{6,7},{7,6},{8,9},{9,8},{10,11... | collective-permute-start | bytes 6291464 | tf_op jit(solution)/shard_map/ppermute | solution.py:152
  137.0 4.0 %collective-permute-done.6.got = bf16[128,8192]{1,0:T(8,128)(2,1)S(1)} collective-permute-done((bf16[128,8192]{1,0:T(8,128)(2,1)}, bf16[128,8192]{1,0:T(8,128)(2,1)S(1)}, u32[]{:S(2)}, u32[]{:S(2)}) %collective-permute-start.6) | collective-permute-done | bytes 2097184 | tf_op jit(solution)/shard_map/ppermute | solution.py:152
  141.0 3.1 %join.1 = bf16[128,14336]{1,0:T(8,128)(2,1)} custom-call(s32[2]{0:T(128)S(1)} %pad_add_fusion.place, bf16[128,6144]{1,0:T(8,128)(2,1)S(1)} %get-tuple-element.36.own3, f32[128,2048]{1,0:T(8,128)S(1)} %get-tuple-element.37.own6, bf16[128,8192]{1,0:T(8,128)(2,1)S(1)} %collective-permute-done.6.got), custom_call_target="tpu_custom_call" | custom-call | tf_op jit(solution)/shard_map/join/pallas_call | solution.py:205
  (24 shorter events, 2.8 us)
Async XLA Ops:
  0.7 0.8 copy-start.1
  1.6 0.7 copy-start.5
  2.2 0.7 copy-start.6
  2.9 0.7 copy-start.7
  36.8 11.7 %collective-permute-start.1 = (bf16[16,128,128]{2,1,0:T(8,128)(2,1)S(1)}, bf16[16,128,128]{2,1,0:T(8,128)(2,1)S(1)}, u32[]{:S(2)}, u32[]{:S(2)}) collective-permute-start(bf16[16,128,128]{2,1,0:T(8,128)(2,1)S(1)} %all_gather.3.own), channel_id=1, source_target_pairs={{0,1},{1,0},{2,3},{3,2},{4,5},{5,4},{6,7},{7,6},{8,9},{9,8},{10,11... | collective-permute-start | bytes 1572872 | tf_op jit(solution)/shard_map/ppermute | solution.py:152
  72.4 5.6 %copy-start = (bf16[128,4096]{1,0:T(8,128)(2,1)S(1)}, bf16[128,4096]{1,0:T(8,128)(2,1)}, u32[]{:S(2)}) copy-start(bf16[128,4096]{1,0:T(8,128)(2,1)} %mine) | copy-start | bytes 3145732
  72.4 8.9 %copy-start.2 = (f32[1,128,128]{2,1,0:T(8,128)S(1)}, f32[1,128,128]{2,1,0:T(8,128)}, u32[]{:S(2)}) copy-start(f32[1,128,128]{2,1,0:T(8,128)} %master.2) | copy-start | bytes 196612
  72.4 8.9 %copy-start.3 = (f32[1,128,128]{2,1,0:T(8,128)S(1)}, f32[1,128,128]{2,1,0:T(8,128)}, u32[]{:S(2)}) copy-start(f32[1,128,128]{2,1,0:T(8,128)} %moment) | copy-start | bytes 196612
  72.4 8.9 %copy-start.4 = (f32[1,128,128]{2,1,0:T(8,128)S(1)}, f32[1,128,128]{2,1,0:T(8,128)}, u32[]{:S(2)}) copy-start(f32[1,128,128]{2,1,0:T(8,128)} %second) | copy-start | bytes 196612
  72.5 49.4 %copy-start.8 = (s32[112,4]{0,1:T(4,128)S(1)}, s32[112,4]{0,1:T(4,128)}, u32[]{:S(2)}) copy-start(s32[112,4]{0,1:T(4,128)} %param.15) | copy-start | bytes 5380
  72.5 49.4 %all-to-all-start.1 = ((bf16[4,56,128,128]{3,2,1,0:T(8,128)(2,1)}), bf16[4,56,128,128]{3,2,1,0:T(8,128)(2,1)}, u32[]{:S(2)}, u32[]{:S(2)}) async-start(bf16[4,56,128,128]{3,2,1,0:T(8,128)(2,1)} %broadcast_in_dim.2), calls=%async_computation.1 | async-start | bytes 14680064 | tf_op jit(solution)/shard_map/all_to_all | solution.py:148
  78.1 21.6 %collective-permute-start = (bf16[128,4096]{1,0:T(8,128)(2,1)S(1)}, bf16[128,4096]{1,0:T(8,128)(2,1)S(1)}, u32[]{:S(2)}, u32[]{:S(2)}) collective-permute-start(bf16[128,4096]{1,0:T(8,128)(2,1)S(1)} %copy-done), channel_id=1, source_target_pairs={{0,1},{1,0},{2,3},{3,2},{4,5},{5,4},{6,7},{7,6},{8,9},{9,8},{10,11... | collective-permute-start | bytes 3145736 | tf_op jit(solution)/shard_map/ppermute | solution.py:152
  81.4 7.5 %collective-permute-start.3 = (bf16[3,128,128]{2,1,0:T(8,128)(2,1)S(1)}, bf16[3,128,128]{2,1,0:T(8,128)(2,1)S(1)}, u32[]{:S(2)}, u32[]{:S(2)}) collective-permute-start(bf16[3,128,128]{2,1,0:T(8,128)(2,1)S(1)} %pad_maximum_fusion.own), channel_id=1, source_target_pairs={{0,29},{1,30},{2,31},{3,0},{4,1},{5,2},{6,3},{7,4},{8,5},{9,6},{10... | collective-permute-start | bytes 294920 | tf_op jit(solution)/shard_map/ppermute | solution.py:157
  83.4 8.6 %collective-permute-start.2 = (bf16[3,128,128]{2,1,0:T(8,128)(2,1)S(1)}, bf16[3,128,128]{2,1,0:T(8,128)(2,1)S(1)}, u32[]{:S(2)}, u32[]{:S(2)}) collective-permute-start(bf16[3,128,128]{2,1,0:T(8,128)(2,1)S(1)} %pad_maximum_fusion.own), channel_id=1, source_target_pairs={{0,3},{1,4},{2,5},{3,6},{4,7},{5,8},{6,9},{7,10},{8,11},{9,12},{10... | collective-permute-start | bytes 294920 | tf_op jit(solution)/shard_map/ppermute | solution.py:157
  92.6 3.0 %collective-permute-start.4 = (bf16[3,128,128]{2,1,0:T(8,128)(2,1)S(1)}, bf16[3,128,128]{2,1,0:T(8,128)(2,1)S(1)}, u32[]{:S(2)}, u32[]{:S(2)}) collective-permute-start(bf16[3,128,128]{2,1,0:T(8,128)(2,1)S(1)} %get-tuple-element.28), channel_id=1, source_target_pairs={{0,1},{1,2},{2,3},{3,4},{4,5},{5,6},{6,7},{7,8},{8,9},{9,10},{10,1... | collective-permute-start | bytes 294920 | tf_op jit(solution)/shard_map/ppermute | solution.py:157
  94.0 4.4 %collective-permute-start.5 = (bf16[3,128,128]{2,1,0:T(8,128)(2,1)S(1)}, bf16[3,128,128]{2,1,0:T(8,128)(2,1)S(1)}, u32[]{:S(2)}, u32[]{:S(2)}) collective-permute-start(bf16[3,128,128]{2,1,0:T(8,128)(2,1)S(1)} %get-tuple-element.29), channel_id=1, source_target_pairs={{0,31},{1,0},{2,1},{3,2},{4,3},{5,4},{6,5},{7,6},{8,7},{9,8},{10,9... | collective-permute-start | bytes 294920 | tf_op jit(solution)/shard_map/ppermute | solution.py:157
  132.9 8.1 %collective-permute-start.6 = (bf16[128,8192]{1,0:T(8,128)(2,1)}, bf16[128,8192]{1,0:T(8,128)(2,1)S(1)}, u32[]{:S(2)}, u32[]{:S(2)}) collective-permute-start(bf16[128,8192]{1,0:T(8,128)(2,1)} %get-tuple-element.38), channel_id=1, source_target_pairs={{0,1},{1,0},{2,3},{3,2},{4,5},{5,4},{6,7},{7,6},{8,9},{9,8},{10,11... | collective-permute-start | bytes 6291464 | tf_op jit(solution)/shard_map/ppermute | solution.py:152

commit v2 on v1

--- a/solution.py
+++ b/solution.py
@@ -1,3 +1,4 @@
+import functools
 import numpy as np
 import jax
 import jax.numpy as jnp
@@ -18,6 +19,7 @@
 ALL = ("x", "y", "z", "core")
 VMEM = pl.BlockSpec(memory_space=pltpu.VMEM)
 SMEM = pl.BlockSpec(memory_space=pltpu.SMEM)
+ANY = pl.BlockSpec(memory_space=pl.ANY)
 PARAMS = pltpu.CompilerParams(vmem_limit_bytes=48 << 20)
 
 
@@ -35,12 +37,13 @@
     return out
 
 
-def slot_of(c, j):
-    return (3 * c + j // K, j % K) if j < 12 else (COLS - 1, 2 * c + j - 12)
-
-
-def group_at(c, i):
-    return jnp.where(c == 0, (i % 4) * 4 + i // 4, i)
+PARTS = {"early": ((0, 0), (3, 0), (1, 0)), "opposite": ((2, 0), (2, 2))}
+STEPS = {"early": 4, "opposite": 2}
+
+
+def group_at(place, c, shift, q):
+    line = (jnp.where(c == 0, place[3], place[2]) + shift) % 4
+    return jnp.where(c == 0, q * 4 + line, line * 4 + q)
 
 
 def prep_kernel(place, old, new, regrown, master, block, info):
@@ -104,11 +107,23 @@
             out[t, j] = block
 
 
-def product_kernel(place, rows, mine, theirs, blocks, own3, own6, send):
+def product_kernel(part, place, rows, mine, theirs, *refs):
+    layout, steps = PARTS[part], STEPS[part]
+    given, refs = refs[: len(layout)], refs[len(layout) :]
+    hidden, send, own6, stage, sem = refs[-5:]
     c = place[1]
-
-    def group(i, _):
-        f = group_at(c, i)
+    step = pl.program_id(0)
+
+    def copy_out(n, s):
+        shift, first = layout[n]
+        i = n * steps + s
+        col = group_at(place, c, shift, first + s) * COLS + 3 * c
+        to = hidden.at[:, pl.ds(pl.multiple_of(col * B, B), 3 * B)]
+        return pltpu.make_async_copy(stage.at[i], to, sem.at[i])
+
+    for n, (shift, first) in enumerate(layout):
+        i = n * steps + step
+        f = group_at(place, c, shift, first + step)
         for j in range(4):
             col = f * COLS + (3 * c + j if j < 3 else COLS - 1)
             count = K if j < 3 else 2
@@ -117,35 +132,68 @@
             left = jnp.concatenate(
                 [jnp.concatenate([ref[:, pl.ds(p, B)] for p in at], axis=1) for ref in (mine, theirs)], axis=0
             )
-            right = blocks[pl.ds(i * MINE + j * K, count)].reshape(count * B, B)
+            right = given[n][j * K : j * K + count].reshape(count * B, B)
             acc = jnp.dot(left, right, preferred_element_type=F32)
             if j < 3:
-                own3[:, pl.ds(pl.multiple_of(i * 384 + j * B, B), B)] = acc[:T].astype(BF)
+                stage[i, :, j * B : j * B + B] = acc[:T].astype(BF)
             else:
-                own6[:, pl.ds(pl.multiple_of(i * B, B), B)] = acc[:T]
+                own6[i] = acc[:T]
             send[:, pl.ds(pl.multiple_of(i * 512 + j * B, B), B)] = acc[T:].astype(BF)
-        return 0
-
-    lax.fori_loop(0, G, group, 0)
-
-
-def join_kernel(place, own3, own6, got, out):
+        copy_out(n, step).start()
+
+    @pl.when(step == steps - 1)
+    def _():
+        for n in range(len(layout)):
+            for s in range(steps):
+                copy_out(n, s).wait()
+
+
+def join_kernel(parts, last, *refs):
+    refs = list(refs)
+    place = refs.pop(0)
+    got = {part: refs.pop(0) for part in (PARTS if last else parts)}
+    own6 = {part: refs.pop(0) for part in PARTS} if last else {}
+    refs.pop(0)
+    hidden = refs.pop(0)
+    sem = refs.pop()
     c = place[1]
-    for t in range(4):
-        f = pl.program_id(0) * 4 + t
-        turned = (f % 4) * 4 + f // 4
-        i = jnp.where(c == 0, turned, f)
-        o = jnp.where(c == 0, f, turned)
-        base = t * COLS * B
-        out[:, pl.ds(pl.multiple_of(base + c * 384, B), 384)] = own3[:, pl.ds(pl.multiple_of(i * 384, B), 384)]
-        out[:, pl.ds(pl.multiple_of(base + (1 - c) * 384, B), 384)] = got[:, pl.ds(pl.multiple_of(o * 512, B), 384)]
-        last = own6[:, pl.ds(pl.multiple_of(i * B, B), B)]
-        last = last + got[:, pl.ds(pl.multiple_of(o * 512 + 384, B), B)].astype(F32)
-        out[:, base + 768 : base + 896] = last.astype(BF)
+
+    def items(part):
+        for n, (shift, first) in enumerate(PARTS[part]):
+            for s in range(STEPS[part]):
+                yield n * STEPS[part] + s, shift, first + s
+
+    copies = []
+
+    def put(source, f, col, width):
+        to = hidden.at[:, pl.ds(pl.multiple_of((f * COLS + col) * B, B), width)]
+        copies.append(pltpu.make_async_copy(source, to, sem.at[len(copies)]))
+        copies[-1].start()
+
+    for part in parts:
+        for i, shift, q in items(part):
+            put(got[part].at[:, i * 512 : i * 512 + 384], group_at(place, 1 - c, shift, q), 3 * (1 - c), 384)
+    if last:
+        total, stage = refs
+        for part in PARTS:
+            for i, shift, q in items(part):
+                total[group_at(place, c, shift, q)] = own6[part][i]
+        for part in PARTS:
+            for i, shift, q in items(part):
+                f = group_at(place, 1 - c, shift, q)
+                stage[f] = (total[f] + got[part][:, i * 512 + 384 : i * 512 + 512].astype(F32)).astype(BF)
+                put(stage.at[f], f, COLS - 1, B)
+    for copy in copies:
+        copy.wait()
 
 
 def gather(blocks, groups):
     return lax.all_to_all(blocks, ALL, 0, 0, tiled=True, axis_index_groups=groups)
+
+
+def along_ring(value, distance):
+    route = [(ring[i], ring[(i + distance) % 4]) for ring in line_groups(False) for i in range(4)]
+    return lax.ppermute(value, ALL, route)
 
 
 def to_sibling(value):
@@ -164,11 +212,47 @@
     )
 
 
+def product(part, place, rows, mine, theirs, given, hidden):
+    count = len(given) * STEPS[part]
+    whole = lambda s: pl.BlockSpec(s, lambda g: (0,) * len(s))
+    args = [place, rows, mine, theirs, *given] + ([] if hidden is None else [hidden])
+    return call(
+        functools.partial(product_kernel, part),
+        [((T, G * COLS * B), BF), ((T, count * 512), BF), ((count, T, B), F32)],
+        [SMEM, SMEM, whole(mine.shape), whole(theirs.shape)]
+        + [pl.BlockSpec((MINE, B, B), lambda g: (g, 0, 0))] * len(given)
+        + ([] if hidden is None else [ANY]),
+        [ANY, whole((T, count * 512)), whole((count, T, B))],
+        "product_" + part,
+        grid=(STEPS[part],),
+        cost_estimate=pl.CostEstimate(
+            flops=count * MINE * 2 * B * B * 2 * T, bytes_accessed=count * (MINE * B * B * 2 + T * B * 20), transcendentals=0
+        ),
+        scratch_shapes=[pltpu.VMEM((count, T, 384), BF), pltpu.SemaphoreType.DMA((count,))],
+        input_output_aliases={} if hidden is None else {len(args) - 1: 0},
+    )(*args)
+
+
+def join(parts, place, got, own6, hidden):
+    args = [place, *got, *own6, hidden]
+    count = sum(len(PARTS[p]) * STEPS[p] for p in parts) + (G if own6 else 0)
+    stage = [pltpu.VMEM((G, T, B), F32), pltpu.VMEM((G, T, B), BF)] if own6 else []
+    return call(
+        functools.partial(join_kernel, parts, bool(own6)),
+        [(hidden.shape, BF)],
+        [SMEM] + [VMEM] * (len(args) - 2) + [ANY],
+        [ANY],
+        "join_" + parts[-1],
+        scratch_shapes=stage + [pltpu.SemaphoreType.DMA((count,))],
+        input_output_aliases={len(args) - 1: 0},
+    )(*args)[0]
+
+
 def on_device(tokens, master, moment, second, old_cell, new_cell, regrown, new_rows):
     c = lax.axis_index("core")
     cell = lax.axis_index("z") * C + c
-    place = jnp.stack([cell, c]).astype(jnp.int32)
-    theirs = to_sibling(tokens)
+    place = jnp.stack([cell, c, lax.axis_index("x"), lax.axis_index("y")]).astype(jnp.int32)
+    rows = new_rows.T
     old_cell, new_cell, regrown = old_cell.T, new_cell.T, regrown.T
     block, info = call(
         prep_kernel, [((1, B, B), BF), ((8,), jnp.int32)], [SMEM] * 4 + [VMEM], [VMEM, SMEM], "prep"
@@ -179,7 +263,9 @@
         place, old_cell, own, other
     )
     line = gather(picked, line_groups(True)).reshape(4 * MINE, B, B)
-    line, master, moment, second = lax.optimization_barrier((line, master, moment, second))
+    line, master, moment, second, tokens = lax.optimization_barrier((line, master, moment, second, tokens))
+    lower, upper = along_ring(line, 1), along_ring(line, -1)
+    theirs = to_sibling(tokens)
     load = jnp.concatenate([master, moment, second]).astype(BF)
     low = along_cells(load, 3)
     high = along_cells(load, -3)
@@ -188,28 +274,20 @@
     )
     below = along_cells(up, 1)
     above = along_cells(down, -1)
-    wide = jnp.broadcast_to(line[None], (4, 4 * MINE, B, B))
-    blocks = gather(wide, line_groups(False)).reshape(G * MINE, B, B)
+    lower, upper, below, above = lax.optimization_barrier((lower, upper, below, above))
     states = call(settle_kernel, [((1, B, B), F32)] * 3, [SMEM] + [VMEM] * 7, [VMEM] * 3, "settle")(
         info, master, moment, second, low, high, below, above
     )
-    tokens, theirs, states = lax.optimization_barrier((tokens, theirs, tuple(states)))
-    own3, own6, send = call(
-        product_kernel,
-        [((T, G * 384), BF), ((T, G * B), F32), ((T, G * 512), BF)],
-        [SMEM, SMEM, VMEM, VMEM, VMEM],
-        [VMEM] * 3,
-        "product",
-    )(place, new_rows.T, tokens, theirs, blocks)
-    got = to_sibling(send)
-    (hidden,) = call(
-        join_kernel,
-        [((T, G * COLS * B), BF)],
-        [SMEM, VMEM, VMEM, VMEM],
-        [pl.BlockSpec((T, 4 * COLS * B), lambda g: (0, g))],
-        "join",
-        grid=(4,),
-    )(place, own3, own6, got)
+    half = 2 * MINE
+    go_up, go_down, tokens = lax.optimization_barrier((lower[:half], upper[half:], tokens))
+    over = [along_ring(go_up, 1), along_ring(go_down, -1)]
+    hidden, send, own6_early = product("early", place, rows, tokens, theirs, [line, lower, upper], None)
+    send, over = lax.optimization_barrier((send, over))
+    got_early = to_sibling(send)
+    hidden, send, own6_opposite = product("opposite", place, rows, tokens, theirs, over, hidden)
+    got_opposite = to_sibling(send)
+    hidden = join(("early",), place, (got_early,), (), hidden)
+    hidden = join(("opposite",), place, (got_early, got_opposite), (own6_early, own6_opposite), hidden)
     return (hidden, *states)
 
 

time: 145 us -> 130 us (0.90)
  waiting for transfers between devices: 35.5 us -> 15.5 us
  starting transfers between devices: 31.6 us -> 43.4 us
  local copies, waits for them, and re-layouts: 7.78 us -> 3.07 us
  Pallas kernels: 18.3 us -> 16.4 us
    all_to_all x1 -> x0, waiting for transfers between devices: 22.2 us -> none  [gather(): lax.all_to_all(blocks, ALL, 0, 0, tiled=True, axis_index_groups=groups)]
    ppermute x0 -> x4, starting transfers between devices: none -> 12.5 us  [along_ring(): return lax.ppermute(value, ALL, route)]
    ppermute x0 -> x4, waiting for transfers between devices: none -> 6.43 us  [along_ring(): return lax.ppermute(value, ALL, route)]
    all_to_all x1 -> x0, starting transfers between devices: 5.6 us -> none  [gather(): lax.all_to_all(blocks, ALL, 0, 0, tiled=True, axis_index_groups=groups)]
    broadcast_in_dim x1 -> x0, local copies, waits for them, and re-layouts: 4.88 us -> none  [on_device(): wide = jnp.broadcast_to(line[None], (4, 4 * MINE, B, B))]
    ppermute x3 -> x4, starting transfers between devices: 17.4 us -> 22.2 us  [to_sibling(): return lax.ppermute(value, 'core', [(0, 1), (1, 0)])]
    ppermute x3 -> x4, waiting for transfers between devices: 5.49 us -> 1.52 us  [to_sibling(): return lax.ppermute(value, 'core', [(0, 1), (1, 0)])]
    pallas_call x2 -> x4, Pallas kernels: 14.1 us -> 12.2 us  [the longest x2 8.93 us: product(): call(functools.partial(product_kernel, part), [((T, G * COLS * B), BF), (...]
  transfers between devices with their start and end apart: 8 -> 12, of which waited for: 7 -> 8; matrix products, arithmetic and copies ran while one was open for 0% -> 0% of each run, Pallas kernels for 1% -> 10%
where the time goes in v2:
time: 130 us
  blocking collectives  50.2 us (39%)
  starting transfers between devices  43.4 us (33%)
  Pallas kernels  16.4 us (13%)
  waiting for transfers between devices  15.5 us (12%)
  local copies, waits for them, and re-layouts  3.07 us (2%)
    all_gather x1, blocking collectives, on_device(): own = lax.all_gather(block, 'z', axis=0, tiled=True)  31.8 us
    ppermute x4, starting transfers between devices, to_sibling(): return lax.ppermute(value, 'core', [(0, 1), (1, 0)])  22.2 us
    all_to_all x1, blocking collectives, gather(): lax.all_to_all(blocks, ALL, 0, 0, tiled=True, axis_index_groups=groups)  18.4 us
    ppermute x4, starting transfers between devices, along_ring(): return lax.ppermute(value, ALL, route)  12.5 us
    pallas_call x2, Pallas kernels, product(): call(functools.partial(product_kernel, part), [((T, G * COLS * B), BF), (...  8.93 us
    ppermute x4, starting transfers between devices, along_cells(): return lax.ppermute(value, ('z', 'core'), route)  8.68 us
    ppermute x4, waiting for transfers between devices, along_cells(): return lax.ppermute(value, ('z', 'core'), route)  7.57 us
    ppermute x4, waiting for transfers between devices, along_ring(): return lax.ppermute(value, ALL, route)  6.43 us
  transfers between devices with their start and end apart: 12, of which 8 were waited for; matrix products, arithmetic and copies ran while one was open for 0% of the time, Pallas kernels for 10%

profile of v2, /device:TPU:1, one launch (start us, length us, event | category | flops | bytes accessed | tf_op | source)
XLA Modules:
  0.0 129.5 jit_solution(15629653018127286642)
XLA Ops:
  3.6 1.4 %prep.1 = (bf16[1,128,128]{2,1,0:T(8,128)(2,1)S(1)}, s32[8]{0:T(128)S(1)}) custom-call(s32[4]{0:T(128)S(1)} %pad_add_fusion.place.refs_0_, s32[4,7]{1,0:T(4,128)S(1)} %bitcast.11, s32[4,7]{1,0:T(4,128)S(1)} %bitcast.13, s32[4,7]{1,0:T(4,128)S(1)} %bitcast.14, f32[1,128,128]{2,1,0:T(8,128)S(1)} %copy-done.1), custom_call_target="tpu_custom_call" | custom-call | tf_op jit(solution)/shard_map/prep/pallas_call | solution.py:257
  5.0 31.8 %all_gather.3.own = bf16[16,128,128]{2,1,0:T(8,128)(2,1)S(1)} all-gather(bf16[1,128,128]{2,1,0:T(8,128)(2,1)S(1)} %get-tuple-element.32), channel_id=1, replica_groups=mesh['x'=4,'y'=4,'z'=16,'core'=2] {'z'}, dimensions={0}, use_global_device_ids=true | all-gather | bytes 557056 | tf_op jit(solution)/shard_map/all_gather | solution.py:260
  36.8 10.1 %collective-permute-start = (bf16[16,128,128]{2,1,0:T(8,128)(2,1)S(1)}, bf16[16,128,128]{2,1,0:T(8,128)(2,1)S(1)}, u32[]{:S(2)}, u32[]{:S(2)}) collective-permute-start(bf16[16,128,128]{2,1,0:T(8,128)(2,1)S(1)} %all_gather.3.own), channel_id=1, source_target_pairs={{0,1},{1,0},{2,3},{3,2},{4,5},{5,4},{6,7},{7,6},{8,9},{9,8},{10,11... | collective-permute-start | bytes 1572872 | tf_op jit(solution)/shard_map/ppermute | solution.py:200
  47.0 1.5 %collective-permute-done.other = bf16[16,128,128]{2,1,0:T(8,128)(2,1)S(1)} collective-permute-done((bf16[16,128,128]{2,1,0:T(8,128)(2,1)S(1)}, bf16[16,128,128]{2,1,0:T(8,128)(2,1)S(1)}, u32[]{:S(2)}, u32[]{:S(2)}) %collective-permute-start) | collective-permute-done | bytes 524320 | tf_op jit(solution)/shard_map/ppermute | solution.py:200
  49.4 18.4 %all_to_all.5 = bf16[4,14,128,128]{3,2,1,0:T(8,128)(2,1)S(1)} all-to-all(bf16[4,14,128,128]{3,2,1,0:T(8,128)(2,1)S(1)} %pick.1), channel_id=1, replica_groups={{0,128,256,384},{32,160,288,416},{64,192,320,448},{96,224,352,480},{2,1..., dimensions={0} | all-to-all | bytes 3670016 | tf_op jit(solution)/shard_map/all_to_all | solution.py:191
  67.7 4.1 %collective-permute-start.2 = (bf16[56,128,128]{2,1,0:T(8,128)(2,1)S(1)}, bf16[56,128,128]{2,1,0:T(8,128)(2,1)S(1)}, u32[]{:S(2)}, u32[]{:S(2)}) collective-permute-start(bf16[56,128,128]{2,1,0:T(8,128)(2,1)S(1)} %bitcast.15), channel_id=1, source_target_pairs={{0,96},{32,0},{64,32},{96,64},{128,224},{160,128},{192,160},{224,1... | collective-permute-start | bytes 5505032 | tf_op jit(solution)/shard_map/ppermute | solution.py:196
  71.8 1.9 %collective-permute-start.1 = (bf16[56,128,128]{2,1,0:T(8,128)(2,1)S(1)}, bf16[56,128,128]{2,1,0:T(8,128)(2,1)S(1)}, u32[]{:S(2)}, u32[]{:S(2)}) collective-permute-start(bf16[56,128,128]{2,1,0:T(8,128)(2,1)S(1)} %bitcast.16), channel_id=1, source_target_pairs={{0,32},{32,64},{64,96},{96,0},{128,160},{160,192},{192,224},{224,1... | collective-permute-start | bytes 5505032 | tf_op jit(solution)/shard_map/ppermute | solution.py:196
  73.8 4.1 %collective-permute-start.7 = (bf16[128,4096]{1,0:T(8,128)(2,1)S(1)}, bf16[128,4096]{1,0:T(8,128)(2,1)S(1)}, u32[]{:S(2)}, u32[]{:S(2)}) collective-permute-start(bf16[128,4096]{1,0:T(8,128)(2,1)S(1)} %copy-done), channel_id=1, source_target_pairs={{0,1},{1,0},{2,3},{3,2},{4,5},{5,4},{6,7},{7,6},{8,9},{9,8},{10,11... | collective-permute-start | bytes 3145736 | tf_op jit(solution)/shard_map/ppermute | solution.py:200
  77.9 1.9 %collective-permute-start.4 = (bf16[3,128,128]{2,1,0:T(8,128)(2,1)S(1)}, bf16[3,128,128]{2,1,0:T(8,128)(2,1)S(1)}, u32[]{:S(2)}, u32[]{:S(2)}) collective-permute-start(bf16[3,128,128]{2,1,0:T(8,128)(2,1)S(1)} %pad_maximum_fusion.own), channel_id=1, source_target_pairs={{0,29},{1,30},{2,31},{3,0},{4,1},{5,2},{6,3},{7,4},{8,5},{9,6},{10... | collective-permute-start | bytes 294920 | tf_op jit(solution)/shard_map/ppermute | solution.py:205
  79.9 4.5 %collective-permute-start.3 = (bf16[3,128,128]{2,1,0:T(8,128)(2,1)S(1)}, bf16[3,128,128]{2,1,0:T(8,128)(2,1)S(1)}, u32[]{:S(2)}, u32[]{:S(2)}) collective-permute-start(bf16[3,128,128]{2,1,0:T(8,128)(2,1)S(1)} %pad_maximum_fusion.own), channel_id=1, source_target_pairs={{0,3},{1,4},{2,5},{3,6},{4,7},{5,8},{6,9},{7,10},{8,11},{9,12},{10... | collective-permute-start | bytes 294920 | tf_op jit(solution)/shard_map/ppermute | solution.py:205
  85.3 3.0 %collective-permute-done.3.low = bf16[3,128,128]{2,1,0:T(8,128)(2,1)S(1)} collective-permute-done((bf16[3,128,128]{2,1,0:T(8,128)(2,1)S(1)}, bf16[3,128,128]{2,1,0:T(8,128)(2,1)S(1)}, u32[]{:S(2)}, u32[]{:S(2)}) %collective-permute-start.3) | collective-permute-done | bytes 98336 | tf_op jit(solution)/shard_map/ppermute | solution.py:205
  89.0 1.5 %collective-permute-start.5 = (bf16[3,128,128]{2,1,0:T(8,128)(2,1)S(1)}, bf16[3,128,128]{2,1,0:T(8,128)(2,1)S(1)}, u32[]{:S(2)}, u32[]{:S(2)}) collective-permute-start(bf16[3,128,128]{2,1,0:T(8,128)(2,1)S(1)} %get-tuple-element.38), channel_id=1, source_target_pairs={{0,1},{1,2},{2,3},{3,4},{4,5},{5,6},{6,7},{7,8},{8,9},{9,10},{10,1... | collective-permute-start | bytes 294920 | tf_op jit(solution)/shard_map/ppermute | solution.py:205
  92.1 2.7 %collective-permute-done.6.above = bf16[3,128,128]{2,1,0:T(8,128)(2,1)S(1)} collective-permute-done((bf16[3,128,128]{2,1,0:T(8,128)(2,1)S(1)}, bf16[3,128,128]{2,1,0:T(8,128)(2,1)S(1)}, u32[]{:S(2)}, u32[]{:S(2)}) %collective-permute-start.6) | collective-permute-done | bytes 98336 | tf_op jit(solution)/shard_map/ppermute | solution.py:205
  94.8 2.5 %collective-permute-done.1.refs_1_ = bf16[56,128,128]{2,1,0:T(8,128)(2,1)S(1)} collective-permute-done((bf16[56,128,128]{2,1,0:T(8,128)(2,1)S(1)}, bf16[56,128,128]{2,1,0:T(8,128)(2,1)S(1)}, u32[]{:S(2)}, u32[]{:S(2)}) %collective-permute-start.1) | collective-permute-done | bytes 1835040 | tf_op jit(solution)/shard_map/ppermute | solution.py:196
  97.5 1.9 %collective-permute-start.8 = (bf16[28,128,128]{2,1,0:T(8,128)(2,1)S(1)}, bf16[28,128,128]{2,1,0:T(8,128)(2,1)S(1)}, u32[]{:S(2)}, u32[]{:S(2)}) collective-permute-start(bf16[28,128,128]{2,1,0:T(8,128)(2,1)S(1)} %slice.6), channel_id=1, source_target_pairs={{0,32},{32,64},{64,96},{96,0},{128,160},{160,192},{192,224},{224,1... | collective-permute-start | bytes 2752520 | tf_op jit(solution)/shard_map/ppermute | solution.py:196
  99.4 4.6 %collective-permute-start.9 = (bf16[28,128,128]{2,1,0:T(8,128)(2,1)S(1)}, bf16[28,128,128]{2,1,0:T(8,128)(2,1)S(1)}, u32[]{:S(2)}, u32[]{:S(2)}) collective-permute-start(bf16[28,128,128]{2,1,0:T(8,128)(2,1)S(1)} %slice.7), channel_id=1, source_target_pairs={{0,96},{32,0},{64,32},{96,64},{128,224},{160,128},{192,160},{224,1... | collective-permute-start | bytes 2752520 | tf_op jit(solution)/shard_map/ppermute | solution.py:196
  104.0 6.3 %product_early.1 = (bf16[128,14336]{1,0:T(8,128)(2,1)}, bf16[128,6144]{1,0:T(8,128)(2,1)S(1)}, f32[12,128,128]{2,1,0:T(8,128)S(1)}) custom-call(s32[4]{0:T(128)S(1)} %pad_add_fusion.place.refs_0_, s32[4,112]{1,0:T(4,128)S(1)} %bitcast.9, bf16[128,4096]{1,0:T(8,128)(2,1)S(1)} %copy-done, bf16[128,4096]{1,0:T(8,128)(2,1)S(1)} %collective-permute-done.7.theirs, ...), custom_call_target="tpu_custom_call" | custom-call | flops 1409286144 | bytes 9437184 | tf_op jit(solution)/shard_map/product_early/pallas_call | solution.py:219
  110.4 2.8 %collective-permute-done.8.refs_0_ = bf16[28,128,128]{2,1,0:T(8,128)(2,1)S(1)} collective-permute-done((bf16[28,128,128]{2,1,0:T(8,128)(2,1)S(1)}, bf16[28,128,128]{2,1,0:T(8,128)(2,1)S(1)}, u32[]{:S(2)}, u32[]{:S(2)}) %collective-permute-start.8) | collective-permute-done | bytes 917536 | tf_op jit(solution)/shard_map/ppermute | solution.py:196
  114.3 6.1 %collective-permute-start.10 = (bf16[128,6144]{1,0:T(8,128)(2,1)S(1)}, bf16[128,6144]{1,0:T(8,128)(2,1)S(1)}, u32[]{:S(2)}, u32[]{:S(2)}) collective-permute-start(bf16[128,6144]{1,0:T(8,128)(2,1)S(1)} %get-tuple-element.47), channel_id=1, source_target_pairs={{0,1},{1,0},{2,3},{3,2},{4,5},{5,4},{6,7},{7,6},{8,9},{9,8},{10,11... | collective-permute-start | bytes 4718600 | tf_op jit(solution)/shard_map/ppermute | solution.py:200
  120.4 2.6 %product_opposite.1 = (bf16[128,14336]{1,0:T(8,128)(2,1)}, bf16[128,2048]{1,0:T(8,128)(2,1)S(1)}, f32[4,128,128]{2,1,0:T(8,128)S(1)}) custom-call(s32[4]{0:T(128)S(1)} %pad_add_fusion.place.refs_0_, s32[4,112]{1,0:T(4,128)S(1)} %bitcast.10, bf16[128,4096]{1,0:T(8,128)(2,1)S(1)} %copy-done, ...), custom_call_target="tpu_custom_call", output_to_operand_aliasing={{0}: (6, {})} | custom-call | flops 469762048 | bytes 3145728 | tf_op jit(solution)/shard_map/product_opposite/pallas_call | solution.py:219
  123.0 1.9 %collective-permute-start.11 = (bf16[128,2048]{1,0:T(8,128)(2,1)S(1)}, bf16[128,2048]{1,0:T(8,128)(2,1)S(1)}, u32[]{:S(2)}, u32[]{:S(2)}) collective-permute-start(bf16[128,2048]{1,0:T(8,128)(2,1)S(1)} %get-tuple-element.51), channel_id=1, source_target_pairs={{0,1},{1,0},{2,3},{3,2},{4,5},{5,4},{6,7},{7,6},{8,9},{9,8},{10,11... | collective-permute-start | bytes 1572872 | tf_op jit(solution)/shard_map/ppermute | solution.py:200
  124.9 1.3 settle.1
  126.2 1.7 %join_early.1.refs_5_ = bf16[128,14336]{1,0:T(8,128)(2,1)} custom-call(s32[4]{0:T(128)S(1)} %pad_add_fusion.place.refs_0_, bf16[128,6144]{1,0:T(8,128)(2,1)S(1)} %collective-permute-done.10.refs_1_, bf16[128,14336]{1,0:T(8,128)(2,1)} %get-tuple-element.54.refs_2_), custom_call_target="tpu_custom_call", output_to_operand_aliasing={{}: (2, {})} | custom-call | tf_op jit(solution)/shard_map/join_early/pallas_call | solution.py:240
  127.9 1.6 %join_opposite.1 = bf16[128,14336]{1,0:T(8,128)(2,1)} custom-call(s32[4]{0:T(128)S(1)} %pad_add_fusion.place.refs_0_, bf16[128,6144]{1,0:T(8,128)(2,1)S(1)} %collective-permute-done.10.refs_1_, bf16[128,2048]{1,0:T(8,128)(2,1)S(1)} %collective-permute-done.11.refs_2_, f32[12,128,128]{2,1,0:T(8,128)S(1)} %get-tuple-element.52.refs_3_, ...), custom_call_target="tpu_custom_call", output_to_operand_aliasing={{}: (5, {})} | custom-call | tf_op jit(solution)/shard_map/join_opposite/pallas_call | solution.py:240
  (41 shorter events, 8.4 us)
Async XLA Ops:
  0.7 0.8 copy-start.1
  1.6 0.7 copy-start.6
  2.2 0.7 copy-start.7
  2.9 0.7 copy-start.8
  36.8 11.7 %collective-permute-start = (bf16[16,128,128]{2,1,0:T(8,128)(2,1)S(1)}, bf16[16,128,128]{2,1,0:T(8,128)(2,1)S(1)}, u32[]{:S(2)}, u32[]{:S(2)}) collective-permute-start(bf16[16,128,128]{2,1,0:T(8,128)(2,1)S(1)} %all_gather.3.own), channel_id=1, source_target_pairs={{0,1},{1,0},{2,3},{3,2},{4,5},{5,4},{6,7},{7,6},{8,9},{9,8},{10,11... | collective-permute-start | bytes 1572872 | tf_op jit(solution)/shard_map/ppermute | solution.py:200
  49.3 24.4 %copy-start.3 = (f32[1,128,128]{2,1,0:T(8,128)S(1)}, f32[1,128,128]{2,1,0:T(8,128)}, u32[]{:S(2)}) copy-start(f32[1,128,128]{2,1,0:T(8,128)} %moment) | copy-start | bytes 196612
  49.3 24.5 %copy-start.4 = (f32[1,128,128]{2,1,0:T(8,128)S(1)}, f32[1,128,128]{2,1,0:T(8,128)}, u32[]{:S(2)}) copy-start(f32[1,128,128]{2,1,0:T(8,128)} %second) | copy-start | bytes 196612
  49.4 24.5 %copy-start = (bf16[128,4096]{1,0:T(8,128)(2,1)S(1)}, bf16[128,4096]{1,0:T(8,128)(2,1)}, u32[]{:S(2)}) copy-start(bf16[128,4096]{1,0:T(8,128)(2,1)} %mine.1) | copy-start | bytes 3145732
  67.7 29.7 %copy-start.9 = (bf16[4,14,128,128]{3,2,1,0:T(8,128)(2,1)}, bf16[4,14,128,128]{3,2,1,0:T(8,128)(2,1)S(1)}, u32[]{:S(2)}) copy-start(bf16[4,14,128,128]{3,2,1,0:T(8,128)(2,1)S(1)} %all_to_all.5) | copy-start | bytes 5505028
  67.7 27.1 %collective-permute-start.2 = (bf16[56,128,128]{2,1,0:T(8,128)(2,1)S(1)}, bf16[56,128,128]{2,1,0:T(8,128)(2,1)S(1)}, u32[]{:S(2)}, u32[]{:S(2)}) collective-permute-start(bf16[56,128,128]{2,1,0:T(8,128)(2,1)S(1)} %bitcast.15), channel_id=1, source_target_pairs={{0,96},{32,0},{64,32},{96,64},{128,224},{160,128},{192,160},{224,1... | collective-permute-start | bytes 5505032 | tf_op jit(solution)/shard_map/ppermute | solution.py:196
  71.8 25.5 %collective-permute-start.1 = (bf16[56,128,128]{2,1,0:T(8,128)(2,1)S(1)}, bf16[56,128,128]{2,1,0:T(8,128)(2,1)S(1)}, u32[]{:S(2)}, u32[]{:S(2)}) collective-permute-start(bf16[56,128,128]{2,1,0:T(8,128)(2,1)S(1)} %bitcast.16), channel_id=1, source_target_pairs={{0,32},{32,64},{64,96},{96,0},{128,160},{160,192},{192,224},{224,1... | collective-permute-start | bytes 5505032 | tf_op jit(solution)/shard_map/ppermute | solution.py:196
  73.8 30.2 %collective-permute-start.7 = (bf16[128,4096]{1,0:T(8,128)(2,1)S(1)}, bf16[128,4096]{1,0:T(8,128)(2,1)S(1)}, u32[]{:S(2)}, u32[]{:S(2)}) collective-permute-start(bf16[128,4096]{1,0:T(8,128)(2,1)S(1)} %copy-done), channel_id=1, source_target_pairs={{0,1},{1,0},{2,3},{3,2},{4,5},{5,4},{6,7},{7,6},{8,9},{9,8},{10,11... | collective-permute-start | bytes 3145736 | tf_op jit(solution)/shard_map/ppermute | solution.py:200
  77.9 7.4 %collective-permute-start.4 = (bf16[3,128,128]{2,1,0:T(8,128)(2,1)S(1)}, bf16[3,128,128]{2,1,0:T(8,128)(2,1)S(1)}, u32[]{:S(2)}, u32[]{:S(2)}) collective-permute-start(bf16[3,128,128]{2,1,0:T(8,128)(2,1)S(1)} %pad_maximum_fusion.own), channel_id=1, source_target_pairs={{0,29},{1,30},{2,31},{3,0},{4,1},{5,2},{6,3},{7,4},{8,5},{9,6},{10... | collective-permute-start | bytes 294920 | tf_op jit(solution)/shard_map/ppermute | solution.py:205
  79.9 8.5 %collective-permute-start.3 = (bf16[3,128,128]{2,1,0:T(8,128)(2,1)S(1)}, bf16[3,128,128]{2,1,0:T(8,128)(2,1)S(1)}, u32[]{:S(2)}, u32[]{:S(2)}) collective-permute-start(bf16[3,128,128]{2,1,0:T(8,128)(2,1)S(1)} %pad_maximum_fusion.own), channel_id=1, source_target_pairs={{0,3},{1,4},{2,5},{3,6},{4,7},{5,8},{6,9},{7,10},{8,11},{9,12},{10... | collective-permute-start | bytes 294920 | tf_op jit(solution)/shard_map/ppermute | solution.py:205
  89.0 3.1 %collective-permute-start.5 = (bf16[3,128,128]{2,1,0:T(8,128)(2,1)S(1)}, bf16[3,128,128]{2,1,0:T(8,128)(2,1)S(1)}, u32[]{:S(2)}, u32[]{:S(2)}) collective-permute-start(bf16[3,128,128]{2,1,0:T(8,128)(2,1)S(1)} %get-tuple-element.38), channel_id=1, source_target_pairs={{0,1},{1,2},{2,3},{3,4},{4,5},{5,6},{6,7},{7,8},{8,9},{9,10},{10,1... | collective-permute-start | bytes 294920 | tf_op jit(solution)/shard_map/ppermute | solution.py:205
  90.5 13.5 %copy-start.5 = (s32[112,4]{0,1:T(4,128)S(1)}, s32[112,4]{0,1:T(4,128)}, u32[]{:S(2)}) copy-start(s32[112,4]{0,1:T(4,128)} %param.15) | copy-start | bytes 5380
  90.5 4.3 %collective-permute-start.6 = (bf16[3,128,128]{2,1,0:T(8,128)(2,1)S(1)}, bf16[3,128,128]{2,1,0:T(8,128)(2,1)S(1)}, u32[]{:S(2)}, u32[]{:S(2)}) collective-permute-start(bf16[3,128,128]{2,1,0:T(8,128)(2,1)S(1)} %get-tuple-element.39), channel_id=1, source_target_pairs={{0,31},{1,0},{2,1},{3,2},{4,3},{5,4},{6,5},{7,6},{8,7},{9,8},{10,9... | collective-permute-start | bytes 294920 | tf_op jit(solution)/shard_map/ppermute | solution.py:205
  94.8 2.7 %copy-start.10 = (bf16[56,128,128]{2,1,0:T(8,128)(2,1)}, bf16[56,128,128]{2,1,0:T(8,128)(2,1)S(1)}, u32[]{:S(2)}) copy-start(bf16[56,128,128]{2,1,0:T(8,128)(2,1)S(1)} %collective-permute-done.2.refs_2_) | copy-start | bytes 5505028
  97.3 6.7 %copy-start.11 = (bf16[56,128,128]{2,1,0:T(8,128)(2,1)}, bf16[56,128,128]{2,1,0:T(8,128)(2,1)S(1)}, u32[]{:S(2)}) copy-start(bf16[56,128,128]{2,1,0:T(8,128)(2,1)S(1)} %collective-permute-done.1.refs_1_) | copy-start | bytes 5505028
  97.5 15.6 %collective-permute-start.8 = (bf16[28,128,128]{2,1,0:T(8,128)(2,1)S(1)}, bf16[28,128,128]{2,1,0:T(8,128)(2,1)S(1)}, u32[]{:S(2)}, u32[]{:S(2)}) collective-permute-start(bf16[28,128,128]{2,1,0:T(8,128)(2,1)S(1)} %slice.6), channel_id=1, source_target_pairs={{0,32},{32,64},{64,96},{96,0},{128,160},{160,192},{192,224},{224,1... | collective-permute-start | bytes 2752520 | tf_op jit(solution)/shard_map/ppermute | solution.py:196
  99.4 14.9 %collective-permute-start.9 = (bf16[28,128,128]{2,1,0:T(8,128)(2,1)S(1)}, bf16[28,128,128]{2,1,0:T(8,128)(2,1)S(1)}, u32[]{:S(2)}, u32[]{:S(2)}) collective-permute-start(bf16[28,128,128]{2,1,0:T(8,128)(2,1)S(1)} %slice.7), channel_id=1, source_target_pairs={{0,96},{32,0},{64,32},{96,64},{128,224},{160,128},{192,160},{224,1... | collective-permute-start | bytes 2752520 | tf_op jit(solution)/shard_map/ppermute | solution.py:196
  114.3 11.9 %collective-permute-start.10 = (bf16[128,6144]{1,0:T(8,128)(2,1)S(1)}, bf16[128,6144]{1,0:T(8,128)(2,1)S(1)}, u32[]{:S(2)}, u32[]{:S(2)}) collective-permute-start(bf16[128,6144]{1,0:T(8,128)(2,1)S(1)} %get-tuple-element.47), channel_id=1, source_target_pairs={{0,1},{1,0},{2,3},{3,2},{4,5},{5,4},{6,7},{7,6},{8,9},{9,8},{10,11... | collective-permute-start | bytes 4718600 | tf_op jit(solution)/shard_map/ppermute | solution.py:200
  120.4 4.6 %copy-start.2 = (f32[1,128,128]{2,1,0:T(8,128)S(1)}, f32[1,128,128]{2,1,0:T(8,128)}, u32[]{:S(2)}) copy-start(f32[1,128,128]{2,1,0:T(8,128)} %master.2) | copy-start | bytes 196612
  123.0 4.9 %collective-permute-start.11 = (bf16[128,2048]{1,0:T(8,128)(2,1)S(1)}, bf16[128,2048]{1,0:T(8,128)(2,1)S(1)}, u32[]{:S(2)}, u32[]{:S(2)}) collective-permute-start(bf16[128,2048]{1,0:T(8,128)(2,1)S(1)} %get-tuple-element.51), channel_id=1, source_target_pairs={{0,1},{1,0},{2,3},{3,2},{4,5},{5,4},{6,7},{7,6},{8,9},{9,8},{10,11... | collective-permute-start | bytes 1572872 | tf_op jit(solution)/shard_map/ppermute | solution.py:200

commit v3 on v2

--- a/solution.py
+++ b/solution.py
@@ -37,8 +37,11 @@
     return out
 
 
-PARTS = {"early": ((0, 0), (3, 0), (1, 0)), "opposite": ((2, 0), (2, 2))}
-STEPS = {"early": 4, "opposite": 2}
+PARTS = {
+    "early": ((0, 0), (0, 2), (3, 0), (3, 2), (1, 0), (1, 2)),
+    "opposite": ((2, 0), (2, 2)),
+}
+STEPS = {"early": 2, "opposite": 2}
 
 
 def group_at(place, c, shift, q):
@@ -262,9 +265,8 @@
     (picked,) = call(pick_kernel, [((4, MINE, B, B), BF)], [SMEM, SMEM, VMEM, VMEM], [VMEM], "pick")(
         place, old_cell, own, other
     )
+    picked, master, moment, second, tokens = lax.optimization_barrier((picked, master, moment, second, tokens))
     line = gather(picked, line_groups(True)).reshape(4 * MINE, B, B)
-    line, master, moment, second, tokens = lax.optimization_barrier((line, master, moment, second, tokens))
-    lower, upper = along_ring(line, 1), along_ring(line, -1)
     theirs = to_sibling(tokens)
     load = jnp.concatenate([master, moment, second]).astype(BF)
     low = along_cells(load, 3)
@@ -272,18 +274,22 @@
     up, down = call(middle_kernel, [((3, B, B), BF)] * 2, [SMEM] + [VMEM] * 3, [VMEM] * 2, "middle")(
         info, load, low, high
     )
+    line, up, down, theirs = lax.optimization_barrier((line, up, down, theirs))
+    halves = [line[: 2 * MINE], line[2 * MINE :]]
+    lower, upper = [along_ring(halves[0], 1)], [along_ring(halves[1], -1)]
+    lower.append(along_ring(halves[1], 1))
+    upper.insert(0, along_ring(halves[0], -1))
     below = along_cells(up, 1)
     above = along_cells(down, -1)
-    lower, upper, below, above = lax.optimization_barrier((lower, upper, below, above))
+    over = [along_ring(lower[0], 1), along_ring(upper[1], -1)]
+    tokens, below, above = lax.optimization_barrier((tokens, below, above))
+    hidden, send, own6_early = product("early", place, rows, tokens, theirs, [*halves, *lower, *upper], None)
+    send, over = lax.optimization_barrier((send, over))
+    got_early = to_sibling(send)
     states = call(settle_kernel, [((1, B, B), F32)] * 3, [SMEM] + [VMEM] * 7, [VMEM] * 3, "settle")(
         info, master, moment, second, low, high, below, above
     )
-    half = 2 * MINE
-    go_up, go_down, tokens = lax.optimization_barrier((lower[:half], upper[half:], tokens))
-    over = [along_ring(go_up, 1), along_ring(go_down, -1)]
-    hidden, send, own6_early = product("early", place, rows, tokens, theirs, [line, lower, upper], None)
-    send, over = lax.optimization_barrier((send, over))
-    got_early = to_sibling(send)
+    over, states = lax.optimization_barrier((over, tuple(states)))
     hidden, send, own6_opposite = product("opposite", place, rows, tokens, theirs, over, hidden)
     got_opposite = to_sibling(send)
     hidden = join(("early",), place, (got_early,), (), hidden)

time: 130 us -> 123 us (0.946)
  blocking collectives: 50.2 us -> 31.8 us
  starting transfers between devices: 43.4 us -> 54.6 us
  waiting for transfers between devices: 15.5 us -> 11.5 us
  Pallas kernels: 16.4 us -> 18.5 us
  local copies, waits for them, and re-layouts: 3.07 us -> 4.51 us
    all_to_all x1 -> x0, blocking collectives: 18.4 us -> none  [gather(): lax.all_to_all(blocks, ALL, 0, 0, tiled=True, axis_index_groups=groups)]
    ppermute x4 -> x6, starting transfers between devices: 12.5 us -> 19.5 us  [along_ring(): return lax.ppermute(value, ALL, route)]
    ppermute x4, starting transfers between devices: 22.2 us -> 17.6 us  [to_sibling(): return lax.ppermute(value, 'core', [(0, 1), (1, 0)])]
    all_to_all x0 -> x1, starting transfers between devices: none -> 4.57 us  [gather(): lax.all_to_all(blocks, ALL, 0, 0, tiled=True, axis_index_groups=groups)]
    ppermute x4, starting transfers between devices: 8.68 us -> 13 us  [along_cells(): return lax.ppermute(value, ('z', 'core'), route)]
    ppermute x4 -> x6, waiting for transfers between devices: 6.43 us -> 2.64 us  [along_ring(): return lax.ppermute(value, ALL, route)]
    ppermute x4, waiting for transfers between devices: 7.57 us -> 5.92 us  [along_cells(): return lax.ppermute(value, ('z', 'core'), route)]
    slice x2 -> x1, local copies, waits for them, and re-layouts: 0.15 us -> 1.59 us  [on_device(): halves = [line[:2 * MINE], line[2 * MINE:]]]
  transfers between devices with their start and end apart: 12 -> 15, of which waited for: 8 -> 8; matrix products, arithmetic and copies ran while one was open for 0% -> 0% of each run, Pallas kernels for 10% -> 11%
where the time goes in v3:
time: 123 us; the launch traced here: 122 us
  starting transfers between devices  54.6 us (44%)
  blocking collectives  31.8 us (26%)
  Pallas kernels  18.5 us (15%)
  waiting for transfers between devices  11.5 us (9%)
  local copies, waits for them, and re-layouts  4.51 us (4%)
    all_gather x1, blocking collectives, on_device(): own = lax.all_gather(block, 'z', axis=0, tiled=True)  31.8 us
    ppermute x6, starting transfers between devices, along_ring(): return lax.ppermute(value, ALL, route)  19.5 us
    ppermute x4, starting transfers between devices, to_sibling(): return lax.ppermute(value, 'core', [(0, 1), (1, 0)])  17.6 us
    ppermute x4, starting transfers between devices, along_cells(): return lax.ppermute(value, ('z', 'core'), route)  13 us
    pallas_call x2, Pallas kernels, product(): call(functools.partial(product_kernel, part), [((T, G * COLS * B), BF), (...  9.83 us
    ppermute x4, waiting for transfers between devices, along_cells(): return lax.ppermute(value, ('z', 'core'), route)  5.92 us
    all_to_all x1, starting transfers between devices, gather(): lax.all_to_all(blocks, ALL, 0, 0, tiled=True, axis_index_groups=groups)  4.57 us
    pallas_call x2, Pallas kernels, join(): call(functools.partial(join_kernel, parts, bool(own6)), [(hidden.shape, B...  3.29 us
  transfers between devices with their start and end apart: 15, of which 8 were waited for; matrix products, arithmetic and copies ran while one was open for 0% of the time, Pallas kernels for 11%

profile of v3, /device:TPU:1, one launch (start us, length us, event | category | flops | bytes accessed | tf_op | source)
XLA Modules:
  0.0 121.9 jit_solution(4121754563168172276)
XLA Ops:
  5.0 31.8 %all_gather.3.own = bf16[16,128,128]{2,1,0:T(8,128)(2,1)S(1)} all-gather(bf16[1,128,128]{2,1,0:T(8,128)(2,1)S(1)} %get-tuple-element.37), channel_id=1, replica_groups=mesh['x'=4,'y'=4,'z'=16,'core'=2] {'z'}, dimensions={0}, use_global_device_ids=true | all-gather | bytes 557056 | tf_op jit(solution)/shard_map/all_gather | solution.py:263
  36.8 10.1 %collective-permute-start = (bf16[16,128,128]{2,1,0:T(8,128)(2,1)S(1)}, bf16[16,128,128]{2,1,0:T(8,128)(2,1)S(1)}, u32[]{:S(2)}, u32[]{:S(2)}) collective-permute-start(bf16[16,128,128]{2,1,0:T(8,128)(2,1)S(1)} %all_gather.3.own), channel_id=1, source_target_pairs={{0,1},{1,0},{2,3},{3,2},{4,5},{5,4},{6,7},{7,6},{8,9},{9,8},{10,11... | collective-permute-start | bytes 1572872 | tf_op jit(solution)/shard_map/ppermute | solution.py:203
  48.5 2.1 %pick.1 = bf16[4,14,128,128]{3,2,1,0:T(8,128)(2,1)} custom-call(s32[4]{0:T(128)S(1)} %pad_add_fusion.place.refs_0_, s32[4,7]{1,0:T(4,128)S(1)} %bitcast.12, bf16[16,128,128]{2,1,0:T(8,128)(2,1)S(1)} %all_gather.3.own, bf16[16,128,128]{2,1,0:T(8,128)(2,1)S(1)} %collective-permute-done.other), custom_call_target="tpu_custom_call" | custom-call | tf_op jit(solution)/shard_map/pick/pallas_call | solution.py:265
  50.6 4.6 %all-to-all-start = ((bf16[4,14,128,128]{3,2,1,0:T(8,128)(2,1)}), bf16[4,14,128,128]{3,2,1,0:T(8,128)(2,1)}, u32[]{:S(2)}, u32[]{:S(2)}) async-start(bf16[4,14,128,128]{3,2,1,0:T(8,128)(2,1)} %pick.1), calls=%async_computation | async-start | bytes 3670016 | tf_op jit(solution)/shard_map/all_to_all | solution.py:194
  55.2 2.3 %collective-permute-start.3 = (bf16[128,4096]{1,0:T(8,128)(2,1)S(1)}, bf16[128,4096]{1,0:T(8,128)(2,1)S(1)}, u32[]{:S(2)}, u32[]{:S(2)}) collective-permute-start(bf16[128,4096]{1,0:T(8,128)(2,1)S(1)} %copy-done), channel_id=1, source_target_pairs={{0,1},{1,0},{2,3},{3,2},{4,5},{5,4},{6,7},{7,6},{8,9},{9,8},{10,11... | collective-permute-start | bytes 3145736 | tf_op jit(solution)/shard_map/ppermute | solution.py:203
  57.5 1.9 %collective-permute-start.1 = (bf16[3,128,128]{2,1,0:T(8,128)(2,1)S(1)}, bf16[3,128,128]{2,1,0:T(8,128)(2,1)S(1)}, u32[]{:S(2)}, u32[]{:S(2)}) collective-permute-start(bf16[3,128,128]{2,1,0:T(8,128)(2,1)S(1)} %pad_maximum_fusion.own), channel_id=1, source_target_pairs={{0,3},{1,4},{2,5},{3,6},{4,7},{5,8},{6,9},{7,10},{8,11},{9,12},{10... | collective-permute-start | bytes 294920 | tf_op jit(solution)/shard_map/ppermute | solution.py:208
  59.5 4.9 %collective-permute-start.2 = (bf16[3,128,128]{2,1,0:T(8,128)(2,1)S(1)}, bf16[3,128,128]{2,1,0:T(8,128)(2,1)S(1)}, u32[]{:S(2)}, u32[]{:S(2)}) collective-permute-start(bf16[3,128,128]{2,1,0:T(8,128)(2,1)S(1)} %pad_maximum_fusion.own), channel_id=1, source_target_pairs={{0,29},{1,30},{2,31},{3,0},{4,1},{5,2},{6,3},{7,4},{8,5},{9,6},{10... | collective-permute-start | bytes 294920 | tf_op jit(solution)/shard_map/ppermute | solution.py:208
  64.3 1.8 %collective-permute-done.1.low = bf16[3,128,128]{2,1,0:T(8,128)(2,1)S(1)} collective-permute-done((bf16[3,128,128]{2,1,0:T(8,128)(2,1)S(1)}, bf16[3,128,128]{2,1,0:T(8,128)(2,1)S(1)}, u32[]{:S(2)}, u32[]{:S(2)}) %collective-permute-start.1) | collective-permute-done | bytes 98336 | tf_op jit(solution)/shard_map/ppermute | solution.py:208
  71.1 2.8 %collective-permute-start.6 = (bf16[28,128,128]{2,1,0:T(8,128)(2,1)S(1)}, bf16[28,128,128]{2,1,0:T(8,128)(2,1)S(1)}, u32[]{:S(2)}, u32[]{:S(2)}) collective-permute-start(bf16[28,128,128]{2,1,0:T(8,128)(2,1)S(1)} %get-tuple-element.71.refs_0_), channel_id=1, source_target_pairs={{0,32},{32,64},{64,96},{96,0},{128,160},{160,192},{192,224},{224,1... | collective-permute-start | bytes 2752520 | tf_op jit(solution)/shard_map/ppermute | solution.py:199
  73.9 3.7 %collective-permute-start.9 = (bf16[28,128,128]{2,1,0:T(8,128)(2,1)S(1)}, bf16[28,128,128]{2,1,0:T(8,128)(2,1)S(1)}, u32[]{:S(2)}, u32[]{:S(2)}) collective-permute-start(bf16[28,128,128]{2,1,0:T(8,128)(2,1)S(1)} %get-tuple-element.70.refs_1_), channel_id=1, source_target_pairs={{0,96},{32,0},{64,32},{96,64},{128,224},{160,128},{192,160},{224,1... | collective-permute-start | bytes 2752520 | tf_op jit(solution)/shard_map/ppermute | solution.py:199
  77.6 1.9 %collective-permute-start.7 = (bf16[28,128,128]{2,1,0:T(8,128)(2,1)S(1)}, bf16[28,128,128]{2,1,0:T(8,128)(2,1)S(1)}, u32[]{:S(2)}, u32[]{:S(2)}) collective-permute-start(bf16[28,128,128]{2,1,0:T(8,128)(2,1)S(1)} %get-tuple-element.70.refs_1_), channel_id=1, source_target_pairs={{0,32},{32,64},{64,96},{96,0},{128,160},{160,192},{192,224},{224,1... | collective-permute-start | bytes 2752520 | tf_op jit(solution)/shard_map/ppermute | solution.py:199
  79.5 4.6 %collective-permute-start.8 = (bf16[28,128,128]{2,1,0:T(8,128)(2,1)S(1)}, bf16[28,128,128]{2,1,0:T(8,128)(2,1)S(1)}, u32[]{:S(2)}, u32[]{:S(2)}) collective-permute-start(bf16[28,128,128]{2,1,0:T(8,128)(2,1)S(1)} %get-tuple-element.71.refs_0_), channel_id=1, source_target_pairs={{0,96},{32,0},{64,32},{96,64},{128,224},{160,128},{192,160},{224,1... | collective-permute-start | bytes 2752520 | tf_op jit(solution)/shard_map/ppermute | solution.py:199
  84.1 2.6 %collective-permute-done.6.refs_2_ = bf16[28,128,128]{2,1,0:T(8,128)(2,1)S(1)} collective-permute-done((bf16[28,128,128]{2,1,0:T(8,128)(2,1)S(1)}, bf16[28,128,128]{2,1,0:T(8,128)(2,1)S(1)}, u32[]{:S(2)}, u32[]{:S(2)}) %collective-permute-start.6) | collective-permute-done | bytes 917536 | tf_op jit(solution)/shard_map/ppermute | solution.py:199
  86.7 1.9 %collective-permute-start.10 = (bf16[28,128,128]{2,1,0:T(8,128)(2,1)S(1)}, bf16[28,128,128]{2,1,0:T(8,128)(2,1)S(1)}, u32[]{:S(2)}, u32[]{:S(2)}) collective-permute-start(bf16[28,128,128]{2,1,0:T(8,128)(2,1)S(1)} %collective-permute-done.6.refs_2_), channel_id=1, source_target_pairs={{0,32},{32,64},{64,96},{96,0},{128,160},{160,192},{192,224},{224,1... | collective-permute-start | bytes 2752520 | tf_op jit(solution)/shard_map/ppermute | solution.py:199
  88.6 4.6 %collective-permute-start.11 = (bf16[28,128,128]{2,1,0:T(8,128)(2,1)S(1)}, bf16[28,128,128]{2,1,0:T(8,128)(2,1)S(1)}, u32[]{:S(2)}, u32[]{:S(2)}) collective-permute-start(bf16[28,128,128]{2,1,0:T(8,128)(2,1)S(1)} %collective-permute-done.9.refs_5_), channel_id=1, source_target_pairs={{0,96},{32,0},{64,32},{96,64},{128,224},{160,128},{192,160},{224,1... | collective-permute-start | bytes 2752520 | tf_op jit(solution)/shard_map/ppermute | solution.py:199
  93.2 1.7 %collective-permute-start.4 = (bf16[3,128,128]{2,1,0:T(8,128)(2,1)S(1)}, bf16[3,128,128]{2,1,0:T(8,128)(2,1)S(1)}, u32[]{:S(2)}, u32[]{:S(2)}) collective-permute-start(bf16[3,128,128]{2,1,0:T(8,128)(2,1)S(1)} %get-tuple-element.46), channel_id=1, source_target_pairs={{0,1},{1,2},{2,3},{3,4},{4,5},{5,6},{6,7},{7,8},{8,9},{9,10},{10,1... | collective-permute-start | bytes 294920 | tf_op jit(solution)/shard_map/ppermute | solution.py:208
  94.9 1.7 %collective-permute-done.4.below = bf16[3,128,128]{2,1,0:T(8,128)(2,1)S(1)} collective-permute-done((bf16[3,128,128]{2,1,0:T(8,128)(2,1)S(1)}, bf16[3,128,128]{2,1,0:T(8,128)(2,1)S(1)}, u32[]{:S(2)}, u32[]{:S(2)}) %collective-permute-start.4) | collective-permute-done | bytes 98336 | tf_op jit(solution)/shard_map/ppermute | solution.py:208
  96.7 4.5 %collective-permute-start.5 = (bf16[3,128,128]{2,1,0:T(8,128)(2,1)S(1)}, bf16[3,128,128]{2,1,0:T(8,128)(2,1)S(1)}, u32[]{:S(2)}, u32[]{:S(2)}) collective-permute-start(bf16[3,128,128]{2,1,0:T(8,128)(2,1)S(1)} %get-tuple-element.47), channel_id=1, source_target_pairs={{0,31},{1,0},{2,1},{3,2},{4,3},{5,4},{6,5},{7,6},{8,7},{9,8},{10,9... | collective-permute-start | bytes 294920 | tf_op jit(solution)/shard_map/ppermute | solution.py:208
  102.1 7.2 %product_early.1 = (bf16[128,14336]{1,0:T(8,128)(2,1)}, bf16[128,6144]{1,0:T(8,128)(2,1)}, f32[12,128,128]{2,1,0:T(8,128)S(1)}) custom-call(s32[4]{0:T(128)S(1)} %pad_add_fusion.place.refs_0_, s32[4,112]{1,0:T(4,128)S(1)} %bitcast.9, bf16[128,4096]{1,0:T(8,128)(2,1)} %mine.1, bf16[128,4096]{1,0:T(8,128)(2,1)} %copy-done.2, ...), custom_call_target="tpu_custom_call" | custom-call | flops 1409286144 | bytes 9437184 | tf_op jit(solution)/shard_map/product_early/pallas_call | solution.py:222
  109.4 3.2 %collective-permute-start.12 = (bf16[128,6144]{1,0:T(8,128)(2,1)}, bf16[128,6144]{1,0:T(8,128)(2,1)S(1)}, u32[]{:S(2)}, u32[]{:S(2)}) collective-permute-start(bf16[128,6144]{1,0:T(8,128)(2,1)} %get-tuple-element.52), channel_id=1, source_target_pairs={{0,1},{1,0},{2,3},{3,2},{4,5},{5,4},{6,7},{7,6},{8,9},{9,8},{10,11... | collective-permute-start | bytes 4718600 | tf_op jit(solution)/shard_map/ppermute | solution.py:203
  113.9 2.6 %product_opposite.1 = (bf16[128,14336]{1,0:T(8,128)(2,1)}, bf16[128,2048]{1,0:T(8,128)(2,1)S(1)}, f32[4,128,128]{2,1,0:T(8,128)S(1)}) custom-call(s32[4]{0:T(128)S(1)} %pad_add_fusion.place.refs_0_, s32[4,112]{1,0:T(4,128)S(1)} %bitcast.10, bf16[128,4096]{1,0:T(8,128)(2,1)S(1)} %copy-done.1, ...), custom_call_target="tpu_custom_call", output_to_operand_aliasing={{0}: (6, {})} | custom-call | flops 469762048 | bytes 3145728 | tf_op jit(solution)/shard_map/product_opposite/pallas_call | solution.py:222
  116.5 1.9 %collective-permute-start.13 = (bf16[128,2048]{1,0:T(8,128)(2,1)S(1)}, bf16[128,2048]{1,0:T(8,128)(2,1)S(1)}, u32[]{:S(2)}, u32[]{:S(2)}) collective-permute-start(bf16[128,2048]{1,0:T(8,128)(2,1)S(1)} %get-tuple-element.63), channel_id=1, source_target_pairs={{0,1},{1,0},{2,3},{3,2},{4,5},{5,4},{6,7},{7,6},{8,9},{9,8},{10,11... | collective-permute-start | bytes 1572872 | tf_op jit(solution)/shard_map/ppermute | solution.py:203
  118.4 1.7 %join_early.1.refs_5_ = bf16[128,14336]{1,0:T(8,128)(2,1)} custom-call(s32[4]{0:T(128)S(1)} %pad_add_fusion.place.refs_0_, bf16[128,6144]{1,0:T(8,128)(2,1)S(1)} %collective-permute-done.12.refs_1_, bf16[128,14336]{1,0:T(8,128)(2,1)} %get-tuple-element.66.refs_2_), custom_call_target="tpu_custom_call", output_to_operand_aliasing={{}: (2, {})} | custom-call | tf_op jit(solution)/shard_map/join_early/pallas_call | solution.py:243
  120.3 1.6 %join_opposite.1 = bf16[128,14336]{1,0:T(8,128)(2,1)} custom-call(s32[4]{0:T(128)S(1)} %pad_add_fusion.place.refs_0_, bf16[128,6144]{1,0:T(8,128)(2,1)S(1)} %collective-permute-done.12.refs_1_, bf16[128,2048]{1,0:T(8,128)(2,1)S(1)} %collective-permute-done.13.refs_2_, f32[12,128,128]{2,1,0:T(8,128)S(1)} %get-tuple-element.64.refs_3_, ...), custom_call_target="tpu_custom_call", output_to_operand_aliasing={{}: (5, {})} | custom-call | tf_op jit(solution)/shard_map/join_opposite/pallas_call | solution.py:243
  (47 shorter events, 13.2 us)
Async XLA Ops:
  36.8 11.7 %collective-permute-start = (bf16[16,128,128]{2,1,0:T(8,128)(2,1)S(1)}, bf16[16,128,128]{2,1,0:T(8,128)(2,1)S(1)}, u32[]{:S(2)}, u32[]{:S(2)}) collective-permute-start(bf16[16,128,128]{2,1,0:T(8,128)(2,1)S(1)} %all_gather.3.own), channel_id=1, source_target_pairs={{0,1},{1,0},{2,3},{3,2},{4,5},{5,4},{6,7},{7,6},{8,9},{9,8},{10,11... | collective-permute-start | bytes 1572872 | tf_op jit(solution)/shard_map/ppermute | solution.py:203
  50.6 4.6 %copy-start = (bf16[128,4096]{1,0:T(8,128)(2,1)S(1)}, bf16[128,4096]{1,0:T(8,128)(2,1)}, u32[]{:S(2)}) copy-start(bf16[128,4096]{1,0:T(8,128)(2,1)} %mine.1) | copy-start | bytes 3145732
  50.6 6.9 %copy-start.7 = (f32[1,128,128]{2,1,0:T(8,128)S(1)}, f32[1,128,128]{2,1,0:T(8,128)}, u32[]{:S(2)}) copy-start(f32[1,128,128]{2,1,0:T(8,128)} %second) | copy-start | bytes 196612
  50.6 6.9 %copy-start.6 = (f32[1,128,128]{2,1,0:T(8,128)S(1)}, f32[1,128,128]{2,1,0:T(8,128)}, u32[]{:S(2)}) copy-start(f32[1,128,128]{2,1,0:T(8,128)} %moment) | copy-start | bytes 196612
  50.6 6.9 %copy-start.5 = (f32[1,128,128]{2,1,0:T(8,128)S(1)}, f32[1,128,128]{2,1,0:T(8,128)}, u32[]{:S(2)}) copy-start(f32[1,128,128]{2,1,0:T(8,128)} %master.2) | copy-start | bytes 196612
  50.6 18.9 %all-to-all-start = ((bf16[4,14,128,128]{3,2,1,0:T(8,128)(2,1)}), bf16[4,14,128,128]{3,2,1,0:T(8,128)(2,1)}, u32[]{:S(2)}, u32[]{:S(2)}) async-start(bf16[4,14,128,128]{3,2,1,0:T(8,128)(2,1)} %pick.1), calls=%async_computation | async-start | bytes 3670016 | tf_op jit(solution)/shard_map/all_to_all | solution.py:194
  55.2 13.0 %collective-permute-start.3 = (bf16[128,4096]{1,0:T(8,128)(2,1)S(1)}, bf16[128,4096]{1,0:T(8,128)(2,1)S(1)}, u32[]{:S(2)}, u32[]{:S(2)}) collective-permute-start(bf16[128,4096]{1,0:T(8,128)(2,1)S(1)} %copy-done), channel_id=1, source_target_pairs={{0,1},{1,0},{2,3},{3,2},{4,5},{5,4},{6,7},{7,6},{8,9},{9,8},{10,11... | collective-permute-start | bytes 3145736 | tf_op jit(solution)/shard_map/ppermute | solution.py:203
  57.5 8.6 %collective-permute-start.1 = (bf16[3,128,128]{2,1,0:T(8,128)(2,1)S(1)}, bf16[3,128,128]{2,1,0:T(8,128)(2,1)S(1)}, u32[]{:S(2)}, u32[]{:S(2)}) collective-permute-start(bf16[3,128,128]{2,1,0:T(8,128)(2,1)S(1)} %pad_maximum_fusion.own), channel_id=1, source_target_pairs={{0,3},{1,4},{2,5},{3,6},{4,7},{5,8},{6,9},{7,10},{8,11},{9,12},{10... | collective-permute-start | bytes 294920 | tf_op jit(solution)/shard_map/ppermute | solution.py:208
  59.5 8.1 %collective-permute-start.2 = (bf16[3,128,128]{2,1,0:T(8,128)(2,1)S(1)}, bf16[3,128,128]{2,1,0:T(8,128)(2,1)S(1)}, u32[]{:S(2)}, u32[]{:S(2)}) collective-permute-start(bf16[3,128,128]{2,1,0:T(8,128)(2,1)S(1)} %pad_maximum_fusion.own), channel_id=1, source_target_pairs={{0,29},{1,30},{2,31},{3,0},{4,1},{5,2},{6,3},{7,4},{8,5},{9,6},{10... | collective-permute-start | bytes 294920 | tf_op jit(solution)/shard_map/ppermute | solution.py:208
  68.2 2.8 %copy-start.2 = (bf16[128,4096]{1,0:T(8,128)(2,1)}, bf16[128,4096]{1,0:T(8,128)(2,1)S(1)}, u32[]{:S(2)}) copy-start(bf16[128,4096]{1,0:T(8,128)(2,1)S(1)} %collective-permute-done.3.theirs) | copy-start | bytes 3145732
  69.5 32.6 %copy-start.8 = (s32[112,4]{0,1:T(4,128)S(1)}, s32[112,4]{0,1:T(4,128)}, u32[]{:S(2)}) copy-start(s32[112,4]{0,1:T(4,128)} %param.15) | copy-start | bytes 5380
  71.1 15.6 %collective-permute-start.6 = (bf16[28,128,128]{2,1,0:T(8,128)(2,1)S(1)}, bf16[28,128,128]{2,1,0:T(8,128)(2,1)S(1)}, u32[]{:S(2)}, u32[]{:S(2)}) collective-permute-start(bf16[28,128,128]{2,1,0:T(8,128)(2,1)S(1)} %get-tuple-element.71.refs_0_), channel_id=1, source_target_pairs={{0,32},{32,64},{64,96},{96,0},{128,160},{160,192},{192,224},{224,1... | collective-permute-start | bytes 2752520 | tf_op jit(solution)/shard_map/ppermute | solution.py:199
  73.9 14.7 %collective-permute-start.9 = (bf16[28,128,128]{2,1,0:T(8,128)(2,1)S(1)}, bf16[28,128,128]{2,1,0:T(8,128)(2,1)S(1)}, u32[]{:S(2)}, u32[]{:S(2)}) collective-permute-start(bf16[28,128,128]{2,1,0:T(8,128)(2,1)S(1)} %get-tuple-element.70.refs_1_), channel_id=1, source_target_pairs={{0,96},{32,0},{64,32},{96,64},{128,224},{160,128},{192,160},{224,1... | collective-permute-start | bytes 2752520 | tf_op jit(solution)/shard_map/ppermute | solution.py:199
  77.6 24.5 %collective-permute-start.7 = (bf16[28,128,128]{2,1,0:T(8,128)(2,1)S(1)}, bf16[28,128,128]{2,1,0:T(8,128)(2,1)S(1)}, u32[]{:S(2)}, u32[]{:S(2)}) collective-permute-start(bf16[28,128,128]{2,1,0:T(8,128)(2,1)S(1)} %get-tuple-element.70.refs_1_), channel_id=1, source_target_pairs={{0,32},{32,64},{64,96},{96,0},{128,160},{160,192},{192,224},{224,1... | collective-permute-start | bytes 2752520 | tf_op jit(solution)/shard_map/ppermute | solution.py:199
  79.5 22.6 %collective-permute-start.8 = (bf16[28,128,128]{2,1,0:T(8,128)(2,1)S(1)}, bf16[28,128,128]{2,1,0:T(8,128)(2,1)S(1)}, u32[]{:S(2)}, u32[]{:S(2)}) collective-permute-start(bf16[28,128,128]{2,1,0:T(8,128)(2,1)S(1)} %get-tuple-element.71.refs_0_), channel_id=1, source_target_pairs={{0,96},{32,0},{64,32},{96,64},{128,224},{160,128},{192,160},{224,1... | collective-permute-start | bytes 2752520 | tf_op jit(solution)/shard_map/ppermute | solution.py:199
  86.7 22.7 %collective-permute-start.10 = (bf16[28,128,128]{2,1,0:T(8,128)(2,1)S(1)}, bf16[28,128,128]{2,1,0:T(8,128)(2,1)S(1)}, u32[]{:S(2)}, u32[]{:S(2)}) collective-permute-start(bf16[28,128,128]{2,1,0:T(8,128)(2,1)S(1)} %collective-permute-done.6.refs_2_), channel_id=1, source_target_pairs={{0,32},{32,64},{64,96},{96,0},{128,160},{160,192},{192,224},{224,1... | collective-permute-start | bytes 2752520 | tf_op jit(solution)/shard_map/ppermute | solution.py:199
  88.6 13.5 %copy-start.12 = (bf16[28,128,128]{2,1,0:T(8,128)(2,1)}, bf16[28,128,128]{2,1,0:T(8,128)(2,1)S(1)}, u32[]{:S(2)}) copy-start(bf16[28,128,128]{2,1,0:T(8,128)(2,1)S(1)} %collective-permute-done.9.refs_5_) | copy-start | bytes 2752516
  88.6 20.7 %collective-permute-start.11 = (bf16[28,128,128]{2,1,0:T(8,128)(2,1)S(1)}, bf16[28,128,128]{2,1,0:T(8,128)(2,1)S(1)}, u32[]{:S(2)}, u32[]{:S(2)}) collective-permute-start(bf16[28,128,128]{2,1,0:T(8,128)(2,1)S(1)} %collective-permute-done.9.refs_5_), channel_id=1, source_target_pairs={{0,96},{32,0},{64,32},{96,64},{128,224},{160,128},{192,160},{224,1... | collective-permute-start | bytes 2752520 | tf_op jit(solution)/shard_map/ppermute | solution.py:199
  93.2 3.5 %collective-permute-start.4 = (bf16[3,128,128]{2,1,0:T(8,128)(2,1)S(1)}, bf16[3,128,128]{2,1,0:T(8,128)(2,1)S(1)}, u32[]{:S(2)}, u32[]{:S(2)}) collective-permute-start(bf16[3,128,128]{2,1,0:T(8,128)(2,1)S(1)} %get-tuple-element.46), channel_id=1, source_target_pairs={{0,1},{1,2},{2,3},{3,4},{4,5},{5,6},{6,7},{7,8},{8,9},{9,10},{10,1... | collective-permute-start | bytes 294920 | tf_op jit(solution)/shard_map/ppermute | solution.py:208
  96.7 5.4 %collective-permute-start.5 = (bf16[3,128,128]{2,1,0:T(8,128)(2,1)S(1)}, bf16[3,128,128]{2,1,0:T(8,128)(2,1)S(1)}, u32[]{:S(2)}, u32[]{:S(2)}) collective-permute-start(bf16[3,128,128]{2,1,0:T(8,128)(2,1)S(1)} %get-tuple-element.47), channel_id=1, source_target_pairs={{0,31},{1,0},{2,1},{3,2},{4,3},{5,4},{6,5},{7,6},{8,7},{9,8},{10,9... | collective-permute-start | bytes 294920 | tf_op jit(solution)/shard_map/ppermute | solution.py:208
  102.1 11.8 %copy-start.1 = (bf16[128,4096]{1,0:T(8,128)(2,1)S(1)}, bf16[128,4096]{1,0:T(8,128)(2,1)}, u32[]{:S(2)}) copy-start(bf16[128,4096]{1,0:T(8,128)(2,1)} %mine.1) | copy-start | bytes 3145732
  102.1 11.8 %copy-start.3 = (bf16[128,4096]{1,0:T(8,128)(2,1)S(1)}, bf16[128,4096]{1,0:T(8,128)(2,1)}, u32[]{:S(2)}) copy-start(bf16[128,4096]{1,0:T(8,128)(2,1)} %copy-done.2) | copy-start | bytes 3145732
  109.4 9.0 %collective-permute-start.12 = (bf16[128,6144]{1,0:T(8,128)(2,1)}, bf16[128,6144]{1,0:T(8,128)(2,1)S(1)}, u32[]{:S(2)}, u32[]{:S(2)}) collective-permute-start(bf16[128,6144]{1,0:T(8,128)(2,1)} %get-tuple-element.52), channel_id=1, source_target_pairs={{0,1},{1,0},{2,3},{3,2},{4,5},{5,4},{6,7},{7,6},{8,9},{9,8},{10,11... | collective-permute-start | bytes 4718600 | tf_op jit(solution)/shard_map/ppermute | solution.py:203
  116.5 3.8 %collective-permute-start.13 = (bf16[128,2048]{1,0:T(8,128)(2,1)S(1)}, bf16[128,2048]{1,0:T(8,128)(2,1)S(1)}, u32[]{:S(2)}, u32[]{:S(2)}) collective-permute-start(bf16[128,2048]{1,0:T(8,128)(2,1)S(1)} %get-tuple-element.63), channel_id=1, source_target_pairs={{0,1},{1,0},{2,3},{3,2},{4,5},{5,4},{6,7},{7,6},{8,9},{9,8},{10,11... | collective-permute-start | bytes 1572872 | tf_op jit(solution)/shard_map/ppermute | solution.py:203
  (4 other events, 2.9 us)

commit v4 on v3

--- a/solution.py
+++ b/solution.py
@@ -49,13 +49,14 @@
     return jnp.where(c == 0, q * 4 + line, line * 4 + q)
 
 
-def prep_kernel(place, old, new, regrown, master, block, info):
+def prep_kernel(place, slots, master, block, info):
     cell = place[0]
     above, below = (cell + 1) % (Z * C), (cell - 1) % (Z * C)
 
     def look(s, carry):
         kept, o0, k0, op, om = carry
-        o, n, r = old[s % K, s // K], new[s % K, s // K], regrown[s % K, s // K]
+        packed = slots[s % K, s // K]
+        o, n, r = packed % 32, packed // 32 % 32, packed // 1024
         kept = jnp.where((o == cell) & (r == 0), 1, kept)
         k0 = jnp.where((n == cell) & (r == 0), 1, k0)
         o0 = jnp.where(n == cell, o, o0)
@@ -97,13 +98,13 @@
         out[0] = jnp.where(keep == 1, value, 0.0)
 
 
-def pick_kernel(place, old, own, other, out):
+def pick_kernel(place, slots, own, other, out):
     c = place[1]
     for j in range(MINE):
         if j < 12:
-            o = old[j % K, 3 * c + j // K]
+            o = slots[j % K, 3 * c + j // K] % 32
         else:
-            o = old[2 * c + j - 12, COLS - 1]
+            o = slots[2 * c + j - 12, COLS - 1] % 32
         at = o // 2
         block = jnp.where(o % 2 == c, own[at], other[at])
         for t in range(4):
@@ -256,25 +257,26 @@
     cell = lax.axis_index("z") * C + c
     place = jnp.stack([cell, c, lax.axis_index("x"), lax.axis_index("y")]).astype(jnp.int32)
     rows = new_rows.T
-    old_cell, new_cell, regrown = old_cell.T, new_cell.T, regrown.T
+    slots = old_cell.T + 32 * new_cell.T + 1024 * (regrown.T != 0).astype(jnp.int32)
     block, info = call(
-        prep_kernel, [((1, B, B), BF), ((8,), jnp.int32)], [SMEM] * 4 + [VMEM], [VMEM, SMEM], "prep"
-    )(place, old_cell, new_cell, regrown, master)
+        prep_kernel, [((1, B, B), BF), ((8,), jnp.int32)], [SMEM] * 2 + [VMEM], [VMEM, SMEM], "prep"
+    )(place, slots, master)
     own = lax.all_gather(block, "z", axis=0, tiled=True)
+    own, tokens = lax.optimization_barrier((own, tokens))
     other = to_sibling(own)
+    theirs = to_sibling(tokens)
     (picked,) = call(pick_kernel, [((4, MINE, B, B), BF)], [SMEM, SMEM, VMEM, VMEM], [VMEM], "pick")(
-        place, old_cell, own, other
-    )
-    picked, master, moment, second, tokens = lax.optimization_barrier((picked, master, moment, second, tokens))
+        place, slots, own, other
+    )
+    picked, master, moment, second, theirs = lax.optimization_barrier((picked, master, moment, second, theirs))
     line = gather(picked, line_groups(True)).reshape(4 * MINE, B, B)
-    theirs = to_sibling(tokens)
     load = jnp.concatenate([master, moment, second]).astype(BF)
     low = along_cells(load, 3)
     high = along_cells(load, -3)
     up, down = call(middle_kernel, [((3, B, B), BF)] * 2, [SMEM] + [VMEM] * 3, [VMEM] * 2, "middle")(
         info, load, low, high
     )
-    line, up, down, theirs = lax.optimization_barrier((line, up, down, theirs))
+    line, up, down = lax.optimization_barrier((line, up, down))
     halves = [line[: 2 * MINE], line[2 * MINE :]]
     lower, upper = [along_ring(halves[0], 1)], [along_ring(halves[1], -1)]
     lower.append(along_ring(halves[1], 1))
@@ -289,11 +291,9 @@
     states = call(settle_kernel, [((1, B, B), F32)] * 3, [SMEM] + [VMEM] * 7, [VMEM] * 3, "settle")(
         info, master, moment, second, low, high, below, above
     )
-    over, states = lax.optimization_barrier((over, tuple(states)))
     hidden, send, own6_opposite = product("opposite", place, rows, tokens, theirs, over, hidden)
     got_opposite = to_sibling(send)
-    hidden = join(("early",), place, (got_early,), (), hidden)
-    hidden = join(("opposite",), place, (got_early, got_opposite), (own6_early, own6_opposite), hidden)
+    hidden = join(("early", "opposite"), place, (got_early, got_opposite), (own6_early, own6_opposite), hidden)
     return (hidden, *states)
 
 

time: 123 us -> 122 us (level)
  waiting for transfers between devices: 11.5 us -> 14.6 us
  local copies, waits for them, and re-layouts: 4.51 us -> 1.97 us
    all_to_all x1, waiting for transfers between devices: 1.24 us -> 3.81 us  [gather(): lax.all_to_all(blocks, ALL, 0, 0, tiled=True, axis_index_groups=groups)]
    slice x1, local copies, waits for them, and re-layouts: 1.59 us -> 0.12 us  [on_device(): halves = [line[:2 * MINE], line[2 * MINE:]]]
    pallas_call x2 -> x1, Pallas kernels: 3.29 us -> 2.13 us  [join(): call(functools.partial(join_kernel, parts, bool(own6)), [(hidden.shape, B...]
    unnamed x26 -> x18, local copies, waits for them, and re-layouts: 2.92 us -> 1.85 us
where the time goes in v4:
time: 122 us; the launch traced here: 121 us
  starting transfers between devices  53.7 us (44%)
  blocking collectives  31.8 us (26%)
  Pallas kernels  17.7 us (15%)
  waiting for transfers between devices  14.6 us (12%)
  local copies, waits for them, and re-layouts  1.97 us (2%)
    all_gather x1, blocking collectives, on_device(): own = lax.all_gather(block, 'z', axis=0, tiled=True)  31.8 us
    ppermute x6, starting transfers between devices, along_ring(): return lax.ppermute(value, ALL, route)  19.5 us
    ppermute x4, starting transfers between devices, to_sibling(): return lax.ppermute(value, 'core', [(0, 1), (1, 0)])  17.2 us
    ppermute x4, starting transfers between devices, along_cells(): return lax.ppermute(value, ('z', 'core'), route)  12.8 us
    pallas_call x2, Pallas kernels, product(): call(functools.partial(product_kernel, part), [((T, G * COLS * B), BF), (...  9.88 us
    ppermute x4, waiting for transfers between devices, along_cells(): return lax.ppermute(value, ('z', 'core'), route)  5.62 us
    all_to_all x1, starting transfers between devices, gather(): lax.all_to_all(blocks, ALL, 0, 0, tiled=True, axis_index_groups=groups)  4.18 us
    all_to_all x1, waiting for transfers between devices, gather(): lax.all_to_all(blocks, ALL, 0, 0, tiled=True, axis_index_groups=groups)  3.81 us
  transfers between devices with their start and end apart: 15, of which 8 were waited for; matrix products, arithmetic and copies ran while one was open for 0% of the time, Pallas kernels for 11%

profile of v4, /device:TPU:1, one launch (start us, length us, event | category | flops | bytes accessed | tf_op | source)
XLA Modules:
  0.0 121.4 jit_solution(16317587106018664876)
XLA Ops:
  4.0 31.8 %all_gather.3.own = bf16[16,128,128]{2,1,0:T(8,128)(2,1)S(1)} all-gather(bf16[1,128,128]{2,1,0:T(8,128)(2,1)S(1)} %get-tuple-element.33), channel_id=1, replica_groups=mesh['x'=4,'y'=4,'z'=16,'core'=2] {'z'}, dimensions={0}, use_global_device_ids=true | all-gather | bytes 557056 | tf_op jit(solution)/shard_map/all_gather | solution.py:264
  35.8 10.1 %collective-permute-start.1 = (bf16[128,4096]{1,0:T(8,128)(2,1)}, bf16[128,4096]{1,0:T(8,128)(2,1)S(1)}, u32[]{:S(2)}, u32[]{:S(2)}) collective-permute-start(bf16[128,4096]{1,0:T(8,128)(2,1)} %mine.1), channel_id=1, source_target_pairs={{0,1},{1,0},{2,3},{3,2},{4,5},{5,4},{6,7},{7,6},{8,9},{9,8},{10,11... | collective-permute-start | bytes 3145736 | tf_op jit(solution)/shard_map/ppermute | solution.py:204
  45.9 1.9 %collective-permute-start = (bf16[16,128,128]{2,1,0:T(8,128)(2,1)S(1)}, bf16[16,128,128]{2,1,0:T(8,128)(2,1)S(1)}, u32[]{:S(2)}, u32[]{:S(2)}) collective-permute-start(bf16[16,128,128]{2,1,0:T(8,128)(2,1)S(1)} %all_gather.3.own), channel_id=1, source_target_pairs={{0,1},{1,0},{2,3},{3,2},{4,5},{5,4},{6,7},{7,6},{8,9},{9,8},{10,11... | collective-permute-start | bytes 1572872 | tf_op jit(solution)/shard_map/ppermute | solution.py:204
  47.8 1.9 %collective-permute-done.other = bf16[16,128,128]{2,1,0:T(8,128)(2,1)S(1)} collective-permute-done((bf16[16,128,128]{2,1,0:T(8,128)(2,1)S(1)}, bf16[16,128,128]{2,1,0:T(8,128)(2,1)S(1)}, u32[]{:S(2)}, u32[]{:S(2)}) %collective-permute-start) | collective-permute-done | bytes 524320 | tf_op jit(solution)/shard_map/ppermute | solution.py:204
  49.7 2.1 %pick.1 = bf16[4,14,128,128]{3,2,1,0:T(8,128)(2,1)} custom-call(s32[4]{0:T(128)S(1)} %pad_add_fusion.place.refs_0_, s32[4,7]{1,0:T(4,128)S(1)} %add_bitcast_fusion.slots, bf16[16,128,128]{2,1,0:T(8,128)(2,1)S(1)} %all_gather.3.own, bf16[16,128,128]{2,1,0:T(8,128)(2,1)S(1)} %collective-permute-done.other), custom_call_target="tpu_custom_call" | custom-call | tf_op jit(solution)/shard_map/pick/pallas_call | solution.py:268
  52.8 4.2 %all-to-all-start = ((bf16[4,14,128,128]{3,2,1,0:T(8,128)(2,1)}), bf16[4,14,128,128]{3,2,1,0:T(8,128)(2,1)S(1)}, u32[]{:S(2)}, u32[]{:S(2)}) async-start(bf16[4,14,128,128]{3,2,1,0:T(8,128)(2,1)} %pick.1), calls=%async_computation | async-start | bytes 3670016 | tf_op jit(solution)/shard_map/all_to_all | solution.py:195
  57.1 2.0 %collective-permute-start.2 = (bf16[3,128,128]{2,1,0:T(8,128)(2,1)S(1)}, bf16[3,128,128]{2,1,0:T(8,128)(2,1)S(1)}, u32[]{:S(2)}, u32[]{:S(2)}) collective-permute-start(bf16[3,128,128]{2,1,0:T(8,128)(2,1)S(1)} %pad_maximum_fusion.own), channel_id=1, source_target_pairs={{0,3},{1,4},{2,5},{3,6},{4,7},{5,8},{6,9},{7,10},{8,11},{9,12},{10... | collective-permute-start | bytes 294920 | tf_op jit(solution)/shard_map/ppermute | solution.py:209
  59.1 4.8 %collective-permute-start.3 = (bf16[3,128,128]{2,1,0:T(8,128)(2,1)S(1)}, bf16[3,128,128]{2,1,0:T(8,128)(2,1)S(1)}, u32[]{:S(2)}, u32[]{:S(2)}) collective-permute-start(bf16[3,128,128]{2,1,0:T(8,128)(2,1)S(1)} %pad_maximum_fusion.own), channel_id=1, source_target_pairs={{0,29},{1,30},{2,31},{3,0},{4,1},{5,2},{6,3},{7,4},{8,5},{9,6},{10... | collective-permute-start | bytes 294920 | tf_op jit(solution)/shard_map/ppermute | solution.py:209
  63.9 1.7 %collective-permute-done.2.low = bf16[3,128,128]{2,1,0:T(8,128)(2,1)S(1)} collective-permute-done((bf16[3,128,128]{2,1,0:T(8,128)(2,1)S(1)}, bf16[3,128,128]{2,1,0:T(8,128)(2,1)S(1)}, u32[]{:S(2)}, u32[]{:S(2)}) %collective-permute-start.2) | collective-permute-done | bytes 98336 | tf_op jit(solution)/shard_map/ppermute | solution.py:209
  67.4 3.8 %all-to-all-done = bf16[4,14,128,128]{3,2,1,0:T(8,128)(2,1)S(1)} async-done(((bf16[4,14,128,128]{3,2,1,0:T(8,128)(2,1)}), bf16[4,14,128,128]{3,2,1,0:T(8,128)(2,1)S(1)}, u32[]{:S(2)}, u32[]{:S(2)}) %all-to-all-start) | async-done | bytes 1835040 | tf_op jit(solution)/shard_map/all_to_all | solution.py:195
  71.4 2.8 %collective-permute-start.6 = (bf16[28,128,128]{2,1,0:T(8,128)(2,1)S(1)}, bf16[28,128,128]{2,1,0:T(8,128)(2,1)S(1)}, u32[]{:S(2)}, u32[]{:S(2)}) collective-permute-start(bf16[28,128,128]{2,1,0:T(8,128)(2,1)S(1)} %get-tuple-element.63.refs_0_), channel_id=1, source_target_pairs={{0,32},{32,64},{64,96},{96,0},{128,160},{160,192},{192,224},{224,1... | collective-permute-start | bytes 2752520 | tf_op jit(solution)/shard_map/ppermute | solution.py:200
  74.2 3.7 %collective-permute-start.9 = (bf16[28,128,128]{2,1,0:T(8,128)(2,1)S(1)}, bf16[28,128,128]{2,1,0:T(8,128)(2,1)S(1)}, u32[]{:S(2)}, u32[]{:S(2)}) collective-permute-start(bf16[28,128,128]{2,1,0:T(8,128)(2,1)S(1)} %get-tuple-element.62.refs_1_), channel_id=1, source_target_pairs={{0,96},{32,0},{64,32},{96,64},{128,224},{160,128},{192,160},{224,1... | collective-permute-start | bytes 2752520 | tf_op jit(solution)/shard_map/ppermute | solution.py:200
  77.9 1.9 %collective-permute-start.7 = (bf16[28,128,128]{2,1,0:T(8,128)(2,1)S(1)}, bf16[28,128,128]{2,1,0:T(8,128)(2,1)S(1)}, u32[]{:S(2)}, u32[]{:S(2)}) collective-permute-start(bf16[28,128,128]{2,1,0:T(8,128)(2,1)S(1)} %get-tuple-element.62.refs_1_), channel_id=1, source_target_pairs={{0,32},{32,64},{64,96},{96,0},{128,160},{160,192},{192,224},{224,1... | collective-permute-start | bytes 2752520 | tf_op jit(solution)/shard_map/ppermute | solution.py:200
  79.8 4.6 %collective-permute-start.8 = (bf16[28,128,128]{2,1,0:T(8,128)(2,1)S(1)}, bf16[28,128,128]{2,1,0:T(8,128)(2,1)S(1)}, u32[]{:S(2)}, u32[]{:S(2)}) collective-permute-start(bf16[28,128,128]{2,1,0:T(8,128)(2,1)S(1)} %get-tuple-element.63.refs_0_), channel_id=1, source_target_pairs={{0,96},{32,0},{64,32},{96,64},{128,224},{160,128},{192,160},{224,1... | collective-permute-start | bytes 2752520 | tf_op jit(solution)/shard_map/ppermute | solution.py:200
  84.4 2.6 %collective-permute-done.6.refs_2_ = bf16[28,128,128]{2,1,0:T(8,128)(2,1)S(1)} collective-permute-done((bf16[28,128,128]{2,1,0:T(8,128)(2,1)S(1)}, bf16[28,128,128]{2,1,0:T(8,128)(2,1)S(1)}, u32[]{:S(2)}, u32[]{:S(2)}) %collective-permute-start.6) | collective-permute-done | bytes 917536 | tf_op jit(solution)/shard_map/ppermute | solution.py:200
  87.0 1.9 %collective-permute-start.10 = (bf16[28,128,128]{2,1,0:T(8,128)(2,1)S(1)}, bf16[28,128,128]{2,1,0:T(8,128)(2,1)S(1)}, u32[]{:S(2)}, u32[]{:S(2)}) collective-permute-start(bf16[28,128,128]{2,1,0:T(8,128)(2,1)S(1)} %collective-permute-done.6.refs_2_), channel_id=1, source_target_pairs={{0,32},{32,64},{64,96},{96,0},{128,160},{160,192},{192,224},{224,1... | collective-permute-start | bytes 2752520 | tf_op jit(solution)/shard_map/ppermute | solution.py:200
  89.0 4.6 %collective-permute-start.11 = (bf16[28,128,128]{2,1,0:T(8,128)(2,1)S(1)}, bf16[28,128,128]{2,1,0:T(8,128)(2,1)S(1)}, u32[]{:S(2)}, u32[]{:S(2)}) collective-permute-start(bf16[28,128,128]{2,1,0:T(8,128)(2,1)S(1)} %collective-permute-done.9.refs_5_), channel_id=1, source_target_pairs={{0,96},{32,0},{64,32},{96,64},{128,224},{160,128},{192,160},{224,1... | collective-permute-start | bytes 2752520 | tf_op jit(solution)/shard_map/ppermute | solution.py:200
  95.1 1.7 %collective-permute-done.4.below = bf16[3,128,128]{2,1,0:T(8,128)(2,1)S(1)} collective-permute-done((bf16[3,128,128]{2,1,0:T(8,128)(2,1)S(1)}, bf16[3,128,128]{2,1,0:T(8,128)(2,1)S(1)}, u32[]{:S(2)}, u32[]{:S(2)}) %collective-permute-start.4) | collective-permute-done | bytes 98336 | tf_op jit(solution)/shard_map/ppermute | solution.py:209
  96.9 4.5 %collective-permute-start.5 = (bf16[3,128,128]{2,1,0:T(8,128)(2,1)S(1)}, bf16[3,128,128]{2,1,0:T(8,128)(2,1)S(1)}, u32[]{:S(2)}, u32[]{:S(2)}) collective-permute-start(bf16[3,128,128]{2,1,0:T(8,128)(2,1)S(1)} %get-tuple-element.44), channel_id=1, source_target_pairs={{0,31},{1,0},{2,1},{3,2},{4,3},{5,4},{6,5},{7,6},{8,7},{9,8},{10,9... | collective-permute-start | bytes 294920 | tf_op jit(solution)/shard_map/ppermute | solution.py:209
  102.3 7.3 %product_early.1 = (bf16[128,14336]{1,0:T(8,128)(2,1)}, bf16[128,6144]{1,0:T(8,128)(2,1)}, f32[12,128,128]{2,1,0:T(8,128)S(1)}) custom-call(s32[4]{0:T(128)S(1)} %pad_add_fusion.place.refs_0_, s32[4,112]{1,0:T(4,128)S(1)} %bitcast.8, bf16[128,4096]{1,0:T(8,128)(2,1)} %mine.1, bf16[128,4096]{1,0:T(8,128)(2,1)} %copy-done.1, ...), custom_call_target="tpu_custom_call" | custom-call | flops 1409286144 | bytes 9437184 | tf_op jit(solution)/shard_map/product_early/pallas_call | solution.py:223
  109.6 3.2 %collective-permute-start.12 = (bf16[128,6144]{1,0:T(8,128)(2,1)}, bf16[128,6144]{1,0:T(8,128)(2,1)S(1)}, u32[]{:S(2)}, u32[]{:S(2)}) collective-permute-start(bf16[128,6144]{1,0:T(8,128)(2,1)} %get-tuple-element.49), channel_id=1, source_target_pairs={{0,1},{1,0},{2,3},{3,2},{4,5},{5,4},{6,7},{7,6},{8,9},{9,8},{10,11... | collective-permute-start | bytes 4718600 | tf_op jit(solution)/shard_map/ppermute | solution.py:204
  112.9 2.6 %product_opposite.1 = (bf16[128,14336]{1,0:T(8,128)(2,1)}, bf16[128,2048]{1,0:T(8,128)(2,1)S(1)}, f32[4,128,128]{2,1,0:T(8,128)S(1)}) custom-call(s32[4]{0:T(128)S(1)} %pad_add_fusion.place.refs_0_, s32[4,112]{1,0:T(4,128)S(1)} %bitcast.9, bf16[128,4096]{1,0:T(8,128)(2,1)S(1)} %copy-done, ...), custom_call_target="tpu_custom_call", output_to_operand_aliasing={{0}: (6, {})} | custom-call | flops 469762048 | bytes 3145728 | tf_op jit(solution)/shard_map/product_opposite/pallas_call | solution.py:223
  115.5 1.9 %collective-permute-start.13 = (bf16[128,2048]{1,0:T(8,128)(2,1)S(1)}, bf16[128,2048]{1,0:T(8,128)(2,1)S(1)}, u32[]{:S(2)}, u32[]{:S(2)}) collective-permute-start(bf16[128,2048]{1,0:T(8,128)(2,1)S(1)} %get-tuple-element.53), channel_id=1, source_target_pairs={{0,1},{1,0},{2,3},{3,2},{4,5},{5,4},{6,7},{7,6},{8,9},{9,8},{10,11... | collective-permute-start | bytes 1572872 | tf_op jit(solution)/shard_map/ppermute | solution.py:204
  119.3 2.1 %join_opposite.1 = bf16[128,14336]{1,0:T(8,128)(2,1)} custom-call(s32[4]{0:T(128)S(1)} %pad_add_fusion.place.refs_0_, bf16[128,6144]{1,0:T(8,128)(2,1)S(1)} %collective-permute-done.12.refs_1_, bf16[128,2048]{1,0:T(8,128)(2,1)S(1)} %collective-permute-done.13.refs_2_, f32[12,128,128]{2,1,0:T(8,128)S(1)} %get-tuple-element.54.refs_3_, ...), custom_call_target="tpu_custom_call", output_to_operand_aliasing={{}: (5, {})} | custom-call | tf_op jit(solution)/shard_map/join_opposite/pallas_call | solution.py:244
  (39 shorter events, 10.8 us)
Async XLA Ops:
  1.4 0.8 copy-start.3
  35.8 16.1 %collective-permute-start.1 = (bf16[128,4096]{1,0:T(8,128)(2,1)}, bf16[128,4096]{1,0:T(8,128)(2,1)S(1)}, u32[]{:S(2)}, u32[]{:S(2)}) collective-permute-start(bf16[128,4096]{1,0:T(8,128)(2,1)} %mine.1), channel_id=1, source_target_pairs={{0,1},{1,0},{2,3},{3,2},{4,5},{5,4},{6,7},{7,6},{8,9},{9,8},{10,11... | collective-permute-start | bytes 3145736 | tf_op jit(solution)/shard_map/ppermute | solution.py:204
  45.9 3.8 %collective-permute-start = (bf16[16,128,128]{2,1,0:T(8,128)(2,1)S(1)}, bf16[16,128,128]{2,1,0:T(8,128)(2,1)S(1)}, u32[]{:S(2)}, u32[]{:S(2)}) collective-permute-start(bf16[16,128,128]{2,1,0:T(8,128)(2,1)S(1)} %all_gather.3.own), channel_id=1, source_target_pairs={{0,1},{1,0},{2,3},{3,2},{4,5},{5,4},{6,7},{7,6},{8,9},{9,8},{10,11... | collective-permute-start | bytes 1572872 | tf_op jit(solution)/shard_map/ppermute | solution.py:204
  51.8 5.2 %copy-start.5 = (f32[1,128,128]{2,1,0:T(8,128)S(1)}, f32[1,128,128]{2,1,0:T(8,128)}, u32[]{:S(2)}) copy-start(f32[1,128,128]{2,1,0:T(8,128)} %moment) | copy-start | bytes 196612
  51.8 5.2 %copy-start.6 = (f32[1,128,128]{2,1,0:T(8,128)S(1)}, f32[1,128,128]{2,1,0:T(8,128)}, u32[]{:S(2)}) copy-start(f32[1,128,128]{2,1,0:T(8,128)} %second) | copy-start | bytes 196612
  51.8 5.2 %copy-start.4 = (f32[1,128,128]{2,1,0:T(8,128)S(1)}, f32[1,128,128]{2,1,0:T(8,128)}, u32[]{:S(2)}) copy-start(f32[1,128,128]{2,1,0:T(8,128)} %master.2) | copy-start | bytes 196612
  51.8 1.0 copy-start.1
  52.8 18.4 %all-to-all-start = ((bf16[4,14,128,128]{3,2,1,0:T(8,128)(2,1)}), bf16[4,14,128,128]{3,2,1,0:T(8,128)(2,1)S(1)}, u32[]{:S(2)}, u32[]{:S(2)}) async-start(bf16[4,14,128,128]{3,2,1,0:T(8,128)(2,1)} %pick.1), calls=%async_computation | async-start | bytes 3670016 | tf_op jit(solution)/shard_map/all_to_all | solution.py:195
  57.1 8.5 %collective-permute-start.2 = (bf16[3,128,128]{2,1,0:T(8,128)(2,1)S(1)}, bf16[3,128,128]{2,1,0:T(8,128)(2,1)S(1)}, u32[]{:S(2)}, u32[]{:S(2)}) collective-permute-start(bf16[3,128,128]{2,1,0:T(8,128)(2,1)S(1)} %pad_maximum_fusion.own), channel_id=1, source_target_pairs={{0,3},{1,4},{2,5},{3,6},{4,7},{5,8},{6,9},{7,10},{8,11},{9,12},{10... | collective-permute-start | bytes 294920 | tf_op jit(solution)/shard_map/ppermute | solution.py:209
  59.1 7.7 %collective-permute-start.3 = (bf16[3,128,128]{2,1,0:T(8,128)(2,1)S(1)}, bf16[3,128,128]{2,1,0:T(8,128)(2,1)S(1)}, u32[]{:S(2)}, u32[]{:S(2)}) collective-permute-start(bf16[3,128,128]{2,1,0:T(8,128)(2,1)S(1)} %pad_maximum_fusion.own), channel_id=1, source_target_pairs={{0,29},{1,30},{2,31},{3,0},{4,1},{5,2},{6,3},{7,4},{8,5},{9,6},{10... | collective-permute-start | bytes 294920 | tf_op jit(solution)/shard_map/ppermute | solution.py:209
  71.3 31.0 %copy-start.7 = (s32[112,4]{0,1:T(4,128)S(1)}, s32[112,4]{0,1:T(4,128)}, u32[]{:S(2)}) copy-start(s32[112,4]{0,1:T(4,128)} %param.15) | copy-start | bytes 5380
  71.4 15.6 %collective-permute-start.6 = (bf16[28,128,128]{2,1,0:T(8,128)(2,1)S(1)}, bf16[28,128,128]{2,1,0:T(8,128)(2,1)S(1)}, u32[]{:S(2)}, u32[]{:S(2)}) collective-permute-start(bf16[28,128,128]{2,1,0:T(8,128)(2,1)S(1)} %get-tuple-element.63.refs_0_), channel_id=1, source_target_pairs={{0,32},{32,64},{64,96},{96,0},{128,160},{160,192},{192,224},{224,1... | collective-permute-start | bytes 2752520 | tf_op jit(solution)/shard_map/ppermute | solution.py:200
  74.2 14.7 %collective-permute-start.9 = (bf16[28,128,128]{2,1,0:T(8,128)(2,1)S(1)}, bf16[28,128,128]{2,1,0:T(8,128)(2,1)S(1)}, u32[]{:S(2)}, u32[]{:S(2)}) collective-permute-start(bf16[28,128,128]{2,1,0:T(8,128)(2,1)S(1)} %get-tuple-element.62.refs_1_), channel_id=1, source_target_pairs={{0,96},{32,0},{64,32},{96,64},{128,224},{160,128},{192,160},{224,1... | collective-permute-start | bytes 2752520 | tf_op jit(solution)/shard_map/ppermute | solution.py:200
  77.9 24.4 %collective-permute-start.7 = (bf16[28,128,128]{2,1,0:T(8,128)(2,1)S(1)}, bf16[28,128,128]{2,1,0:T(8,128)(2,1)S(1)}, u32[]{:S(2)}, u32[]{:S(2)}) collective-permute-start(bf16[28,128,128]{2,1,0:T(8,128)(2,1)S(1)} %get-tuple-element.62.refs_1_), channel_id=1, source_target_pairs={{0,32},{32,64},{64,96},{96,0},{128,160},{160,192},{192,224},{224,1... | collective-permute-start | bytes 2752520 | tf_op jit(solution)/shard_map/ppermute | solution.py:200
  79.8 22.5 %collective-permute-start.8 = (bf16[28,128,128]{2,1,0:T(8,128)(2,1)S(1)}, bf16[28,128,128]{2,1,0:T(8,128)(2,1)S(1)}, u32[]{:S(2)}, u32[]{:S(2)}) collective-permute-start(bf16[28,128,128]{2,1,0:T(8,128)(2,1)S(1)} %get-tuple-element.63.refs_0_), channel_id=1, source_target_pairs={{0,96},{32,0},{64,32},{96,64},{128,224},{160,128},{192,160},{224,1... | collective-permute-start | bytes 2752520 | tf_op jit(solution)/shard_map/ppermute | solution.py:200
  87.0 22.6 %collective-permute-start.10 = (bf16[28,128,128]{2,1,0:T(8,128)(2,1)S(1)}, bf16[28,128,128]{2,1,0:T(8,128)(2,1)S(1)}, u32[]{:S(2)}, u32[]{:S(2)}) collective-permute-start(bf16[28,128,128]{2,1,0:T(8,128)(2,1)S(1)} %collective-permute-done.6.refs_2_), channel_id=1, source_target_pairs={{0,32},{32,64},{64,96},{96,0},{128,160},{160,192},{192,224},{224,1... | collective-permute-start | bytes 2752520 | tf_op jit(solution)/shard_map/ppermute | solution.py:200
  89.0 13.3 %copy-start.8 = (bf16[28,128,128]{2,1,0:T(8,128)(2,1)}, bf16[28,128,128]{2,1,0:T(8,128)(2,1)S(1)}, u32[]{:S(2)}) copy-start(bf16[28,128,128]{2,1,0:T(8,128)(2,1)S(1)} %collective-permute-done.9.refs_5_) | copy-start | bytes 2752516
  89.0 20.6 %collective-permute-start.11 = (bf16[28,128,128]{2,1,0:T(8,128)(2,1)S(1)}, bf16[28,128,128]{2,1,0:T(8,128)(2,1)S(1)}, u32[]{:S(2)}, u32[]{:S(2)}) collective-permute-start(bf16[28,128,128]{2,1,0:T(8,128)(2,1)S(1)} %collective-permute-done.9.refs_5_), channel_id=1, source_target_pairs={{0,96},{32,0},{64,32},{96,64},{128,224},{160,128},{192,160},{224,1... | collective-permute-start | bytes 2752520 | tf_op jit(solution)/shard_map/ppermute | solution.py:200
  93.5 3.3 %collective-permute-start.4 = (bf16[3,128,128]{2,1,0:T(8,128)(2,1)S(1)}, bf16[3,128,128]{2,1,0:T(8,128)(2,1)S(1)}, u32[]{:S(2)}, u32[]{:S(2)}) collective-permute-start(bf16[3,128,128]{2,1,0:T(8,128)(2,1)S(1)} %get-tuple-element.43), channel_id=1, source_target_pairs={{0,1},{1,2},{2,3},{3,4},{4,5},{5,6},{6,7},{7,8},{8,9},{9,10},{10,1... | collective-permute-start | bytes 294920 | tf_op jit(solution)/shard_map/ppermute | solution.py:209
  96.9 5.4 %collective-permute-start.5 = (bf16[3,128,128]{2,1,0:T(8,128)(2,1)S(1)}, bf16[3,128,128]{2,1,0:T(8,128)(2,1)S(1)}, u32[]{:S(2)}, u32[]{:S(2)}) collective-permute-start(bf16[3,128,128]{2,1,0:T(8,128)(2,1)S(1)} %get-tuple-element.44), channel_id=1, source_target_pairs={{0,31},{1,0},{2,1},{3,2},{4,3},{5,4},{6,5},{7,6},{8,7},{9,8},{10,9... | collective-permute-start | bytes 294920 | tf_op jit(solution)/shard_map/ppermute | solution.py:209
  102.3 10.5 %copy-start = (bf16[128,4096]{1,0:T(8,128)(2,1)S(1)}, bf16[128,4096]{1,0:T(8,128)(2,1)}, u32[]{:S(2)}) copy-start(bf16[128,4096]{1,0:T(8,128)(2,1)} %mine.1) | copy-start | bytes 3145732
  102.3 10.5 %copy-start.2 = (bf16[128,4096]{1,0:T(8,128)(2,1)S(1)}, bf16[128,4096]{1,0:T(8,128)(2,1)}, u32[]{:S(2)}) copy-start(bf16[128,4096]{1,0:T(8,128)(2,1)} %copy-done.1) | copy-start | bytes 3145732
  109.6 9.7 %collective-permute-start.12 = (bf16[128,6144]{1,0:T(8,128)(2,1)}, bf16[128,6144]{1,0:T(8,128)(2,1)S(1)}, u32[]{:S(2)}, u32[]{:S(2)}) collective-permute-start(bf16[128,6144]{1,0:T(8,128)(2,1)} %get-tuple-element.49), channel_id=1, source_target_pairs={{0,1},{1,0},{2,3},{3,2},{4,5},{5,4},{6,7},{7,6},{8,9},{9,8},{10,11... | collective-permute-start | bytes 4718600 | tf_op jit(solution)/shard_map/ppermute | solution.py:204
  115.5 3.8 %collective-permute-start.13 = (bf16[128,2048]{1,0:T(8,128)(2,1)S(1)}, bf16[128,2048]{1,0:T(8,128)(2,1)S(1)}, u32[]{:S(2)}, u32[]{:S(2)}) collective-permute-start(bf16[128,2048]{1,0:T(8,128)(2,1)S(1)} %get-tuple-element.53), channel_id=1, source_target_pairs={{0,1},{1,0},{2,3},{3,2},{4,5},{5,4},{6,7},{7,6},{8,9},{9,8},{10,11... | collective-permute-start | bytes 1572872 | tf_op jit(solution)/shard_map/ppermute | solution.py:204

commit v5 on v4

--- a/solution.py
+++ b/solution.py
@@ -56,7 +56,7 @@
     def look(s, carry):
         kept, o0, k0, op, om = carry
         packed = slots[s % K, s // K]
-        o, n, r = packed % 32, packed // 32 % 32, packed // 1024
+        o, n, r = packed & 31, (packed >> 5) & 31, packed >> 10
         kept = jnp.where((o == cell) & (r == 0), 1, kept)
         k0 = jnp.where((n == cell) & (r == 0), 1, k0)
         o0 = jnp.where(n == cell, o, o0)
@@ -102,11 +102,11 @@
     c = place[1]
     for j in range(MINE):
         if j < 12:
-            o = slots[j % K, 3 * c + j // K] % 32
+            o = slots[j % K, 3 * c + j // K] & 31
         else:
-            o = slots[2 * c + j - 12, COLS - 1] % 32
-        at = o // 2
-        block = jnp.where(o % 2 == c, own[at], other[at])
+            o = slots[2 * c + j - 12, COLS - 1] & 31
+        at = o >> 1
+        block = jnp.where((o & 1) == c, own[at], other[at])
         for t in range(4):
             out[t, j] = block
 
@@ -268,7 +268,7 @@
     (picked,) = call(pick_kernel, [((4, MINE, B, B), BF)], [SMEM, SMEM, VMEM, VMEM], [VMEM], "pick")(
         place, slots, own, other
     )
-    picked, master, moment, second, theirs = lax.optimization_barrier((picked, master, moment, second, theirs))
+    picked, master, moment, second = lax.optimization_barrier((picked, master, moment, second))
     line = gather(picked, line_groups(True)).reshape(4 * MINE, B, B)
     load = jnp.concatenate([master, moment, second]).astype(BF)
     low = along_cells(load, 3)
@@ -276,6 +276,7 @@
     up, down = call(middle_kernel, [((3, B, B), BF)] * 2, [SMEM] + [VMEM] * 3, [VMEM] * 2, "middle")(
         info, load, low, high
     )
+    up, down, theirs = lax.optimization_barrier((up, down, theirs))
     line, up, down = lax.optimization_barrier((line, up, down))
     halves = [line[: 2 * MINE], line[2 * MINE :]]
     lower, upper = [along_ring(halves[0], 1)], [along_ring(halves[1], -1)]

time: 122 us -> 120 us (0.984)
  waiting for transfers between devices: 14.6 us -> 11.9 us
    all_to_all x1, waiting for transfers between devices: 3.81 us -> 1.24 us  [gather(): lax.all_to_all(blocks, ALL, 0, 0, tiled=True, axis_index_groups=groups)]
    slice x1, local copies, waits for them, and re-layouts: 0.12 us -> 1.59 us  [on_device(): halves = [line[:2 * MINE], line[2 * MINE:]]]
  transfers between devices with their start and end apart: 15 -> 15, of which waited for: 8 -> 8; matrix products, arithmetic and copies ran while one was open for 0% -> 0% of each run, Pallas kernels for 11% -> 10%
where the time goes in v5:
time: 120 us
  starting transfers between devices  54.6 us (46%)
  blocking collectives  31.8 us (26%)
  Pallas kernels  17.3 us (14%)
  waiting for transfers between devices  11.9 us (10%)
  local copies, waits for them, and re-layouts  2.47 us (2%)
    all_gather x1, blocking collectives, on_device(): own = lax.all_gather(block, 'z', axis=0, tiled=True)  31.8 us
    ppermute x6, starting transfers between devices, along_ring(): return lax.ppermute(value, ALL, route)  19.5 us
    ppermute x4, starting transfers between devices, to_sibling(): return lax.ppermute(value, 'core', [(0, 1), (1, 0)])  17.6 us
    ppermute x4, starting transfers between devices, along_cells(): return lax.ppermute(value, ('z', 'core'), route)  13 us
    pallas_call x2, Pallas kernels, product(): call(functools.partial(product_kernel, part), [((T, G * COLS * B), BF), (...  9.83 us
    ppermute x4, waiting for transfers between devices, along_cells(): return lax.ppermute(value, ('z', 'core'), route)  5.92 us
    all_to_all x1, starting transfers between devices, gather(): lax.all_to_all(blocks, ALL, 0, 0, tiled=True, axis_index_groups=groups)  4.54 us
    ppermute x6, waiting for transfers between devices, along_ring(): return lax.ppermute(value, ALL, route)  2.64 us
  transfers between devices with their start and end apart: 15, of which 8 were waited for; matrix products, arithmetic and copies ran while one was open for 0% of the time, Pallas kernels for 10%

profile of v5, /device:TPU:1, one launch (start us, length us, event | category | flops | bytes accessed | tf_op | source)
XLA Modules:
  0.0 119.8 jit_solution(4725409860706453968)
XLA Ops:
  3.7 31.8 %all_gather.3.own = bf16[16,128,128]{2,1,0:T(8,128)(2,1)S(1)} all-gather(bf16[1,128,128]{2,1,0:T(8,128)(2,1)S(1)} %get-tuple-element.35), channel_id=1, replica_groups=mesh['x'=4,'y'=4,'z'=16,'core'=2] {'z'}, dimensions={0}, use_global_device_ids=true | all-gather | bytes 557056 | tf_op jit(solution)/shard_map/all_gather | solution.py:264
  35.5 10.1 %collective-permute-start = (bf16[16,128,128]{2,1,0:T(8,128)(2,1)S(1)}, bf16[16,128,128]{2,1,0:T(8,128)(2,1)S(1)}, u32[]{:S(2)}, u32[]{:S(2)}) collective-permute-start(bf16[16,128,128]{2,1,0:T(8,128)(2,1)S(1)} %all_gather.3.own), channel_id=1, source_target_pairs={{0,1},{1,0},{2,3},{3,2},{4,5},{5,4},{6,7},{7,6},{8,9},{9,8},{10,11... | collective-permute-start | bytes 1572872 | tf_op jit(solution)/shard_map/ppermute | solution.py:204
  47.1 2.1 %pick.1 = bf16[4,14,128,128]{3,2,1,0:T(8,128)(2,1)} custom-call(s32[4]{0:T(128)S(1)} %pad_add_fusion.place.refs_0_, s32[4,7]{1,0:T(4,128)S(1)} %add_bitcast_fusion.slots, bf16[16,128,128]{2,1,0:T(8,128)(2,1)S(1)} %all_gather.3.own, bf16[16,128,128]{2,1,0:T(8,128)(2,1)S(1)} %collective-permute-done.other), custom_call_target="tpu_custom_call" | custom-call | tf_op jit(solution)/shard_map/pick/pallas_call | solution.py:268
  49.2 4.5 %all-to-all-start = ((bf16[4,14,128,128]{3,2,1,0:T(8,128)(2,1)}), bf16[4,14,128,128]{3,2,1,0:T(8,128)(2,1)}, u32[]{:S(2)}, u32[]{:S(2)}) async-start(bf16[4,14,128,128]{3,2,1,0:T(8,128)(2,1)} %pick.1), calls=%async_computation | async-start | bytes 3670016 | tf_op jit(solution)/shard_map/all_to_all | solution.py:195
  53.7 2.3 %collective-permute-start.3 = (bf16[128,4096]{1,0:T(8,128)(2,1)S(1)}, bf16[128,4096]{1,0:T(8,128)(2,1)S(1)}, u32[]{:S(2)}, u32[]{:S(2)}) collective-permute-start(bf16[128,4096]{1,0:T(8,128)(2,1)S(1)} %copy-done), channel_id=1, source_target_pairs={{0,1},{1,0},{2,3},{3,2},{4,5},{5,4},{6,7},{7,6},{8,9},{9,8},{10,11... | collective-permute-start | bytes 3145736 | tf_op jit(solution)/shard_map/ppermute | solution.py:204
  56.1 1.9 %collective-permute-start.1 = (bf16[3,128,128]{2,1,0:T(8,128)(2,1)S(1)}, bf16[3,128,128]{2,1,0:T(8,128)(2,1)S(1)}, u32[]{:S(2)}, u32[]{:S(2)}) collective-permute-start(bf16[3,128,128]{2,1,0:T(8,128)(2,1)S(1)} %pad_maximum_fusion.own), channel_id=1, source_target_pairs={{0,3},{1,4},{2,5},{3,6},{4,7},{5,8},{6,9},{7,10},{8,11},{9,12},{10... | collective-permute-start | bytes 294920 | tf_op jit(solution)/shard_map/ppermute | solution.py:209
  58.1 4.9 %collective-permute-start.2 = (bf16[3,128,128]{2,1,0:T(8,128)(2,1)S(1)}, bf16[3,128,128]{2,1,0:T(8,128)(2,1)S(1)}, u32[]{:S(2)}, u32[]{:S(2)}) collective-permute-start(bf16[3,128,128]{2,1,0:T(8,128)(2,1)S(1)} %pad_maximum_fusion.own), channel_id=1, source_target_pairs={{0,29},{1,30},{2,31},{3,0},{4,1},{5,2},{6,3},{7,4},{8,5},{9,6},{10... | collective-permute-start | bytes 294920 | tf_op jit(solution)/shard_map/ppermute | solution.py:209
  62.9 1.8 %collective-permute-done.1.low = bf16[3,128,128]{2,1,0:T(8,128)(2,1)S(1)} collective-permute-done((bf16[3,128,128]{2,1,0:T(8,128)(2,1)S(1)}, bf16[3,128,128]{2,1,0:T(8,128)(2,1)S(1)}, u32[]{:S(2)}, u32[]{:S(2)}) %collective-permute-start.1) | collective-permute-done | bytes 98336 | tf_op jit(solution)/shard_map/ppermute | solution.py:209
  68.1 1.6 %fusion = (bf16[28,128,128]{2,1,0:T(8,128)(2,1)S(1)}, bf16[28,128,128]{2,1,0:T(8,128)(2,1)S(1)}) fusion(bf16[56,128,128]{2,1,0:T(8,128)(2,1)} %bitcast.6), kind=kLoop, calls=%fused_computation.3 | loop fusion | bytes 3670016 | tf_op jit(solution)/shard_map/slice | solution.py:281
  69.7 2.8 %collective-permute-start.6 = (bf16[28,128,128]{2,1,0:T(8,128)(2,1)S(1)}, bf16[28,128,128]{2,1,0:T(8,128)(2,1)S(1)}, u32[]{:S(2)}, u32[]{:S(2)}) collective-permute-start(bf16[28,128,128]{2,1,0:T(8,128)(2,1)S(1)} %get-tuple-element.67.refs_0_), channel_id=1, source_target_pairs={{0,32},{32,64},{64,96},{96,0},{128,160},{160,192},{192,224},{224,1... | collective-permute-start | bytes 2752520 | tf_op jit(solution)/shard_map/ppermute | solution.py:200
  72.5 3.7 %collective-permute-start.9 = (bf16[28,128,128]{2,1,0:T(8,128)(2,1)S(1)}, bf16[28,128,128]{2,1,0:T(8,128)(2,1)S(1)}, u32[]{:S(2)}, u32[]{:S(2)}) collective-permute-start(bf16[28,128,128]{2,1,0:T(8,128)(2,1)S(1)} %get-tuple-element.66.refs_1_), channel_id=1, source_target_pairs={{0,96},{32,0},{64,32},{96,64},{128,224},{160,128},{192,160},{224,1... | collective-permute-start | bytes 2752520 | tf_op jit(solution)/shard_map/ppermute | solution.py:200
  76.2 1.9 %collective-permute-start.7 = (bf16[28,128,128]{2,1,0:T(8,128)(2,1)S(1)}, bf16[28,128,128]{2,1,0:T(8,128)(2,1)S(1)}, u32[]{:S(2)}, u32[]{:S(2)}) collective-permute-start(bf16[28,128,128]{2,1,0:T(8,128)(2,1)S(1)} %get-tuple-element.66.refs_1_), channel_id=1, source_target_pairs={{0,32},{32,64},{64,96},{96,0},{128,160},{160,192},{192,224},{224,1... | collective-permute-start | bytes 2752520 | tf_op jit(solution)/shard_map/ppermute | solution.py:200
  78.1 4.6 %collective-permute-start.8 = (bf16[28,128,128]{2,1,0:T(8,128)(2,1)S(1)}, bf16[28,128,128]{2,1,0:T(8,128)(2,1)S(1)}, u32[]{:S(2)}, u32[]{:S(2)}) collective-permute-start(bf16[28,128,128]{2,1,0:T(8,128)(2,1)S(1)} %get-tuple-element.67.refs_0_), channel_id=1, source_target_pairs={{0,96},{32,0},{64,32},{96,64},{128,224},{160,128},{192,160},{224,1... | collective-permute-start | bytes 2752520 | tf_op jit(solution)/shard_map/ppermute | solution.py:200
  82.7 2.6 %collective-permute-done.6.refs_2_ = bf16[28,128,128]{2,1,0:T(8,128)(2,1)S(1)} collective-permute-done((bf16[28,128,128]{2,1,0:T(8,128)(2,1)S(1)}, bf16[28,128,128]{2,1,0:T(8,128)(2,1)S(1)}, u32[]{:S(2)}, u32[]{:S(2)}) %collective-permute-start.6) | collective-permute-done | bytes 917536 | tf_op jit(solution)/shard_map/ppermute | solution.py:200
  85.3 1.9 %collective-permute-start.10 = (bf16[28,128,128]{2,1,0:T(8,128)(2,1)S(1)}, bf16[28,128,128]{2,1,0:T(8,128)(2,1)S(1)}, u32[]{:S(2)}, u32[]{:S(2)}) collective-permute-start(bf16[28,128,128]{2,1,0:T(8,128)(2,1)S(1)} %collective-permute-done.6.refs_2_), channel_id=1, source_target_pairs={{0,32},{32,64},{64,96},{96,0},{128,160},{160,192},{192,224},{224,1... | collective-permute-start | bytes 2752520 | tf_op jit(solution)/shard_map/ppermute | solution.py:200
  87.2 4.6 %collective-permute-start.11 = (bf16[28,128,128]{2,1,0:T(8,128)(2,1)S(1)}, bf16[28,128,128]{2,1,0:T(8,128)(2,1)S(1)}, u32[]{:S(2)}, u32[]{:S(2)}) collective-permute-start(bf16[28,128,128]{2,1,0:T(8,128)(2,1)S(1)} %collective-permute-done.9.refs_5_), channel_id=1, source_target_pairs={{0,96},{32,0},{64,32},{96,64},{128,224},{160,128},{192,160},{224,1... | collective-permute-start | bytes 2752520 | tf_op jit(solution)/shard_map/ppermute | solution.py:200
  91.8 1.7 %collective-permute-start.4 = (bf16[3,128,128]{2,1,0:T(8,128)(2,1)S(1)}, bf16[3,128,128]{2,1,0:T(8,128)(2,1)S(1)}, u32[]{:S(2)}, u32[]{:S(2)}) collective-permute-start(bf16[3,128,128]{2,1,0:T(8,128)(2,1)S(1)} %get-tuple-element.47), channel_id=1, source_target_pairs={{0,1},{1,2},{2,3},{3,4},{4,5},{5,6},{6,7},{7,8},{8,9},{9,10},{10,1... | collective-permute-start | bytes 294920 | tf_op jit(solution)/shard_map/ppermute | solution.py:209
  93.5 1.7 %collective-permute-done.4.below = bf16[3,128,128]{2,1,0:T(8,128)(2,1)S(1)} collective-permute-done((bf16[3,128,128]{2,1,0:T(8,128)(2,1)S(1)}, bf16[3,128,128]{2,1,0:T(8,128)(2,1)S(1)}, u32[]{:S(2)}, u32[]{:S(2)}) %collective-permute-start.4) | collective-permute-done | bytes 98336 | tf_op jit(solution)/shard_map/ppermute | solution.py:209
  95.3 4.5 %collective-permute-start.5 = (bf16[3,128,128]{2,1,0:T(8,128)(2,1)S(1)}, bf16[3,128,128]{2,1,0:T(8,128)(2,1)S(1)}, u32[]{:S(2)}, u32[]{:S(2)}) collective-permute-start(bf16[3,128,128]{2,1,0:T(8,128)(2,1)S(1)} %get-tuple-element.48), channel_id=1, source_target_pairs={{0,31},{1,0},{2,1},{3,2},{4,3},{5,4},{6,5},{7,6},{8,7},{9,8},{10,9... | collective-permute-start | bytes 294920 | tf_op jit(solution)/shard_map/ppermute | solution.py:209
  100.7 7.2 %product_early.1 = (bf16[128,14336]{1,0:T(8,128)(2,1)}, bf16[128,6144]{1,0:T(8,128)(2,1)}, f32[12,128,128]{2,1,0:T(8,128)S(1)}) custom-call(s32[4]{0:T(128)S(1)} %pad_add_fusion.place.refs_0_, s32[4,112]{1,0:T(4,128)S(1)} %bitcast.8, bf16[128,4096]{1,0:T(8,128)(2,1)} %mine.1, bf16[128,4096]{1,0:T(8,128)(2,1)} %copy-done.2, ...), custom_call_target="tpu_custom_call" | custom-call | flops 1409286144 | bytes 9437184 | tf_op jit(solution)/shard_map/product_early/pallas_call | solution.py:223
  108.0 3.3 %collective-permute-start.12 = (bf16[128,6144]{1,0:T(8,128)(2,1)}, bf16[128,6144]{1,0:T(8,128)(2,1)S(1)}, u32[]{:S(2)}, u32[]{:S(2)}) collective-permute-start(bf16[128,6144]{1,0:T(8,128)(2,1)} %get-tuple-element.53), channel_id=1, source_target_pairs={{0,1},{1,0},{2,3},{3,2},{4,5},{5,4},{6,7},{7,6},{8,9},{9,8},{10,11... | collective-permute-start | bytes 4718600 | tf_op jit(solution)/shard_map/ppermute | solution.py:204
  111.3 2.6 %product_opposite.1 = (bf16[128,14336]{1,0:T(8,128)(2,1)}, bf16[128,2048]{1,0:T(8,128)(2,1)S(1)}, f32[4,128,128]{2,1,0:T(8,128)S(1)}) custom-call(s32[4]{0:T(128)S(1)} %pad_add_fusion.place.refs_0_, s32[4,112]{1,0:T(4,128)S(1)} %bitcast.9, bf16[128,4096]{1,0:T(8,128)(2,1)S(1)} %copy-done.1, ...), custom_call_target="tpu_custom_call", output_to_operand_aliasing={{0}: (6, {})} | custom-call | flops 469762048 | bytes 3145728 | tf_op jit(solution)/shard_map/product_opposite/pallas_call | solution.py:223
  113.9 1.9 %collective-permute-start.13 = (bf16[128,2048]{1,0:T(8,128)(2,1)S(1)}, bf16[128,2048]{1,0:T(8,128)(2,1)S(1)}, u32[]{:S(2)}, u32[]{:S(2)}) collective-permute-start(bf16[128,2048]{1,0:T(8,128)(2,1)S(1)} %get-tuple-element.57), channel_id=1, source_target_pairs={{0,1},{1,0},{2,3},{3,2},{4,5},{5,4},{6,7},{7,6},{8,9},{9,8},{10,11... | collective-permute-start | bytes 1572872 | tf_op jit(solution)/shard_map/ppermute | solution.py:204
  117.7 2.1 %join_opposite.1 = bf16[128,14336]{1,0:T(8,128)(2,1)} custom-call(s32[4]{0:T(128)S(1)} %pad_add_fusion.place.refs_0_, bf16[128,6144]{1,0:T(8,128)(2,1)S(1)} %collective-permute-done.12.refs_1_, bf16[128,2048]{1,0:T(8,128)(2,1)S(1)} %collective-permute-done.13.refs_2_, f32[12,128,128]{2,1,0:T(8,128)S(1)} %get-tuple-element.58.refs_3_, ...), custom_call_target="tpu_custom_call", output_to_operand_aliasing={{}: (5, {})} | custom-call | tf_op jit(solution)/shard_map/join_opposite/pallas_call | solution.py:244
  (41 shorter events, 10.7 us)
Async XLA Ops:
  35.5 11.7 %collective-permute-start = (bf16[16,128,128]{2,1,0:T(8,128)(2,1)S(1)}, bf16[16,128,128]{2,1,0:T(8,128)(2,1)S(1)}, u32[]{:S(2)}, u32[]{:S(2)}) collective-permute-start(bf16[16,128,128]{2,1,0:T(8,128)(2,1)S(1)} %all_gather.3.own), channel_id=1, source_target_pairs={{0,1},{1,0},{2,3},{3,2},{4,5},{5,4},{6,7},{7,6},{8,9},{9,8},{10,11... | collective-permute-start | bytes 1572872 | tf_op jit(solution)/shard_map/ppermute | solution.py:204
  49.2 4.6 %copy-start = (bf16[128,4096]{1,0:T(8,128)(2,1)S(1)}, bf16[128,4096]{1,0:T(8,128)(2,1)}, u32[]{:S(2)}) copy-start(bf16[128,4096]{1,0:T(8,128)(2,1)} %mine.1) | copy-start | bytes 3145732
  49.2 6.9 %copy-start.7 = (f32[1,128,128]{2,1,0:T(8,128)S(1)}, f32[1,128,128]{2,1,0:T(8,128)}, u32[]{:S(2)}) copy-start(f32[1,128,128]{2,1,0:T(8,128)} %second) | copy-start | bytes 196612
  49.2 6.9 %copy-start.6 = (f32[1,128,128]{2,1,0:T(8,128)S(1)}, f32[1,128,128]{2,1,0:T(8,128)}, u32[]{:S(2)}) copy-start(f32[1,128,128]{2,1,0:T(8,128)} %moment) | copy-start | bytes 196612
  49.2 6.9 %copy-start.5 = (f32[1,128,128]{2,1,0:T(8,128)S(1)}, f32[1,128,128]{2,1,0:T(8,128)}, u32[]{:S(2)}) copy-start(f32[1,128,128]{2,1,0:T(8,128)} %master.2) | copy-start | bytes 196612
  49.2 18.9 %all-to-all-start = ((bf16[4,14,128,128]{3,2,1,0:T(8,128)(2,1)}), bf16[4,14,128,128]{3,2,1,0:T(8,128)(2,1)}, u32[]{:S(2)}, u32[]{:S(2)}) async-start(bf16[4,14,128,128]{3,2,1,0:T(8,128)(2,1)} %pick.1), calls=%async_computation | async-start | bytes 3670016 | tf_op jit(solution)/shard_map/all_to_all | solution.py:195
  53.7 13.0 %collective-permute-start.3 = (bf16[128,4096]{1,0:T(8,128)(2,1)S(1)}, bf16[128,4096]{1,0:T(8,128)(2,1)S(1)}, u32[]{:S(2)}, u32[]{:S(2)}) collective-permute-start(bf16[128,4096]{1,0:T(8,128)(2,1)S(1)} %copy-done), channel_id=1, source_target_pairs={{0,1},{1,0},{2,3},{3,2},{4,5},{5,4},{6,7},{7,6},{8,9},{9,8},{10,11... | collective-permute-start | bytes 3145736 | tf_op jit(solution)/shard_map/ppermute | solution.py:204
  56.1 8.6 %collective-permute-start.1 = (bf16[3,128,128]{2,1,0:T(8,128)(2,1)S(1)}, bf16[3,128,128]{2,1,0:T(8,128)(2,1)S(1)}, u32[]{:S(2)}, u32[]{:S(2)}) collective-permute-start(bf16[3,128,128]{2,1,0:T(8,128)(2,1)S(1)} %pad_maximum_fusion.own), channel_id=1, source_target_pairs={{0,3},{1,4},{2,5},{3,6},{4,7},{5,8},{6,9},{7,10},{8,11},{9,12},{10... | collective-permute-start | bytes 294920 | tf_op jit(solution)/shard_map/ppermute | solution.py:209
  58.1 8.1 %collective-permute-start.2 = (bf16[3,128,128]{2,1,0:T(8,128)(2,1)S(1)}, bf16[3,128,128]{2,1,0:T(8,128)(2,1)S(1)}, u32[]{:S(2)}, u32[]{:S(2)}) collective-permute-start(bf16[3,128,128]{2,1,0:T(8,128)(2,1)S(1)} %pad_maximum_fusion.own), channel_id=1, source_target_pairs={{0,29},{1,30},{2,31},{3,0},{4,1},{5,2},{6,3},{7,4},{8,5},{9,6},{10... | collective-permute-start | bytes 294920 | tf_op jit(solution)/shard_map/ppermute | solution.py:209
  66.8 2.8 %copy-start.2 = (bf16[128,4096]{1,0:T(8,128)(2,1)}, bf16[128,4096]{1,0:T(8,128)(2,1)S(1)}, u32[]{:S(2)}) copy-start(bf16[128,4096]{1,0:T(8,128)(2,1)S(1)} %collective-permute-done.3.theirs) | copy-start | bytes 3145732
  68.0 32.6 %copy-start.8 = (s32[112,4]{0,1:T(4,128)S(1)}, s32[112,4]{0,1:T(4,128)}, u32[]{:S(2)}) copy-start(s32[112,4]{0,1:T(4,128)} %param.15) | copy-start | bytes 5380
  69.7 15.6 %collective-permute-start.6 = (bf16[28,128,128]{2,1,0:T(8,128)(2,1)S(1)}, bf16[28,128,128]{2,1,0:T(8,128)(2,1)S(1)}, u32[]{:S(2)}, u32[]{:S(2)}) collective-permute-start(bf16[28,128,128]{2,1,0:T(8,128)(2,1)S(1)} %get-tuple-element.67.refs_0_), channel_id=1, source_target_pairs={{0,32},{32,64},{64,96},{96,0},{128,160},{160,192},{192,224},{224,1... | collective-permute-start | bytes 2752520 | tf_op jit(solution)/shard_map/ppermute | solution.py:200
  72.5 14.7 %collective-permute-start.9 = (bf16[28,128,128]{2,1,0:T(8,128)(2,1)S(1)}, bf16[28,128,128]{2,1,0:T(8,128)(2,1)S(1)}, u32[]{:S(2)}, u32[]{:S(2)}) collective-permute-start(bf16[28,128,128]{2,1,0:T(8,128)(2,1)S(1)} %get-tuple-element.66.refs_1_), channel_id=1, source_target_pairs={{0,96},{32,0},{64,32},{96,64},{128,224},{160,128},{192,160},{224,1... | collective-permute-start | bytes 2752520 | tf_op jit(solution)/shard_map/ppermute | solution.py:200
  76.2 24.5 %collective-permute-start.7 = (bf16[28,128,128]{2,1,0:T(8,128)(2,1)S(1)}, bf16[28,128,128]{2,1,0:T(8,128)(2,1)S(1)}, u32[]{:S(2)}, u32[]{:S(2)}) collective-permute-start(bf16[28,128,128]{2,1,0:T(8,128)(2,1)S(1)} %get-tuple-element.66.refs_1_), channel_id=1, source_target_pairs={{0,32},{32,64},{64,96},{96,0},{128,160},{160,192},{192,224},{224,1... | collective-permute-start | bytes 2752520 | tf_op jit(solution)/shard_map/ppermute | solution.py:200
  78.1 22.6 %collective-permute-start.8 = (bf16[28,128,128]{2,1,0:T(8,128)(2,1)S(1)}, bf16[28,128,128]{2,1,0:T(8,128)(2,1)S(1)}, u32[]{:S(2)}, u32[]{:S(2)}) collective-permute-start(bf16[28,128,128]{2,1,0:T(8,128)(2,1)S(1)} %get-tuple-element.67.refs_0_), channel_id=1, source_target_pairs={{0,96},{32,0},{64,32},{96,64},{128,224},{160,128},{192,160},{224,1... | collective-permute-start | bytes 2752520 | tf_op jit(solution)/shard_map/ppermute | solution.py:200
  85.3 22.6 %collective-permute-start.10 = (bf16[28,128,128]{2,1,0:T(8,128)(2,1)S(1)}, bf16[28,128,128]{2,1,0:T(8,128)(2,1)S(1)}, u32[]{:S(2)}, u32[]{:S(2)}) collective-permute-start(bf16[28,128,128]{2,1,0:T(8,128)(2,1)S(1)} %collective-permute-done.6.refs_2_), channel_id=1, source_target_pairs={{0,32},{32,64},{64,96},{96,0},{128,160},{160,192},{192,224},{224,1... | collective-permute-start | bytes 2752520 | tf_op jit(solution)/shard_map/ppermute | solution.py:200
  87.2 13.5 %copy-start.9 = (bf16[28,128,128]{2,1,0:T(8,128)(2,1)}, bf16[28,128,128]{2,1,0:T(8,128)(2,1)S(1)}, u32[]{:S(2)}) copy-start(bf16[28,128,128]{2,1,0:T(8,128)(2,1)S(1)} %collective-permute-done.9.refs_5_) | copy-start | bytes 2752516
  87.2 20.7 %collective-permute-start.11 = (bf16[28,128,128]{2,1,0:T(8,128)(2,1)S(1)}, bf16[28,128,128]{2,1,0:T(8,128)(2,1)S(1)}, u32[]{:S(2)}, u32[]{:S(2)}) collective-permute-start(bf16[28,128,128]{2,1,0:T(8,128)(2,1)S(1)} %collective-permute-done.9.refs_5_), channel_id=1, source_target_pairs={{0,96},{32,0},{64,32},{96,64},{128,224},{160,128},{192,160},{224,1... | collective-permute-start | bytes 2752520 | tf_op jit(solution)/shard_map/ppermute | solution.py:200
  91.8 3.5 %collective-permute-start.4 = (bf16[3,128,128]{2,1,0:T(8,128)(2,1)S(1)}, bf16[3,128,128]{2,1,0:T(8,128)(2,1)S(1)}, u32[]{:S(2)}, u32[]{:S(2)}) collective-permute-start(bf16[3,128,128]{2,1,0:T(8,128)(2,1)S(1)} %get-tuple-element.47), channel_id=1, source_target_pairs={{0,1},{1,2},{2,3},{3,4},{4,5},{5,6},{6,7},{7,8},{8,9},{9,10},{10,1... | collective-permute-start | bytes 294920 | tf_op jit(solution)/shard_map/ppermute | solution.py:209
  95.3 5.4 %collective-permute-start.5 = (bf16[3,128,128]{2,1,0:T(8,128)(2,1)S(1)}, bf16[3,128,128]{2,1,0:T(8,128)(2,1)S(1)}, u32[]{:S(2)}, u32[]{:S(2)}) collective-permute-start(bf16[3,128,128]{2,1,0:T(8,128)(2,1)S(1)} %get-tuple-element.48), channel_id=1, source_target_pairs={{0,31},{1,0},{2,1},{3,2},{4,3},{5,4},{6,5},{7,6},{8,7},{9,8},{10,9... | collective-permute-start | bytes 294920 | tf_op jit(solution)/shard_map/ppermute | solution.py:209
  100.7 10.5 %copy-start.1 = (bf16[128,4096]{1,0:T(8,128)(2,1)S(1)}, bf16[128,4096]{1,0:T(8,128)(2,1)}, u32[]{:S(2)}) copy-start(bf16[128,4096]{1,0:T(8,128)(2,1)} %mine.1) | copy-start | bytes 3145732
  100.7 10.5 %copy-start.3 = (bf16[128,4096]{1,0:T(8,128)(2,1)S(1)}, bf16[128,4096]{1,0:T(8,128)(2,1)}, u32[]{:S(2)}) copy-start(bf16[128,4096]{1,0:T(8,128)(2,1)} %copy-done.2) | copy-start | bytes 3145732
  108.0 9.7 %collective-permute-start.12 = (bf16[128,6144]{1,0:T(8,128)(2,1)}, bf16[128,6144]{1,0:T(8,128)(2,1)S(1)}, u32[]{:S(2)}, u32[]{:S(2)}) collective-permute-start(bf16[128,6144]{1,0:T(8,128)(2,1)} %get-tuple-element.53), channel_id=1, source_target_pairs={{0,1},{1,0},{2,3},{3,2},{4,5},{5,4},{6,7},{7,6},{8,9},{9,8},{10,11... | collective-permute-start | bytes 4718600 | tf_op jit(solution)/shard_map/ppermute | solution.py:204
  113.9 3.8 %collective-permute-start.13 = (bf16[128,2048]{1,0:T(8,128)(2,1)S(1)}, bf16[128,2048]{1,0:T(8,128)(2,1)S(1)}, u32[]{:S(2)}, u32[]{:S(2)}) collective-permute-start(bf16[128,2048]{1,0:T(8,128)(2,1)S(1)} %get-tuple-element.57), channel_id=1, source_target_pairs={{0,1},{1,0},{2,3},{3,2},{4,5},{5,4},{6,7},{7,6},{8,9},{9,8},{10,11... | collective-permute-start | bytes 1572872 | tf_op jit(solution)/shard_map/ppermute | solution.py:204
  (1 other events, 0.8 us)
